TPU v7x, 32 devices: a whole 2x2x4 slice. The times are simulated.
32 devices in a mesh: dp: 8 (over y, x, core), mp: 4 (over z).
Axes of the slice: x: 2, y: 2, z: 4, core: 2. Of those that a mesh axis runs over, the one named last changes fastest.
Arguments:
- tokens: bfloat16 [8192, 2048], P(('dp', 'mp')), may hold values from -6 to 6
- cotangent: bfloat16 [8192, 2048], P(('dp', 'mp')), may hold values from -6 to 6
- lengths: int32 [8], P('dp'), may hold values from 256 to 1024, as said below
- query_weight: bfloat16 [2048, 2048], P(None, 'mp'), may hold values from -0.1875 to 0.1875
- key_weight: bfloat16 [2048, 2048], P(None, 'mp'), may hold values from -0.1875 to 0.1875
- value_weight: bfloat16 [2048, 2048], P(None, 'mp'), may hold values from -0.125 to 0.125
- out_weight: bfloat16 [2048, 2048], P('mp'), may hold values from -2 to 2
- gate_weight: bfloat16 [2048, 8192], P(None, 'mp'), may hold values from -0.125 to 0.125
- up_weight: bfloat16 [2048, 8192], P(None, 'mp'), may hold values from -0.125 to 0.125
- down_weight: bfloat16 [8192, 2048], P('mp'), may hold values from -0.0625 to 0.0625
- attn_gain: float32 [2048], replicated, may hold values from 0.5 to 1.5
- mlp_gain: float32 [2048], replicated, may hold values from 0.5 to 1.5
- memory_gate: float32 [16], P('mp'), may hold values from -2 to 2
Outputs:
- block_out: bfloat16 [8192, 2048], P(('dp', 'mp'))
- grad_tokens: float32 [8192, 2048], P(('dp', 'mp'))
- grad_query: float32 [2048, 2048], P('dp', 'mp')
- grad_key: float32 [2048, 2048], P('dp', 'mp')
- grad_value: float32 [2048, 2048], P('dp', 'mp')
- grad_out: float32 [2048, 2048], P('mp', 'dp')
- grad_gate: float32 [2048, 8192], P('dp', 'mp')
- grad_up: float32 [2048, 8192], P('dp', 'mp')
- grad_down: float32 [8192, 2048], P('mp', 'dp')
- grad_attn_gain: float32 [2048], replicated
- grad_mlp_gain: float32 [2048], replicated
- grad_memory_gate: float32 [16], replicated
Inputs may be any that keep to these rules, and one draw needn't show every extreme that they name: `lengths`: some group holds a sequence of exactly 1024 rows in every draw.
All inputs are finite; a program needn't handle non-finite values.
Results may differ from a plain program's by a relative error of at most 0.013.
The roundings to bfloat16 on the way count: a program that leaves them out, or rounds other values in their place, can miss the bound.
Values may be sent and summed in bfloat16 or wider, within the bound.
No kernel may reach another device: no remote copies, remote signals or barrier semaphores. Data moves between devices by JAX's collectives and lax.ppermute only.
A program may use at most 320 MiB of HBM per device.

v0:
```python
import jax
import jax.numpy as jnp
from jax import lax
from jax.sharding import PartitionSpec as P

DK = 128
SEG = 128


EPS = 1e-05
HIGHEST = lax.Precision.HIGHEST
NEGATIVE = -1e30


def normed(values, gain_vec):
    return values * lax.rsqrt(jnp.mean(values * values, axis=-1, keepdims=True) + EPS) * gain_vec


def lifted(values):
    return jnp.where(values > 0, values + 1.0, jnp.exp(jnp.minimum(values, 0.0)))


def memory_read(queries, key_rows, value_rows, live_all):
    head_count = queries.shape[1]
    blocks = queries.shape[0] // SEG

    def advance(carried, block_in):
        memory, normer = carried
        block_q, block_k, block_v, block_live = block_in
        lifted_q = lifted(block_q)
        lifted_k = lifted(block_k)
        recalled = jnp.einsum("shd,hde->she", lifted_q, memory, precision=HIGHEST)
        recalled = (
            recalled / jnp.einsum("shd,hd->sh", lifted_q, normer, precision=HIGHEST)[:, :, None]
        )
        guessed = jnp.einsum("shd,hde->she", lifted_k, memory, precision=HIGHEST)
        guessed = (
            guessed / jnp.einsum("shd,hd->sh", lifted_k, normer, precision=HIGHEST)[:, :, None]
        )
        written = lifted_k * block_live[:, None, None]
        memory = memory + jnp.einsum("shd,she->hde", written, block_v - guessed, precision=HIGHEST)
        normer = normer + jnp.sum(written, axis=0)
        return ((memory, normer), recalled)

    start_state = (
        jnp.zeros((head_count, DK, DK), jnp.float32),
        jnp.ones((head_count, DK), jnp.float32),
    )
    block_shape = (blocks, SEG, head_count, DK)
    stacked = (
        queries.reshape(block_shape),
        key_rows.reshape(block_shape),
        value_rows.reshape(block_shape),
        live_all.reshape(blocks, SEG),
    )
    _, recalled = lax.scan(advance, start_state, stacked)
    return recalled.reshape(queries.shape)


def masked_scores(queries, key_rows, score_scale):
    scores = (
        jnp.einsum("sqhd,skhd->shqk", queries, key_rows, preferred_element_type=jnp.float32)
        * score_scale
    )
    block_len = queries.shape[1]
    causal = jnp.arange(block_len)[:, None] >= jnp.arange(block_len)[None, :]
    return jnp.where(causal[None, None], scores, NEGATIVE)


def attend(queries, key_rows, value_rows, score_scale):
    scores = masked_scores(queries, key_rows, score_scale)
    highest = jnp.max(scores, axis=-1, keepdims=True)
    log_total = highest + jnp.log(jnp.sum(jnp.exp(scores - highest), axis=-1, keepdims=True))
    weights = jnp.exp(scores - log_total).astype(jnp.bfloat16)
    in_block = jnp.einsum(
        "shqk,skhd->sqhd", weights, value_rows, preferred_element_type=jnp.float32
    )
    return (in_block, log_total)


def attend_back(queries, key_rows, value_rows, log_total, grad_local, score_scale):
    attn_probs = jnp.exp(masked_scores(queries, key_rows, score_scale) - log_total)
    grad_values = jnp.einsum(
        "shqk,sqhd->skhd",
        attn_probs.astype(jnp.bfloat16),
        grad_local,
        preferred_element_type=jnp.float32,
    )
    grad_probs = jnp.einsum(
        "sqhd,skhd->shqk", grad_local, value_rows, preferred_element_type=jnp.float32
    )
    inner_sum = jnp.sum(grad_probs * attn_probs, axis=-1, keepdims=True)
    grad_scores = (attn_probs * (grad_probs - inner_sum)).astype(jnp.bfloat16)
    grad_queries = (
        jnp.einsum("shqk,skhd->sqhd", grad_scores, key_rows, preferred_element_type=jnp.float32)
        * score_scale
    )
    grad_keys = (
        jnp.einsum("shqk,sqhd->skhd", grad_scores, queries, preferred_element_type=jnp.float32)
        * score_scale
    )
    return (grad_queries, grad_keys, grad_values)


def activate(gate_in, up_in):
    return jax.nn.gelu(gate_in) * up_in


def shards(
    tokens,
    cotangent,
    lengths,
    query_weight,
    key_weight,
    value_weight,
    out_weight,
    gate_weight,
    up_weight,
    down_weight,
    attn_gain,
    mlp_gain,
    memory_gate,
):
    row_count = tokens.shape[0]
    group_rows = row_count * lax.axis_size("mp")
    width_local = query_weight.shape[1]
    head_local = width_local // DK
    score_scale = DK ** (-0.5)
    block_count = group_rows // SEG
    block_shape = (block_count, SEG, head_local, DK)
    first_row = lax.axis_index("mp") * row_count
    live_mine = (first_row + jnp.arange(row_count) < lengths[0]).astype(jnp.float32)[:, None]
    live_all = (jnp.arange(group_rows) < lengths[0]).astype(jnp.float32)
    inputs = tokens.astype(jnp.float32)
    normed_one, pull_one = jax.vjp(normed, inputs, attn_gain)
    rows_one = lax.all_gather(normed_one.astype(jnp.bfloat16), "mp", axis=0, tiled=True)

    def project(weight_cols):
        product = jnp.dot(rows_one, weight_cols, preferred_element_type=jnp.float32)
        return product.astype(jnp.bfloat16).reshape(group_rows, head_local, DK)

    query_heads = project(query_weight)
    key_heads = project(key_weight)
    value_heads = project(value_weight)

    def read_memory(query_part, key_part, value_part):
        return memory_read(query_part, key_part, value_part, live_all)

    recalled, pull_memory = jax.vjp(
        read_memory,
        query_heads.astype(jnp.float32),
        key_heads.astype(jnp.float32),
        value_heads.astype(jnp.float32),
    )
    query_blocks = query_heads.reshape(block_shape)
    key_blocks = key_heads.reshape(block_shape)
    value_blocks = value_heads.reshape(block_shape)
    in_block_parts, log_totals = attend(query_blocks, key_blocks, value_blocks, score_scale)
    in_block = in_block_parts.reshape(group_rows, head_local, DK)
    gate_vec = jax.nn.sigmoid(memory_gate)
    mix_gate = gate_vec[None, :, None]
    mixed = mix_gate * recalled + (1.0 - mix_gate) * in_block
    mixed_low = mixed.reshape(group_rows, width_local).astype(jnp.bfloat16)
    attn_rows = lax.psum_scatter(
        jnp.dot(mixed_low, out_weight, preferred_element_type=jnp.float32),
        "mp",
        scatter_dimension=0,
        tiled=True,
    )
    state = inputs + live_mine * attn_rows
    normed_two, pull_two = jax.vjp(normed, state, mlp_gain)
    normed_low = normed_two.astype(jnp.bfloat16)
    rows_two = lax.all_gather(normed_low, "mp", axis=0, tiled=True)
    gate_pre = jnp.dot(rows_two, gate_weight, preferred_element_type=jnp.float32)
    up_pre = jnp.dot(rows_two, up_weight, preferred_element_type=jnp.float32)
    activated, pull_act = jax.vjp(activate, gate_pre, up_pre)
    hidden_low = activated.astype(jnp.bfloat16)
    mlp_rows_sum = lax.psum_scatter(
        jnp.dot(hidden_low, down_weight, preferred_element_type=jnp.float32).astype(jnp.bfloat16),
        "mp",
        scatter_dimension=0,
        tiled=True,
    ).astype(jnp.float32)
    block_out = (state + live_mine * mlp_rows_sum).astype(jnp.bfloat16)
    upstream = cotangent.astype(jnp.float32)
    grad_branch = (upstream * live_mine).astype(jnp.bfloat16)
    grad_branch_all = lax.all_gather(grad_branch, "mp", axis=0, tiled=True)
    grad_hidden = jnp.einsum(
        "td,fd->tf", grad_branch_all, down_weight, preferred_element_type=jnp.float32
    )
    grad_down_part = jnp.einsum(
        "tf,td->fd", hidden_low, grad_branch_all, preferred_element_type=jnp.float32
    )
    grad_gate_pre, grad_up_pre = pull_act(grad_hidden)
    gate_low = grad_gate_pre.astype(jnp.bfloat16)
    up_low = grad_up_pre.astype(jnp.bfloat16)
    grad_gate_part = jnp.einsum("td,tf->df", rows_two, gate_low, preferred_element_type=jnp.float32)
    grad_up_part = jnp.einsum("td,tf->df", rows_two, up_low, preferred_element_type=jnp.float32)
    summed = jnp.einsum("tf,df->td", gate_low, gate_weight, preferred_element_type=jnp.float32)
    grad_normed_two = lax.psum_scatter(
        summed + jnp.einsum("tf,df->td", up_low, up_weight, preferred_element_type=jnp.float32),
        "mp",
        scatter_dimension=0,
        tiled=True,
    )
    grad_through, grad_mlp_gain_part = pull_two(grad_normed_two)
    grad_state = upstream + grad_through
    grad_attn_branch = (grad_state * live_mine).astype(jnp.bfloat16)
    grad_attn_all = lax.all_gather(grad_attn_branch, "mp", axis=0, tiled=True)
    grad_out_part = jnp.einsum(
        "tc,td->cd", mixed_low, grad_attn_all, preferred_element_type=jnp.float32
    )
    grad_mixed = jnp.einsum(
        "td,cd->tc", grad_attn_all, out_weight, preferred_element_type=jnp.float32
    ).reshape(group_rows, head_local, DK)
    grad_gate_param = (
        jnp.sum(grad_mixed * (recalled - in_block), axis=(0, 2)) * gate_vec * (1.0 - gate_vec)
    )
    grad_in_block = ((1.0 - mix_gate) * grad_mixed).astype(jnp.bfloat16)
    back_q, back_k, back_v = attend_back(
        query_blocks,
        key_blocks,
        value_blocks,
        log_totals,
        grad_in_block.reshape(block_shape),
        score_scale,
    )
    memory_q, memory_k, memory_v = pull_memory(mix_gate * grad_mixed)
    grad_q_low = (
        (back_q.reshape(group_rows, head_local, DK) + memory_q)
        .reshape(group_rows, width_local)
        .astype(jnp.bfloat16)
    )
    grad_k_low = (
        (back_k.reshape(group_rows, head_local, DK) + memory_k)
        .reshape(group_rows, width_local)
        .astype(jnp.bfloat16)
    )
    grad_v_low = (
        (back_v.reshape(group_rows, head_local, DK) + memory_v)
        .reshape(group_rows, width_local)
        .astype(jnp.bfloat16)
    )
    grad_query_part = jnp.einsum(
        "td,tc->dc", rows_one, grad_q_low, preferred_element_type=jnp.float32
    )
    grad_key_part = jnp.einsum(
        "td,tc->dc", rows_one, grad_k_low, preferred_element_type=jnp.float32
    )
    grad_value_part = jnp.einsum(
        "td,tc->dc", rows_one, grad_v_low, preferred_element_type=jnp.float32
    )
    summed = jnp.einsum("tc,dc->td", grad_q_low, query_weight, preferred_element_type=jnp.float32)
    summed = summed + jnp.einsum(
        "tc,dc->td", grad_k_low, key_weight, preferred_element_type=jnp.float32
    )
    grad_normed_one = lax.psum_scatter(
        summed
        + jnp.einsum("tc,dc->td", grad_v_low, value_weight, preferred_element_type=jnp.float32),
        "mp",
        scatter_dimension=0,
        tiled=True,
    )
    grad_inputs, grad_attn_gain_part = pull_one(grad_normed_one)
    grad_tokens = grad_state + grad_inputs
    sum_query, sum_key, sum_value, sum_out, sum_gate, sum_up, sum_down = (
        lax.psum_scatter(grad_query_part, "dp", scatter_dimension=0, tiled=True),
        lax.psum_scatter(grad_key_part, "dp", scatter_dimension=0, tiled=True),
        lax.psum_scatter(grad_value_part, "dp", scatter_dimension=0, tiled=True),
        lax.psum_scatter(grad_out_part, "dp", scatter_dimension=1, tiled=True),
        lax.psum_scatter(grad_gate_part, "dp", scatter_dimension=0, tiled=True),
        lax.psum_scatter(grad_up_part, "dp", scatter_dimension=0, tiled=True),
        lax.psum_scatter(grad_down_part, "dp", scatter_dimension=1, tiled=True),
    )
    gate_full = lax.dynamic_update_slice(
        jnp.zeros((head_local * lax.axis_size("mp"),), jnp.float32),
        grad_gate_param,
        (lax.axis_index("mp") * head_local,),
    )
    sum_attn_gain, sum_mlp_gain, sum_memory_gate = lax.psum(
        (grad_attn_gain_part, grad_mlp_gain_part, gate_full), ("dp", "mp")
    )
    return (
        block_out,
        grad_tokens,
        sum_query,
        sum_key,
        sum_value,
        sum_out,
        sum_gate,
        sum_up,
        sum_down,
        sum_attn_gain,
        sum_mlp_gain,
        sum_memory_gate,
    )


def solution(mesh):
    return jax.shard_map(
        shards,
        mesh=mesh,
        in_specs=(
            P(("dp", "mp"), None),
            P(("dp", "mp"), None),
            P("dp"),
            P(None, "mp"),
            P(None, "mp"),
            P(None, "mp"),
            P("mp", None),
            P(None, "mp"),
            P(None, "mp"),
            P("mp", None),
            P(),
            P(),
            P("mp"),
        ),
        out_specs=(
            P(("dp", "mp"), None),
            P(("dp", "mp"), None),
            P("dp", "mp"),
            P("dp", "mp"),
            P("dp", "mp"),
            P("mp", "dp"),
            P("dp", "mp"),
            P("dp", "mp"),
            P("mp", "dp"),
            P(),
            P(),
            P(),
        ),
        check_vma=False,
    )
```

profile of v0, /device:TPU:8, one launch (start us, length us, event | category | flops | bytes accessed | tf_op | source)
XLA Modules:
  0.0 1871.2 jit_solution(408413092074794967)
XLA Ops:
  13.6 78.5 %all-gather.5.cloned.1.call-done = bf16[1024,2048]{1,0:T(8,128)(2,1)} async-done(((bf16[256,2048]{1,0:T(8,128)(2,1)}), bf16[1024,2048]{1,0:T(8,128)(2,1)}) %all-gather.5.cloned.1.call-update) | async-done | bytes 4194320 | tf_op jit(solution)/shard_map/all_gather | solution.py:136
  145.1 115.9 %while.76 = (s32[]{:T(128)}, f32[4,128,128]{2,1,0:T(8,128)S(1)}, f32[4,128]{1,0:T(4,128)S(1)}, f32[8,128,4,128]{3,2,1,0:T(4,128)}, f32[8,128,4,128]{3,1,2,0:T(8,...) while((s32[]{:T(128)}, f32[4,128,128]{2,1,0:T(8,128)S(1)}, ...), condition=%wide.region_3.4_spmd.clone, body=%wide.region_1.3_spmd.clone.sunk | while | flops 306907648 | bytes 18207084 | solution.py:56
  270.5 145.4 %reduce-scatter.12.cloned.1.call-done = f32[256,2048]{1,0:T(8,128)} async-done(((f32[1024,2048]{1,0:T(8,128)}), f32[256,2048]{1,0:T(8,128)}) %reduce-scatter.12.cloned.1.call-update) | async-done | bytes 2097168 | tf_op jit(solution)/shard_map/reduce_scatter | solution.py:164
  422.7 78.7 %all-gather.7.cloned.1.call-done = bf16[1024,2048]{1,0:T(8,128)(2,1)} async-done(((bf16[256,2048]{1,0:T(8,128)(2,1)}), bf16[1024,2048]{1,0:T(8,128)(2,1)}) %all-gather.7.cloned.1.call-update) | async-done | bytes 4194320 | tf_op jit(solution)/shard_map/all_gather | solution.py:173
  501.4 15.5 fusion.142
  530.0 52.7 %all-gather.9.cloned.1.call-done = bf16[1024,2048]{1,0:T(8,128)(2,1)} async-done(((bf16[256,2048]{1,0:T(8,128)(2,1)}), bf16[1024,2048]{1,0:T(8,128)(2,1)}) %all-gather.9.cloned.1.call-update) | async-done | bytes 4194320 | tf_op jit(solution)/shard_map/all_gather | solution.py:187
  582.7 24.6 %multiply_convert_fusion = (bf16[1024,2048]{1,0:T(8,128)(2,1)}, bf16[1024,2048]{1,0:T(8,128)(2,1)}, bf16[1024,2048]{1,0:T(8,128)(2,1)}) fusion(f32[1024,2048]{1,0:T(8,128)} %fusion.142, f32[1024,2048]{1,0:T(8,128)} %fusion.143, bf16[1024,2048]{1,0:T(8,128)(2,1)} %all-gather.9.cloned.1.call-done, bf16[2048,2048]{1,0:T(8,128)(2,1)} %param.26), kind=kOutput, calls=%fused_computation.149 | convolution fusion | flops 8644460544 | bytes 41943040 | tf_op jit(solution)/shard_map/td,fd->tf/dot_general | solution.py:188
  633.8 13.8 convolution_convert_fusion
  647.7 131.5 %reduce-scatter.16.cloned.1.call-done = f32[256,2048]{1,0:T(8,128)} async-done(((f32[1024,2048]{1,0:T(8,128)}), f32[256,2048]{1,0:T(8,128)}) %reduce-scatter.16.cloned.1.call-update) | async-done | bytes 2097168 | tf_op jit(solution)/shard_map/reduce_scatter | solution.py:200
  782.0 77.2 %reduce-scatter.14.cloned.1.call-done = bf16[256,2048]{1,0:T(8,128)(2,1)} async-done(((bf16[1024,2048]{1,0:T(8,128)(2,1)}), bf16[256,2048]{1,0:T(8,128)(2,1)}) %reduce-scatter.14.cloned.1.call-update) | async-done | bytes 1048592 | tf_op jit(solution)/shard_map/reduce_scatter | solution.py:178
  864.1 78.7 %all-gather.11.cloned.1.call-done = bf16[1024,2048]{1,0:T(8,128)(2,1)} async-done(((bf16[256,2048]{1,0:T(8,128)(2,1)}), bf16[1024,2048]{1,0:T(8,128)(2,1)}) %all-gather.11.cloned.1.call-update) | async-done | bytes 4194320 | tf_op jit(solution)/shard_map/all_gather | solution.py:209
  960.6 138.6 %while.77 = (s32[]{:T(128)}, f32[4,128,128]{2,1,0:T(8,128)S(1)}, f32[4,128]{1,0:T(4,128)S(1)}, f32[8,128,4,128]{3,1,2,0:T(8,128)}, f32[8,128,4,128]{3,1,2,0:T(8,...) while((s32[]{:T(128)}, f32[4,128,128]{2,1,0:T(8,128)S(1)}, ...), condition=%wide.region_15.16_spmd.clone, body=%wide.region_12.15_spmd.clone.sunk | while | flops 607847936 | bytes 9651534 | solution.py:56
  1134.9 15.2 fusion.146
  1150.2 15.5 fusion.147
  1165.8 15.2 fusion.148
  1210.5 69.8 %reduce-scatter.18.cloned.1.call-done = f32[256,2048]{1,0:T(8,128)} async-done(((f32[1024,2048]{1,0:T(8,128)}), f32[256,2048]{1,0:T(8,128)}) %reduce-scatter.18.cloned.1.call-update) | async-done | bytes 2097168 | tf_op jit(solution)/shard_map/reduce_scatter | solution.py:257
  1282.7 40.7 %all-reduce = (f32[2048]{0:T(1024)}, f32[2048]{0:T(1024)}, f32[16]{0:T(128)}) all-reduce(f32[2048]{0:T(1024)S(1)} %get-tuple-element.940, f32[2048]{0:T(1024)S(1)} %get-tuple-element.938, f32[16]{0:T(128)S(1)} %multiply_dynamic-update-slice_fusion.1), channel_id=1, replica_groups=mesh['dp'=8,'mp'=4] {'dp','mp'}, use_global_device_ids=true, to_apply=%region_26.27 | all-reduce | flops 4112 | bytes 32896 | tf_op jit(solution)/shard_map/psum | solution.py:280
  1329.0 73.0 %reduce-scatter.28.cloned.1.call-done = f32[256,2048]{1,0:T(8,128)} async-done(((f32[2048,2048]{1,0:T(8,128)}), f32[256,2048]{1,0:T(8,128)}) %reduce-scatter.28.cloned.1.call-update) | async-done | bytes 2097168 | tf_op jit(solution)/shard_map/reduce_scatter | solution.py:271
  1402.0 120.4 %reduce-scatter.30.cloned.1.call-done = f32[256,2048]{1,0:T(8,128)} async-done(((f32[2048,2048]{1,0:T(8,128)}), f32[256,2048]{1,0:T(8,128)}) %reduce-scatter.30.cloned.1.call-update) | async-done | bytes 2097168 | tf_op jit(solution)/shard_map/reduce_scatter | solution.py:272
  1522.4 120.6 %reduce-scatter.32.cloned.1.call-done = f32[2048,256]{1,0:T(8,128)} async-done(((f32[2048,2048]{1,0:T(8,128)}), f32[2048,256]{1,0:T(8,128)}) %reduce-scatter.32.cloned.1.call-update) | async-done | bytes 2097168 | tf_op jit(solution)/shard_map/reduce_scatter | solution.py:273
  1643.0 55.5 %reduce-scatter.20.cloned.1.call-done = f32[256,512]{1,0:T(8,128)} async-done(((f32[2048,512]{1,0:T(8,128)}), f32[256,512]{1,0:T(8,128)}) %reduce-scatter.20.cloned.1.call-update) | async-done | bytes 524304 | tf_op jit(solution)/shard_map/reduce_scatter | solution.py:267
  1698.4 55.3 %reduce-scatter.22.cloned.1.call-done = f32[256,512]{1,0:T(8,128)} async-done(((f32[2048,512]{1,0:T(8,128)}), f32[256,512]{1,0:T(8,128)}) %reduce-scatter.22.cloned.1.call-update) | async-done | bytes 524304 | tf_op jit(solution)/shard_map/reduce_scatter | solution.py:268
  1753.7 55.5 %reduce-scatter.24.cloned.1.call-done = f32[256,512]{1,0:T(8,128)} async-done(((f32[2048,512]{1,0:T(8,128)}), f32[256,512]{1,0:T(8,128)}) %reduce-scatter.24.cloned.1.call-update) | async-done | bytes 524304 | tf_op jit(solution)/shard_map/reduce_scatter | solution.py:269
  1809.2 55.1 %reduce-scatter.26.cloned.1.call-done = f32[512,256]{1,0:T(8,128)} async-done(((f32[512,2048]{1,0:T(8,128)}), f32[512,256]{1,0:T(8,128)}) %reduce-scatter.26.cloned.1.call-update) | async-done | bytes 524304 | tf_op jit(solution)/shard_map/reduce_scatter | solution.py:270
  (522 shorter events, 465.8 us)
Async XLA Ops:
  7.2 257.6 %copy-start = (bf16[512,2048]{1,0:T(8,128)(2,1)S(1)}, bf16[512,2048]{1,0:T(8,128)(2,1)}, u32[]{:S(2)}) copy-start(bf16[512,2048]{1,0:T(8,128)(2,1)} %param.23) | copy-start | bytes 6291460
  7.2 84.8 %all-gather.5.cloned.1.call-start = ((), (), s32[]{:S(2)}) async-start(), calls=%async_computation.11 | async-start | bytes 5242880 | tf_op jit(solution)/shard_map/all_gather | solution.py:136
  12.6 403.3 %reduce-scatter.12.cloned.1.call-start = ((), (), s32[]{:S(2)}) async-start(), calls=%async_computation.12 | async-start | bytes 10485760 | tf_op jit(solution)/shard_map/reduce_scatter | solution.py:164
  270.4 145.5 %copy-start.5 = (bf16[256,2048]{1,0:T(8,128)(2,1)S(1)}, bf16[256,2048]{1,0:T(8,128)(2,1)}, u32[]{:S(2)}) copy-start(bf16[256,2048]{1,0:T(8,128)(2,1)} %param.17) | copy-start | bytes 3145732
  270.4 230.9 %all-gather.7.cloned.1.call-start = ((), (), s32[]{:S(2)}) async-start(), calls=%async_computation.13 | async-start | bytes 5242880 | tf_op jit(solution)/shard_map/all_gather | solution.py:173
  270.5 150.3 %copy-start.24 = (f32[2048]{0:T(1024)S(1)}, f32[2048]{0:T(1024)}, u32[]{:S(2)}) copy-start(f32[2048]{0:T(1024)} %param.28) | copy-start | bytes 24580
  422.1 160.6 %all-gather.9.cloned.1.call-start = ((), (), s32[]{:S(2)}) async-start(), calls=%async_computation.15 | async-start | bytes 5242880 | tf_op jit(solution)/shard_map/all_gather | solution.py:187
  422.6 356.6 %reduce-scatter.16.cloned.1.call-start = ((), (), s32[]{:S(2)}) async-start(), calls=%async_computation.16 | async-start | bytes 10485760 | tf_op jit(solution)/shard_map/reduce_scatter | solution.py:200
  633.7 225.5 %reduce-scatter.14.cloned.1.call-start = ((), (), s32[]{:S(2)}) async-start(), calls=%async_computation.14 | async-start | bytes 5242880 | tf_op jit(solution)/shard_map/reduce_scatter | solution.py:178
  647.7 211.6 %copy-start.14 = (bf16[256,2048]{1,0:T(8,128)(2,1)S(1)}, bf16[256,2048]{1,0:T(8,128)(2,1)}, u32[]{:S(2)}) copy-start(bf16[256,2048]{1,0:T(8,128)(2,1)} %param.18) | copy-start | bytes 3145732
  647.7 295.1 %all-gather.11.cloned.1.call-start = ((), (), s32[]{:S(2)}) async-start(), calls=%async_computation.17 | async-start | bytes 5242880 | tf_op jit(solution)/shard_map/all_gather | solution.py:209
  864.0 416.4 %reduce-scatter.18.cloned.1.call-start = ((), (), s32[]{:S(2)}) async-start(), calls=%async_computation.18 | async-start | bytes 10485760 | tf_op jit(solution)/shard_map/reduce_scatter | solution.py:257
  960.6 138.7 %copy-start.4 = (f32[8,4,128,128]{2,3,1,0:T(8,128)S(1)}, f32[8,4,128,128]{2,3,1,0:T(8,128)}, u32[]{:S(2)}) copy-start(f32[8,4,128,128]{2,3,1,0:T(8,128)} %copy-done.3) | copy-start | bytes 6291460
  960.6 138.7 %copy-start.23 = (f32[4,8,128]{2,1,0:T(8,128)S(1)}, f32[4,8,128]{2,1,0:T(8,128)}, u32[]{:S(2)}) copy-start(f32[4,8,128]{2,1,0:T(8,128)} %copy-done.22) | copy-start | bytes 49156
  960.6 138.7 %copy-start.33 = (f32[4]{0:T(128)S(1)}, f32[4]{0:T(128)}, u32[]{:S(2)}) copy-start(f32[4]{0:T(128)} %copy-done.32) | copy-start | bytes 52
  1134.9 267.1 %reduce-scatter.28.cloned.1.call-start = ((), (), s32[]{:S(2)}) async-start(), calls=%async_computation.23 | async-start | bytes 18874368 | tf_op jit(solution)/shard_map/reduce_scatter | solution.py:271
  1150.2 372.2 %reduce-scatter.30.cloned.1.call-start = ((), (), s32[]{:S(2)}) async-start(), calls=%async_computation.24 | async-start | bytes 18874368 | tf_op jit(solution)/shard_map/reduce_scatter | solution.py:272
  1165.7 477.2 %reduce-scatter.32.cloned.1.call-start = ((), (), s32[]{:S(2)}) async-start(), calls=%async_computation.25 | async-start | bytes 18874368 | tf_op jit(solution)/shard_map/reduce_scatter | solution.py:273
  1181.0 517.4 %reduce-scatter.20.cloned.1.call-start = ((), (), s32[]{:S(2)}) async-start(), calls=%async_computation.19 | async-start | bytes 4718592 | tf_op jit(solution)/shard_map/reduce_scatter | solution.py:267
  1188.8 564.9 %reduce-scatter.22.cloned.1.call-start = ((), (), s32[]{:S(2)}) async-start(), calls=%async_computation.20 | async-start | bytes 4718592 | tf_op jit(solution)/shard_map/reduce_scatter | solution.py:268
  1195.7 613.5 %reduce-scatter.24.cloned.1.call-start = ((), (), s32[]{:S(2)}) async-start(), calls=%async_computation.21 | async-start | bytes 4718592 | tf_op jit(solution)/shard_map/reduce_scatter | solution.py:269
  1202.6 661.8 %reduce-scatter.26.cloned.1.call-start = ((), (), s32[]{:S(2)}) async-start(), calls=%async_computation.22 | async-start | bytes 4718592 | tf_op jit(solution)/shard_map/reduce_scatter | solution.py:270
  1210.3 113.0 %copy-start.29 = (f32[256]{0:T(256)S(1)}, f32[256]{0:T(256)}, u32[]{:S(2)}) copy-start(f32[256]{0:T(256)} %copy-done.28) | copy-start | bytes 3076
  1323.3 541.0 %copy-start.1 = (bf16[512,2048]{1,0:T(8,128)(2,1)S(1)}, bf16[512,2048]{1,0:T(8,128)(2,1)}, u32[]{:S(2)}) copy-start(bf16[512,2048]{1,0:T(8,128)(2,1)} %param.23) | copy-start | bytes 6291460
  (35 other events, 512.1 us)
Sparse Core Ops, SparseCore 0:
  12.7 79.2 all-gather.4
  270.6 145.3 reduce-scatter.11
  422.2 79.1 all-gather.6
  503.4 79.2 all-gather.8
  633.9 145.3 reduce-scatter.15
  781.4 77.7 reduce-scatter.13
  864.1 78.6 all-gather.10
  1135.0 145.3 reduce-scatter.17
  1285.0 116.9 reduce-scatter.27
  1406.4 115.9 reduce-scatter.29
  1527.0 115.9 reduce-scatter.31
  1647.1 51.2 reduce-scatter.19
  1702.4 51.3 reduce-scatter.21
  1757.9 51.2 reduce-scatter.23
  1813.0 51.3 reduce-scatter.25
where the time goes:
time: 1880 us; the launch traced here: 1870 us
  waiting for transfers between devices  1250 us (66%)
  matrix products  406 us (22%)
  local copies, waits for them, and re-layouts  79.6 us (4%)
  other arithmetic  78.8 us (4%)
  blocking collectives  40.7 us (2%)
    reduce_scatter x1, waiting for transfers between devices, shards(): lax.psum_scatter(jnp.dot(mixed_low, out_weight, preferred_element_type=jn...  145 us
    reduce_scatter x1, waiting for transfers between devices, shards(): lax.psum_scatter(summed + jnp.einsum('tf,df->td', up_low, up_weight, pref...  132 us
    reduce_scatter x1, waiting for transfers between devices, shards(): lax.psum_scatter(grad_down_part, 'dp', scatter_dimension=1, tiled=True)  121 us
    reduce_scatter x1, waiting for transfers between devices, shards(): lax.psum_scatter(grad_up_part, 'dp', scatter_dimension=0, tiled=True)  120 us
    all_gather x1, waiting for transfers between devices, shards(): grad_attn_all = lax.all_gather(grad_attn_branch, 'mp', axis=0, tiled=True)  78.7 us
    all_gather x1, waiting for transfers between devices, shards(): rows_two = lax.all_gather(normed_low, 'mp', axis=0, tiled=True)  78.7 us
    all_gather x1, waiting for transfers between devices, shards(): lax.all_gather(normed_one.astype(jnp.bfloat16), 'mp', axis=0, tiled=True)  78.5 us
    reduce_scatter x1, waiting for transfers between devices, shards(): lax.psum_scatter(jnp.dot(hidden_low, down_weight, preferred_element_type=...  77.2 us
  transfers between devices with their start and end apart: 15, of which 15 were waited for; matrix products, arithmetic and copies ran while one was open for 7% of the time, Pallas kernels for 0%

commit v1 on v0

v1 whole, which is shorter than its diff:
```python
import functools

import jax
import jax.numpy as jnp
from jax import lax
from jax.experimental import pallas as pl
from jax.experimental.pallas import tpu as pltpu
from jax.sharding import PartitionSpec as P

DK = 128
SEG = 128
EPS = 1e-05
NEGATIVE = -1e30
LOW = jnp.bfloat16
F32 = jnp.float32


def hop(value, axis, mask):
    size = lax.axis_size(axis)
    return lax.ppermute(value, axis, [(j, j ^ mask) for j in range(size)])


def top_bit(number):
    return 1 << (number.bit_length() - 1)


def singles(size):
    return [p for p in range(1, size) if p == top_bit(p)]


def doubles(size):
    return [p for p in range(1, size) if p != top_bit(p)]


def gather_near(mine, axis):
    return {0: mine, **{p: hop(mine, axis, p) for p in singles(lax.axis_size(axis))}}


def gather_far(pieces, axis):
    size = lax.axis_size(axis)
    return {p: hop(pieces[top_bit(p)], axis, p ^ top_bit(p)) for p in doubles(size)}


def reduce_far(parts, axis):
    size = lax.axis_size(axis)
    return {p: hop(parts[p].astype(LOW), axis, p ^ top_bit(p)) for p in doubles(size)}


def reduce_near(parts, got, axis, only=None):
    size = lax.axis_size(axis)
    sent = {}
    for p in singles(size):
        if only is None or p in only:
            value = parts[p].astype(F32)
            for q in doubles(size):
                if top_bit(q) == p:
                    value = value + got[q].astype(F32)
            sent[p] = hop(value.astype(LOW), axis, p)
    return sent


def total(own, *arrived):
    value = own.astype(F32)
    for some in arrived:
        for p in some:
            value = value + some[p].astype(F32)
    return value


def swap_pieces(pieces, axis):
    return {p: hop(pieces[p], axis, p) if p else pieces[p] for p in range(lax.axis_size(axis))}


def stacked(pieces, axis=0):
    return jnp.concatenate([pieces[p] for p in range(len(pieces))], axis=axis)


def relative_blocks(value, axis):
    size = lax.axis_size(axis)
    mine = lax.axis_index(axis)
    step = value.shape[1] // size

    def take(r):
        return lax.dynamic_slice_in_dim(value, (mine ^ r) * step, step, axis=1)

    return (
        jnp.concatenate([take(r) for r in range(0, size, 2)], axis=1),
        jnp.concatenate([take(r) for r in range(1, size, 2)], axis=1),
    )


class BlockSum:
    def __init__(self, kept, sent, axis, dim):
        self.axis, self.dim, self.kept = axis, dim, kept
        self.size = lax.axis_size(axis)
        self.masks = [1 << b for b in range(1, self.size.bit_length() - 1)]
        self.flight = hop(sent, axis, 1)
        self.halves = None

    def part(self, value, j, low):
        step = self.kept.shape[self.dim] // (self.size // 2)
        if self.dim == 0:
            half = step // 2
            return value[j * step + low * half : j * step + (low + 1) * half].astype(F32)
        half = self.kept.shape[0] // 2
        return value[low * half : (low + 1) * half, j * step : (j + 1) * step].astype(F32)

    def step(self, k):
        if k == 0:
            self.halves = [
                {
                    2 * j: self.part(self.kept, j, low) + self.part(self.flight, j, low)
                    for j in range(self.size // 2)
                }
                for low in (0, 1)
            ]
        else:
            self.land(k - 1)
        self.flight = []
        for low, order in ((0, self.masks), (1, self.masks[::-1])):
            held = self.halves[low]
            gone = [r for r in held if r & order[k]]
            self.flight.append(
                hop(jnp.stack([held[r] for r in gone]).astype(LOW), self.axis, order[k])
            )

    def land(self, k):
        for low, order in ((0, self.masks), (1, self.masks[::-1])):
            held = self.halves[low]
            gone = [r for r in held if r & order[k]]
            self.halves[low] = {
                r ^ order[k]: held[r ^ order[k]] + self.flight[low][n].astype(F32)
                for n, r in enumerate(gone)
            }

    @property
    def steps(self):
        return len(self.masks)

    def result(self):
        self.land(self.steps - 1)
        return jnp.concatenate([half[0] for half in self.halves], axis=0)

    @property
    def state(self):
        return self.kept, self.flight, self.halves

    @state.setter
    def state(self, value):
        self.kept, self.flight, self.halves = value


def sum_everywhere(vector, axes):
    for axis in axes:
        bit = 1
        while bit < lax.axis_size(axis):
            vector = vector + hop(vector, axis, bit)
            bit *= 2
    return vector


def rows_by(left, right, contract, precision=None):
    return lax.dot_general(
        left, right, ((contract[:1], contract[1:]), ((), ())), preferred_element_type=F32
    )


def split(value):
    high = value.astype(LOW)
    return high, (value - high.astype(F32)).astype(LOW)


def fine(left, right, contract):
    (lh, ll), (rh, rl) = split(left), split(right)
    return (
        rows_by(lh, rh, contract) + rows_by(lh, rl, contract) + rows_by(ll, rh, contract)
    )


def lifted(values):
    return jnp.where(values > 0, values + 1.0, jnp.exp(jnp.minimum(values, 0.0)))


def lifted_slope(values):
    slope = jnp.exp(jnp.minimum(values, 0.0))
    return jnp.where(values > 0, 1.0, jnp.where(values < 0, slope, 0.5))


def probabilities(queries, key_rows):
    scores = rows_by(queries, key_rows, (1, 1)) * DK ** (-0.5)
    row = lax.broadcasted_iota(jnp.int32, (SEG, SEG), 0)
    col = lax.broadcasted_iota(jnp.int32, (SEG, SEG), 1)
    scores = jnp.where(row >= col, scores, NEGATIVE)
    lift = jnp.exp(scores - jnp.max(scores, axis=-1, keepdims=True))
    return lift / jnp.sum(lift, axis=-1, keepdims=True)


def live_column(segment, length):
    position = segment * SEG + lax.broadcasted_iota(jnp.int32, (SEG, 1), 0)
    return (position < length).astype(F32)


def attend_kernel(place, share, qkv_ref, mixed_ref, memory_ref, normer_ref, memory, normer):
    heads = memory.shape[0]
    width = heads * DK
    segment = pl.program_id(0)

    @pl.when(segment == 0)
    def _():
        memory[...] = jnp.zeros_like(memory)
        normer[...] = jnp.ones_like(normer)

    live = live_column(segment, place[1])
    memory_ref[0] = memory[...]
    normer_ref[0] = normer[...]
    for h in range(heads):
        at = h * DK
        queries = qkv_ref[:, at : at + DK]
        key_rows = qkv_ref[:, width + at : width + at + DK]
        value_rows = qkv_ref[:, 2 * width + at : 2 * width + at + DK]
        probs = probabilities(queries, key_rows).astype(LOW)
        in_block = rows_by(probs, value_rows, (1, 0))
        lifted_q = lifted(queries.astype(F32))
        lifted_k = lifted(key_rows.astype(F32))
        held = memory[h]
        norm = normer[h : h + 1]
        read = fine(jnp.concatenate([lifted_q, lifted_k], axis=0), held, (1, 0))
        recalled = read[:SEG] / jnp.sum(lifted_q * norm, axis=-1, keepdims=True)
        guessed = read[SEG:] / jnp.sum(lifted_k * norm, axis=-1, keepdims=True)
        mix = share[h]
        mixed_ref[:, at : at + DK] = (mix * recalled + (1.0 - mix) * in_block).astype(LOW)
        written = lifted_k * live
        memory[h] = held + fine(written, value_rows.astype(F32) - guessed, (0, 0))
        normer[h : h + 1] = norm + jnp.sum(written, axis=0, keepdims=True)


def attend_back_kernel(
    place, share, qkv_ref, grad_ref, memory_ref, normer_ref, out_ref, mix_ref, grad_memory, grad_normer
):
    heads = grad_memory.shape[0]
    width = heads * DK
    step = pl.program_id(0)
    segment = pl.num_programs(0) - 1 - step

    @pl.when(step == 0)
    def _():
        grad_memory[...] = jnp.zeros_like(grad_memory)
        grad_normer[...] = jnp.zeros_like(grad_normer)
        mix_ref[...] = jnp.zeros_like(mix_ref)

    live = live_column(segment, place[1])
    for h in range(heads):
        at = h * DK
        queries = qkv_ref[:, at : at + DK]
        key_rows = qkv_ref[:, width + at : width + at + DK]
        value_rows = qkv_ref[:, 2 * width + at : 2 * width + at + DK]
        grad_mixed = grad_ref[:, at : at + DK].astype(F32)
        mix = share[h]
        probs = probabilities(queries, key_rows)
        probs_low = probs.astype(LOW)
        in_block = rows_by(probs_low, value_rows, (1, 0))
        grad_local = ((1.0 - mix) * grad_mixed).astype(LOW)
        back_v = rows_by(probs_low, grad_local, (0, 0))
        grad_probs = rows_by(grad_local, value_rows, (1, 1))
        inner = jnp.sum(grad_probs * probs, axis=-1, keepdims=True)
        grad_scores = (probs * (grad_probs - inner)).astype(LOW)
        back_q = rows_by(grad_scores, key_rows, (1, 0)) * DK ** (-0.5)
        back_k = rows_by(grad_scores, queries, (0, 0)) * DK ** (-0.5)
        float_q = queries.astype(F32)
        float_k = key_rows.astype(F32)
        lifted_q = lifted(float_q)
        lifted_k = lifted(float_k)
        both = jnp.concatenate([lifted_q, lifted_k], axis=0)
        held = memory_ref[0, h]
        norm = normer_ref[0, h : h + 1]
        over_q = 1.0 / jnp.sum(lifted_q * norm, axis=-1, keepdims=True)
        over_k = 1.0 / jnp.sum(lifted_k * norm, axis=-1, keepdims=True)
        read = fine(both, held, (1, 0))
        recalled = read[:SEG] * over_q
        guessed = read[SEG:] * over_k
        mix_ref[h : h + 1] += jnp.sum(
            grad_mixed * (recalled - in_block), axis=0, keepdims=True
        )
        grad_held = grad_memory[h]
        grad_norm = grad_normer[h : h + 1]
        written = lifted_k * live
        grad_update = fine(written, grad_held, (1, 0))
        grad_written = fine(value_rows.astype(F32) - guessed, grad_held, (1, 1)) + grad_norm
        grad_recalled = mix * grad_mixed
        grad_read_q = grad_recalled * over_q
        grad_read_k = -grad_update * over_k
        grad_sum_q = -jnp.sum(grad_read_q * recalled, axis=-1, keepdims=True)
        grad_sum_k = -jnp.sum(grad_read_k * guessed, axis=-1, keepdims=True)
        grad_reads = jnp.concatenate([grad_read_q, grad_read_k], axis=0)
        back = fine(grad_reads, held, (1, 1))
        grad_lifted_q = back[:SEG] + grad_sum_q * norm
        grad_lifted_k = back[SEG:] + grad_sum_k * norm + live * grad_written
        grad_memory[h] = grad_held + fine(both, grad_reads, (0, 0))
        grad_normer[h : h + 1] = grad_norm + jnp.sum(
            lifted_q * grad_sum_q + lifted_k * grad_sum_k, axis=0, keepdims=True
        )
        out_ref[:, at : at + DK] = (back_q + grad_lifted_q * lifted_slope(float_q)).astype(LOW)
        out_ref[:, width + at : width + at + DK] = (
            back_k + grad_lifted_k * lifted_slope(float_k)
        ).astype(LOW)
        out_ref[:, 2 * width + at : 2 * width + at + DK] = (back_v + grad_update).astype(LOW)


def segment_place(segment, place, per_chunk):
    chunk = lax.div(segment, per_chunk) ^ place[0]
    return chunk * per_chunk + lax.rem(segment, per_chunk)


def attend(qkv, place, share, per_chunk):
    rows, wide = qkv.shape
    heads = wide // (3 * DK)
    blocks = rows // SEG

    def row_map(step, place):
        return (segment_place(step, place, per_chunk), 0)

    return pl.pallas_call(
        attend_kernel,
        name="attend",
        out_shape=(
            jax.ShapeDtypeStruct((rows, heads * DK), LOW),
            jax.ShapeDtypeStruct((blocks, heads, DK, DK), F32),
            jax.ShapeDtypeStruct((blocks, heads, DK), F32),
        ),
        grid_spec=pltpu.PrefetchScalarGridSpec(
            num_scalar_prefetch=1,
            grid=(blocks,),
            in_specs=[
                pl.BlockSpec(memory_space=pltpu.SMEM),
                pl.BlockSpec((SEG, wide), row_map),
            ],
            out_specs=[
                pl.BlockSpec((SEG, heads * DK), row_map),
                pl.BlockSpec((1, heads, DK, DK), lambda step, place: (step, 0, 0, 0)),
                pl.BlockSpec((1, heads, DK), lambda step, place: (step, 0, 0)),
            ],
            scratch_shapes=[pltpu.VMEM((heads, DK, DK), F32), pltpu.VMEM((heads, DK), F32)],
        ),
        compiler_params=pltpu.CompilerParams(
            dimension_semantics=("arbitrary",), vmem_limit_bytes=24 << 20
        ),
        cost_estimate=pl.CostEstimate(
            flops=blocks * heads * 14 * 2 * SEG**3 * 4,
            bytes_accessed=rows * wide * 4,
            transcendentals=0,
        ),
    )(place, share, qkv)


def attend_back(qkv, grad_mixed, memories, normers, place, share, per_chunk):
    rows, wide = qkv.shape
    heads = wide // (3 * DK)
    blocks = rows // SEG

    def row_map(step, place):
        return (segment_place(blocks - 1 - step, place, per_chunk), 0)

    return pl.pallas_call(
        attend_back_kernel,
        name="attend_back",
        out_shape=(
            jax.ShapeDtypeStruct((rows, wide), LOW),
            jax.ShapeDtypeStruct((heads, DK), F32),
        ),
        grid_spec=pltpu.PrefetchScalarGridSpec(
            num_scalar_prefetch=1,
            grid=(blocks,),
            in_specs=[
                pl.BlockSpec(memory_space=pltpu.SMEM),
                pl.BlockSpec((SEG, wide), row_map),
                pl.BlockSpec((SEG, heads * DK), row_map),
                pl.BlockSpec(
                    (1, heads, DK, DK), lambda step, place: (blocks - 1 - step, 0, 0, 0)
                ),
                pl.BlockSpec((1, heads, DK), lambda step, place: (blocks - 1 - step, 0, 0)),
            ],
            out_specs=[
                pl.BlockSpec((SEG, wide), row_map),
                pl.BlockSpec((heads, DK), lambda step, place: (0, 0)),
            ],
            scratch_shapes=[pltpu.VMEM((heads, DK, DK), F32), pltpu.VMEM((heads, DK), F32)],
        ),
        compiler_params=pltpu.CompilerParams(
            dimension_semantics=("arbitrary",), vmem_limit_bytes=24 << 20
        ),
        cost_estimate=pl.CostEstimate(
            flops=blocks * heads * 30 * 2 * SEG**3 * 4,
            bytes_accessed=rows * wide * 6,
            transcendentals=0,
        ),
    )(place, share, qkv, grad_mixed, memories, normers)


def live_rows(place, rows):
    position = place[0] * rows + lax.broadcasted_iota(jnp.int32, (rows, 1), 0)
    return (position < place[1]).astype(F32)


def out_project_kernel(place, *refs):
    *mixed_refs, out_ref, tokens_ref, gain_ref, state_ref, normed_ref = refs
    step = pl.program_id(0)

    @pl.when(step == 0)
    def _():
        state_ref[...] = jnp.zeros_like(state_ref)

    weight = out_ref[...].reshape(-1, out_ref.shape[-1])
    for k, mixed_ref in enumerate(mixed_refs):

        @pl.when(step == k)
        def _():
            state_ref[...] += rows_by(mixed_ref[...], weight, (1, 0))

    @pl.when(step == len(mixed_refs) - 1)
    def _():
        live = live_rows(place, state_ref.shape[0])
        state = tokens_ref[...].astype(F32) + live * state_ref[...]
        state_ref[...] = state
        normed_ref[...] = (state * inverse_rms(state) * gain_ref[...]).astype(LOW)


def out_spec(out_full):
    blocks, _, rows, features = out_full.shape
    return pl.BlockSpec((blocks, 1, rows, features), lambda step, *_: (0, step, 0, 0))


def whole(shape):
    return pl.BlockSpec(shape, lambda *_: (0,) * len(shape))


def out_project(mixed, out_full, tokens, gain, place):
    ranks = len(mixed)
    rows, features = tokens.shape
    width = mixed[0].shape[1]
    return pl.pallas_call(
        out_project_kernel,
        name="out_project",
        out_shape=(
            jax.ShapeDtypeStruct((rows, features), F32),
            jax.ShapeDtypeStruct((rows, features), LOW),
        ),
        grid_spec=pltpu.PrefetchScalarGridSpec(
            num_scalar_prefetch=1,
            grid=(ranks,),
            in_specs=[whole((rows, width))] * ranks
            + [out_spec(out_full), whole((rows, features)), whole((1, features))],
            out_specs=[whole((rows, features))] * 2,
        ),
        compiler_params=pltpu.CompilerParams(
            dimension_semantics=("arbitrary",), vmem_limit_bytes=24 << 20
        ),
        cost_estimate=pl.CostEstimate(
            flops=2 * rows * features * ranks * width,
            bytes_accessed=2 * ranks * width * features,
            transcendentals=0,
        ),
    )(place, *[mixed[p] for p in range(ranks)], out_full, tokens, gain[None])


def out_back_kernel(grad_ref, out_ref, back_ref):
    weight = out_ref[...].reshape(-1, out_ref.shape[-1])
    back_ref[0] = rows_by(grad_ref[...], weight, (1, 1)).astype(LOW)


def out_back(grad_attn, out_full):
    rows, features = grad_attn.shape
    blocks, ranks, slice_rows, _ = out_full.shape
    width = blocks * slice_rows
    return pl.pallas_call(
        out_back_kernel,
        name="out_back",
        out_shape=jax.ShapeDtypeStruct((ranks, rows, width), LOW),
        grid=(ranks,),
        in_specs=[whole((rows, features)), out_spec(out_full)],
        out_specs=pl.BlockSpec((1, rows, width), lambda step: (step, 0, 0)),
        compiler_params=pltpu.CompilerParams(
            dimension_semantics=("arbitrary",), vmem_limit_bytes=24 << 20
        ),
        cost_estimate=pl.CostEstimate(
            flops=2 * rows * features * ranks * width,
            bytes_accessed=2 * ranks * width * features,
            transcendentals=0,
        ),
    )(grad_attn, out_full)


def feed_kernel(
    rows_ref,
    branch_ref,
    gate_ref,
    up_ref,
    down_ref,
    hidden_ref,
    gate_back_ref,
    up_back_ref,
    two_ref,
    mlp_ref,
    two_sum,
    mlp_sum,
):
    step = pl.program_id(0)

    @pl.when(step == 0)
    def _():
        two_sum[...] = jnp.zeros_like(two_sum)
        mlp_sum[...] = jnp.zeros_like(mlp_sum)

    rows = rows_ref[...]
    gate_pre = rows_by(rows, gate_ref[...], (1, 0))
    up_pre = rows_by(rows, up_ref[...], (1, 0))
    grad_hidden = rows_by(branch_ref[...], down_ref[...], (1, 1))
    scale, cube = 0.7978845608028654, 0.044715
    square = gate_pre * gate_pre
    bend = jnp.tanh(scale * (gate_pre + cube * (square * gate_pre)))
    half = 0.5 * (1.0 + bend)
    curved = gate_pre * half
    slope = half + (0.5 * scale) * gate_pre * (1.0 - bend * bend) * (1.0 + (3.0 * cube) * square)
    hidden = (curved * up_pre).astype(LOW)
    gate_back = (grad_hidden * up_pre * slope).astype(LOW)
    up_back = (grad_hidden * curved).astype(LOW)
    hidden_ref[...] = hidden
    gate_back_ref[...] = gate_back
    up_back_ref[...] = up_back
    two_sum[...] += rows_by(gate_back, gate_ref[...], (1, 1)) + rows_by(up_back, up_ref[...], (1, 1))
    mlp_sum[...] += rows_by(hidden, down_ref[...], (1, 0))

    @pl.when(step == pl.num_programs(0) - 1)
    def _():
        two_ref[...] = two_sum[...].astype(two_ref.dtype)
        mlp_ref[...] = mlp_sum[...].astype(mlp_ref.dtype)


def feed_forward(rows, branch, gate_weight, up_weight, down_weight, kind):
    count, features = rows.shape
    units = gate_weight.shape[1]
    tile = min(512, units)
    columns = pl.BlockSpec((features, tile), lambda step: (0, step))
    made = pl.BlockSpec((count, tile), lambda step: (0, step))
    return pl.pallas_call(
        feed_kernel,
        name="feed_forward",
        out_shape=(
            *[jax.ShapeDtypeStruct((count, units), LOW)] * 3,
            *[jax.ShapeDtypeStruct((count, features), kind)] * 2,
        ),
        grid=(units // tile,),
        in_specs=[
            whole((count, features)),
            whole((count, features)),
            columns,
            columns,
            pl.BlockSpec((tile, features), lambda step: (step, 0)),
        ],
        out_specs=[made] * 3 + [whole((count, features))] * 2,
        scratch_shapes=[pltpu.VMEM((count, features), F32)] * 2,
        compiler_params=pltpu.CompilerParams(
            dimension_semantics=("arbitrary",), vmem_limit_bytes=40 << 20
        ),
        cost_estimate=pl.CostEstimate(
            flops=12 * count * features * units,
            bytes_accessed=6 * features * units,
            transcendentals=count * units,
        ),
    )(rows, branch, gate_weight, up_weight, down_weight)


def inverse_rms(values):
    return lax.rsqrt(jnp.mean(values * values, axis=-1, keepdims=True) + EPS)


def normed_back(values, inverse, gain_vec, grad):
    unit = values * inverse
    scaled = grad * gain_vec
    grad_values = inverse * (scaled - unit * jnp.mean(scaled * unit, axis=-1, keepdims=True))
    return grad_values, jnp.sum(grad * unit, axis=0)


def hold(value):
    return lax.optimization_barrier(value)


def shards(
    tokens,
    cotangent,
    lengths,
    query_weight,
    key_weight,
    value_weight,
    out_weight,
    gate_weight,
    up_weight,
    down_weight,
    attn_gain,
    mlp_gain,
    memory_gate,
):
    ranks = lax.axis_size("mp")
    row_count = tokens.shape[0]
    width = query_weight.shape[1]
    heads = width // DK
    per_chunk = row_count // SEG
    rank = lax.axis_index("mp")
    pieces = range(ranks)
    place = jnp.stack([rank, lengths[0]]).astype(jnp.int32)
    live = (rank * row_count + jnp.arange(row_count) < lengths[0]).astype(F32)[:, None]
    share = jax.nn.sigmoid(memory_gate)

    features = tokens.shape[1]
    blocks = lax.axis_size("dp")
    near, far = singles(ranks), doubles(ranks)

    def product(left, right):
        return rows_by(left, right, (0, 0)).astype(LOW)

    inputs = tokens.astype(F32)
    inverse_one = inverse_rms(inputs)
    normed_one = (inputs * inverse_one * attn_gain).astype(LOW)
    slice_rows = width // blocks
    out_slice = lax.dynamic_slice_in_dim(
        out_weight, lax.axis_index("dp") * slice_rows, slice_rows, axis=0
    )
    qkv_weight = jnp.concatenate([query_weight, key_weight, value_weight], axis=1)

    def project(rows):
        return rows_by(rows, qkv_weight, (1, 0)).astype(LOW)

    one = gather_near(normed_one, "mp")
    out_slices = gather_near(out_slice, "mp")
    qkv = {0: project(one[0])}
    one, out_slices, qkv, qkv_weight = hold((one, out_slices, qkv, qkv_weight))

    one.update(gather_far(one, "mp"))
    out_slices.update(gather_far(out_slices, "mp"))
    qkv.update({p: project(one[p]) for p in near})
    upstream = cotangent.astype(F32)
    branch_mine = (upstream * live).astype(LOW)
    one, out_slices, qkv, branch_mine = hold((one, out_slices, qkv, branch_mine))
    out_full = lax.all_gather(
        jnp.stack([out_slices[p] for p in pieces]), "dp", axis=0, tiled=True
    )

    branch = gather_near(branch_mine, "mp")
    qkv.update({p: project(one[p]) for p in far})
    qkv = stacked(qkv)
    mixed, memories, normers = attend(qkv, place, share, per_chunk)
    one_blocks = relative_blocks(stacked(one), "dp")
    mixed, one_blocks = hold((mixed, one_blocks))

    mixed = swap_pieces(
        {p: mixed[p * row_count : (p + 1) * row_count] for p in pieces}, "mp"
    )
    mixed, branch, out_full = hold((mixed, branch, out_full))

    out_full = out_full.reshape(blocks, ranks, slice_rows, features)
    state, normed_two = out_project(mixed, out_full, tokens, mlp_gain, place)
    mixed = stacked(mixed, axis=1)

    hidden, gate_back, up_back, two_parts, mlp_parts = {}, {}, {}, {}, {}

    def feed(p):
        kind = LOW if p == 1 or p in far else F32
        hidden[p], gate_back[p], up_back[p], two_parts[p], mlp_parts[p] = feed_forward(
            two[p], branch[p], gate_weight, up_weight, down_weight, kind
        )

    two = gather_near(normed_two, "mp")
    branch.update(gather_far(branch, "mp"))
    feed(0)
    feed(1)
    two, hidden, gate_back, up_back, two_parts, mlp_parts, branch = hold(
        (two, hidden, gate_back, up_back, two_parts, mlp_parts, branch)
    )

    two.update(gather_far(two, "mp"))
    for p in near[1:]:
        feed(p)
    branch_blocks = relative_blocks(stacked(branch), "dp")
    two, hidden, gate_back, up_back, two_parts, mlp_parts, branch, branch_blocks = hold(
        (two, hidden, gate_back, up_back, two_parts, mlp_parts, branch, branch_blocks)
    )

    mlp_near = reduce_near(mlp_parts, None, "mp", (1,))
    for p in far:
        feed(p)
    two, hidden, gate_back, up_back, two_parts, mlp_parts, mlp_near = hold(
        (two, hidden, gate_back, up_back, two_parts, mlp_parts, mlp_near)
    )

    two_far = reduce_far(two_parts, "mp")
    all_two = stacked(two)
    gate_product = product(all_two, stacked(gate_back))
    all_hidden, all_up_back = stacked(hidden), stacked(up_back)
    two_parts, two_far, all_hidden, all_up_back, _ = hold(
        (two_parts, two_far, all_hidden, all_up_back, gate_product)
    )

    two_near = reduce_near(two_parts, two_far, "mp")
    up_product = product(all_two, all_up_back)
    down_products = [product(all_hidden, half) for half in branch_blocks]
    two_near, mlp_parts, down_products, _ = hold(
        (two_near, mlp_parts, down_products, up_product)
    )

    def spread(value, dim):
        return lax.psum_scatter(value, "dp", scatter_dimension=dim, tiled=True).astype(F32)

    grad_gate = spread(gate_product, 0)
    grad_up = spread(up_product, 0)

    mlp_far = reduce_far(mlp_parts, "mp")
    down_sum = BlockSum(*down_products, "dp", 1)
    grad_normed_two = total(two_parts[0], two_near)
    grad_through, grad_mlp_gain = normed_back(
        state, inverse_rms(state), mlp_gain, grad_normed_two
    )
    grad_state = upstream + grad_through
    grad_attn = (grad_state * live).astype(LOW)
    grad_mixed = out_back(grad_attn, out_full)
    grad_mixed = stacked(swap_pieces({p: grad_mixed[p] for p in pieces}, "mp"))
    out_products = [product(mixed, half) for half in relative_blocks(grad_attn, "dp")]
    out_sum = BlockSum(*out_products, "dp", 1)
    down_sum.step(0)
    mlp_far, grad_mixed, out_sum.state, down_sum.state, mlp_parts, grad_state, grad_mlp_gain = hold(
        (mlp_far, grad_mixed, out_sum.state, down_sum.state, mlp_parts, grad_state, grad_mlp_gain)
    )

    out_sum.step(0)
    for k in range(1, down_sum.steps):
        down_sum.step(k)
    mlp_near.update(reduce_near(mlp_parts, mlp_far, "mp", near[1:]))
    grad_qkv, grad_mix = attend_back(
        qkv, grad_mixed, memories, normers, place, share, per_chunk
    )
    grad_qkv, grad_mix, down_sum.state, out_sum.state = hold(
        (grad_qkv, grad_mix, down_sum.state, out_sum.state)
    )
    one_parts = {}

    def project_back(p):
        value = rows_by(grad_qkv[p * row_count : (p + 1) * row_count], qkv_weight, (1, 1))
        one_parts[p] = value.astype(LOW) if p == 1 or p in far else value

    for p in far:
        project_back(p)
    one_parts, grad_qkv = hold((one_parts, grad_qkv))
    one_far = reduce_far(one_parts, "mp")
    qkv_products = [product(half, grad_qkv) for half in one_blocks]
    qkv_sum = BlockSum(*qkv_products, "dp", 0)
    for k in range(1, out_sum.steps):
        out_sum.step(k)
    for p in [0] + near:
        project_back(p)
    grad_down = down_sum.result()
    one_parts, one_far, mlp_near, out_sum.state, qkv_sum.state, grad_down = hold(
        (one_parts, one_far, mlp_near, out_sum.state, qkv_sum.state, grad_down)
    )

    one_near = reduce_near(one_parts, one_far, "mp")
    block_out = (state + live * total(mlp_parts[0], mlp_near)).astype(LOW)
    grad_attn_gain = (
        sum(jnp.sum(one[p].astype(F32) * one_parts[p].astype(F32), axis=0) for p in pieces)
        / attn_gain
    )
    grad_share = jnp.sum(grad_mix, axis=1) * share * (1.0 - share)
    share_full = lax.dynamic_update_slice(
        jnp.zeros((heads * ranks,), F32), grad_share, (rank * heads,)
    )
    small = sum_everywhere(
        jnp.concatenate([grad_attn_gain, grad_mlp_gain, share_full]), ("mp", "dp")
    )
    for k in range(qkv_sum.steps):
        qkv_sum.step(k)
    grad_proj = qkv_sum.result()
    grad_out_part = out_sum.result()
    one_near, small, grad_proj, grad_out_part = hold((one_near, small, grad_proj, grad_out_part))

    grad_query, grad_key, grad_value = (
        grad_proj[:, j * width : (j + 1) * width] for j in range(3)
    )
    out_parts = {p: grad_out_part[p * width : (p + 1) * width] for p in pieces}
    grad_out = total(
        out_parts[0], {p: hop(out_parts[p].astype(LOW), "mp", p) for p in range(1, ranks)}
    )
    grad_normed_one = total(one_parts[0], one_near)
    grad_inputs = normed_back(inputs, inverse_one, attn_gain, grad_normed_one)[0]
    grad_tokens = grad_state + grad_inputs
    return (
        block_out,
        grad_tokens,
        grad_query,
        grad_key,
        grad_value,
        grad_out,
        grad_gate,
        grad_up,
        grad_down,
        small[:features],
        small[features : 2 * features],
        small[2 * features :],
    )


def solution(mesh):
    return jax.shard_map(
        shards,
        mesh=mesh,
        in_specs=(
            P(("dp", "mp"), None),
            P(("dp", "mp"), None),
            P("dp"),
            P(None, "mp"),
            P(None, "mp"),
            P(None, "mp"),
            P("mp", None),
            P(None, "mp"),
            P(None, "mp"),
            P("mp", None),
            P(),
            P(),
            P("mp"),
        ),
        out_specs=(
            P(("dp", "mp"), None),
            P(("dp", "mp"), None),
            P("dp", "mp"),
            P("dp", "mp"),
            P("dp", "mp"),
            P("mp", "dp"),
            P("dp", "mp"),
            P("dp", "mp"),
            P("mp", "dp"),
            P(),
            P(),
            P(),
        ),
        check_vma=False,
    )
```

time: 1880 us -> 677 us (0.36)
  waiting for transfers between devices: 1250 us -> 240 us
  matrix products: 406 us -> 79.1 us
  Pallas kernels: 0 us -> 128 us
  starting transfers between devices: 0.87 us -> 72.6 us
  blocking collectives: 40.7 us -> 0 us
  local copies, waits for them, and re-layouts: 79.6 us -> 44.5 us
    reduce_scatter x11 -> x2, waiting for transfers between devices: 959 us -> 0.01 us  [spread(): lax.psum_scatter(value, 'dp', scatter_dimension=dim, tiled=True).astype(F32)]
    dot_general x131 -> x16, matrix products: 406 us -> 79.1 us  [rows_by(): lax.dot_general(left, right, ((contract[:1], contract[1:]), ((), ())), pr...]
    all_gather x4 -> x1, waiting for transfers between devices: 289 us -> 0.01 us  [shards(): lax.all_gather(jnp.stack([out_slices[p] for p in pieces]), 'dp', axis=0,...]
    ppermute x0 -> x50, waiting for transfers between devices: none -> 240 us  [hop(): return lax.ppermute(value, axis, [(j, j ^ mask) for j in range(size)])]
    pallas_call x0 -> x8, Pallas kernels: none -> 128 us  [the longest x4 76.1 us: feed_forward(): pl.pallas_call(feed_kernel, name='feed_forward', out_shape=(*[jax.ShapeDt...]
    ppermute x0 -> x50, starting transfers between devices: none -> 72.5 us  [hop(): return lax.ppermute(value, axis, [(j, j ^ mask) for j in range(size)])]
    psum x1 -> x0, blocking collectives: 40.7 us -> none  [shards(): lax.psum((grad_attn_gain_part, grad_mlp_gain_part, gate_full), ('dp', 'mp'))]
    dynamic_update_slice x49 -> x1, other arithmetic: 30.6 us -> 0.09 us  [shards(): lax.dynamic_update_slice(jnp.zeros((heads * ranks,), F32), grad_share, (r...]
  transfers between devices with their start and end apart: 15 -> 53, of which waited for: 15 -> 24; matrix products, arithmetic and copies ran while one was open for 7% -> 25% of each run, Pallas kernels for 0% -> 18%
where the time goes in v1:
time: 677 us; the launch traced here: 666 us
  waiting for transfers between devices  240 us (35%)
  Pallas kernels  128 us (19%)
  other arithmetic  86.3 us (13%)
  matrix products  79.1 us (12%)
  starting transfers between devices  72.6 us (11%)
  local copies, waits for them, and re-layouts  44.5 us (7%)
  between operations  16 us (2%)
    ppermute x50, waiting for transfers between devices, hop(): return lax.ppermute(value, axis, [(j, j ^ mask) for j in range(size)])  240 us
    dot_general x16, matrix products, rows_by(): lax.dot_general(left, right, ((contract[:1], contract[1:]), ((), ())), pr...  79.1 us
    pallas_call x4, Pallas kernels, feed_forward(): pl.pallas_call(feed_kernel, name='feed_forward', out_shape=(*[jax.ShapeDt...  76.1 us
    ppermute x50, starting transfers between devices, hop(): return lax.ppermute(value, axis, [(j, j ^ mask) for j in range(size)])  72.5 us
    unnamed x236, local copies, waits for them, and re-layouts  36.4 us
    pallas_call x1, Pallas kernels, attend_back(): pl.pallas_call(attend_back_kernel, name='attend_back', out_shape=(jax.Sha...  28.5 us
    add x13, other arithmetic, land(): held[r ^ order[k]] + self.flight[low][n].astype(F32)  17.7 us
    pallas_call x1, Pallas kernels, attend(): pl.pallas_call(attend_kernel, name='attend', out_shape=(jax.ShapeDtypeStr...  14.6 us
  transfers between devices with their start and end apart: 53, of which 24 were waited for; matrix products, arithmetic and copies ran while one was open for 25% of the time, Pallas kernels for 18%

profile of v1, /device:TPU:8, one launch (start us, length us, event | category | flops | bytes accessed | tf_op | source)
XLA Modules:
  0.0 665.9 jit_solution(9981136801877135501)
XLA Ops:
  31.5 36.0 %collective-permute-done.1 = bf16[256,2048]{1,0:T(8,128)(2,1)S(1)} collective-permute-done((bf16[256,2048]{1,0:T(8,128)(2,1)S(1)}, bf16[256,2048]{1,0:T(8,128)(2,1)S(1)}, u32[]{:S(2)}, u32[]{:S(2)}) %collective-permute-start.1) | collective-permute-done | bytes 1048608 | tf_op jit(solution)/shard_map/ppermute | solution.py:20
  78.1 20.4 %collective-permute-done.4 = bf16[256,2048]{1,0:T(8,128)(2,1)S(1)} collective-permute-done((bf16[256,2048]{1,0:T(8,128)(2,1)S(1)}, bf16[256,2048]{1,0:T(8,128)(2,1)S(1)}, u32[]{:S(2)}, u32[]{:S(2)}) %collective-permute-start.4) | collective-permute-done | bytes 1048608 | tf_op jit(solution)/shard_map/ppermute | solution.py:20
  115.5 14.6 %attend.1 = (bf16[1024,512]{1,0:T(8,128)(2,1)S(1)}, f32[8,4,128,128]{3,2,1,0:T(8,128)S(1)}, f32[8,4,128]{2,1,0:T(4,128)S(1)}) custom-call(s32[2]{0:T(128)S(1)} %pad_add_fusion.place, f32[4]{0:T(128)S(1)} %add_divide_fusion.1.share, bf16[1024,1536]{1,0:T(8,128)(2,1)S(1)} %pad_maximum_fusion.2.qkv_ref), custom_call_target="tpu_custom_call" | custom-call | flops 7516192768 | bytes 6291456 | tf_op jit(solution)/shard_map/attend/pallas_call | solution.py:322
  134.5 32.7 %collective-permute-done.8.refs_3_ = bf16[256,512]{1,0:T(8,128)(2,1)S(1)} collective-permute-done((bf16[256,512]{1,0:T(8,128)(2,1)S(1)}, bf16[256,512]{1,0:T(8,128)(2,1)S(1)}, u32[]{:S(2)}, u32[]{:S(2)}) %collective-permute-start.8) | collective-permute-done | bytes 262176 | tf_op jit(solution)/shard_map/ppermute | solution.py:20
  192.1 18.2 %feed_forward.4 = (bf16[256,2048]{1,0:T(8,128)(2,1)S(1)}, bf16[256,2048]{1,0:T(8,128)(2,1)S(1)}, bf16[256,2048]{1,0:T(8,128)(2,1)S(1)}, f32[256,2048]{1,0:T(8,128)S(1)}, f32[256,2048]{1,0:T(8,128)S(1)}) custom-call(bf16[256,2048]{1,0:T(8,128)(2,1)S(1)} %get-tuple-element.294.rows_ref, bf16[256,2048]{1,0:T(8,128)(2,1)S(1)} %copy-done.7, ...), custom_call_target="tpu_custom_call" | custom-call | flops 12884901888 | bytes 25165824 | tf_op jit(solution)/shard_map/feed_forward/pallas_call | solution.py:544
  213.6 21.1 %collective-permute-done.11.rows_ref = bf16[256,2048]{1,0:T(8,128)(2,1)S(1)} collective-permute-done((bf16[256,2048]{1,0:T(8,128)(2,1)S(1)}, bf16[256,2048]{1,0:T(8,128)(2,1)S(1)}, u32[]{:S(2)}, u32[]{:S(2)}) %collective-permute-start.11) | collective-permute-done | bytes 1048608 | tf_op jit(solution)/shard_map/ppermute | solution.py:20
  234.6 19.6 %feed_forward.5 = (bf16[256,2048]{1,0:T(8,128)(2,1)S(1)}, bf16[256,2048]{1,0:T(8,128)(2,1)S(1)}, bf16[256,2048]{1,0:T(8,128)(2,1)S(1)}, bf16[256,2048]{1,0:T(8,128)(2,1)}, bf16[256,2048]{1,0:T(8,128)(2,1)S(1)}) custom-call(bf16[256,2048]{1,0:T(8,128)(2,1)S(1)} %collective-permute-done.11.rows_ref, bf16[256,2048]{1,0:T(8,128)(2,1)S(1)} %copy-done.27, ...), custom_call_target="tpu_custom_call" | custom-call | flops 12884901888 | bytes 25165824 | tf_op jit(solution)/shard_map/feed_forward/pallas_call | solution.py:544
  262.6 18.2 %feed_forward.6 = (bf16[256,2048]{1,0:T(8,128)(2,1)S(1)}, bf16[256,2048]{1,0:T(8,128)(2,1)S(1)}, bf16[256,2048]{1,0:T(8,128)(2,1)S(1)}, f32[256,2048]{1,0:T(8,128)S(1)}, f32[256,2048]{1,0:T(8,128)S(1)}) custom-call(bf16[256,2048]{1,0:T(8,128)(2,1)S(1)} %collective-permute-done.12.rows_ref, bf16[256,2048]{1,0:T(8,128)(2,1)S(1)} %copy-done.25, ...), custom_call_target="tpu_custom_call" | custom-call | flops 12884901888 | bytes 25165824 | tf_op jit(solution)/shard_map/feed_forward/pallas_call | solution.py:544
  283.0 20.2 %feed_forward.7 = (bf16[256,2048]{1,0:T(8,128)(2,1)S(1)}, bf16[256,2048]{1,0:T(8,128)(2,1)S(1)}, bf16[256,2048]{1,0:T(8,128)(2,1)S(1)}, bf16[256,2048]{1,0:T(8,128)(2,1)S(1)}, bf16[256,2048]{1,0:T(8,128)(2,1)}) custom-call(bf16[256,2048]{1,0:T(8,128)(2,1)S(1)} %collective-permute-done.14.rows_ref, bf16[256,2048]{1,0:T(8,128)(2,1)S(1)} %collective-permute-done.13.branch_ref, ...), custom_call_target="tpu_custom_call" | custom-call | flops 12884901888 | bytes 25165824 | tf_op jit(solution)/shard_map/feed_forward/pallas_call | solution.py:544
  310.1 11.5 %convolution_convert_fusion.1 = bf16[2048,2048]{1,0:T(8,128)(2,1)} fusion(bf16[1024,2048]{1,0:T(8,128)(2,1)S(1)} %constant_dynamic-update-slice_fusion.11, bf16[256,2048]{1,0:T(8,128)(2,1)S(1)} %get-tuple-element.301, bf16[256,2048]{1,0:T(8,128)(2,1)S(1)} %get-tuple-element.300, bf16[256,2048]{1,0:T(8,128)(2,1)S(1)} %get-tuple-element.299, ...), kind=kOutput, calls=%fused_computation.1 | convolution fusion | flops 8610906112 | bytes 16777216 | tf_op jit(solution)/shard_map/dot_general | solution.py:163
  328.9 17.5 %collective-permute-done.16 = bf16[256,2048]{1,0:T(8,128)(2,1)S(1)} collective-permute-done((bf16[256,2048]{1,0:T(8,128)(2,1)}, bf16[256,2048]{1,0:T(8,128)(2,1)S(1)}, u32[]{:S(2)}, u32[]{:S(2)}) %collective-permute-start.16) | collective-permute-done | bytes 1048608 | tf_op jit(solution)/shard_map/ppermute | solution.py:20
  351.6 11.4 %convolution_convert_fusion = bf16[2048,2048]{1,0:T(8,128)(2,1)} fusion(bf16[1024,2048]{1,0:T(8,128)(2,1)S(1)} %copy-done.94, bf16[1024,2048]{1,0:T(8,128)(2,1)S(1)} %pad_maximum_fusion.1), kind=kOutput, calls=%fused_computation | convolution fusion | flops 8594128896 | bytes 16777216 | tf_op jit(solution)/shard_map/dot_general | solution.py:163
  363.0 9.6 %convolution_convert_fusion.6 = bf16[2048,1024]{1,0:T(8,128)(2,1)} fusion(bf16[1024,2048]{1,0:T(8,128)(2,1)} %pad_maximum_fusion, bf16[1024,1024]{1,0:T(8,128)(2,1)} %pad_maximum_fusion.6), kind=kOutput, calls=%fused_computation.15 | convolution fusion | flops 4297064448 | bytes 10485760 | tf_op jit(solution)/shard_map/dot_general | solution.py:163
  377.7 15.4 %collective-permute-done.18 = bf16[256,2048]{1,0:T(8,128)(2,1)} collective-permute-done((bf16[256,2048]{1,0:T(8,128)(2,1)}, bf16[256,2048]{1,0:T(8,128)(2,1)}, u32[]{:S(2)}, u32[]{:S(2)}) %collective-permute-start.18) | collective-permute-done | bytes 1048608 | tf_op jit(solution)/shard_map/ppermute | solution.py:20
  421.0 5.9 collective-permute-done.22
  427.0 12.5 %collective-permute-start.21 = (bf16[256,512]{1,0:T(8,128)(2,1)}, bf16[256,512]{1,0:T(8,128)(2,1)}, u32[]{:S(2)}, u32[]{:S(2)}) collective-permute-start(bf16[256,512]{1,0:T(8,128)(2,1)} %get-tuple-element.435), channel_id=1, source_target_pairs={{0,2},{1,3},{2,0},{3,1},{4,6},{5,7},{6,4},{7,5},{8,10},{9,11},{10,... | collective-permute-start | bytes 786440 | tf_op jit(solution)/shard_map/ppermute | solution.py:20
  439.5 10.2 %collective-permute-done.21 = bf16[256,512]{1,0:T(8,128)(2,1)} collective-permute-done((bf16[256,512]{1,0:T(8,128)(2,1)}, bf16[256,512]{1,0:T(8,128)(2,1)}, u32[]{:S(2)}, u32[]{:S(2)}) %collective-permute-start.21) | collective-permute-done | bytes 262176 | tf_op jit(solution)/shard_map/ppermute | solution.py:20
  477.3 28.5 %attend_back.1 = (bf16[1024,1536]{1,0:T(8,128)(2,1)S(1)}, f32[4,128]{1,0:T(4,128)S(1)}) custom-call(s32[2]{0:T(128)S(1)} %pad_add_fusion.place, f32[4]{0:T(128)S(1)} %add_divide_fusion.1.share, bf16[1024,1536]{1,0:T(8,128)(2,1)S(1)} %copy-done.9, bf16[1024,512]{1,0:T(8,128)(2,1)S(1)} %pad_maximum_fusion.11.grad_ref, f32[8,4,128,128]{3,2,1,0:T(8,128)S(1)} %copy-done.48, ...), custom_call_target="tpu_custom_call" | custom-call | flops 16106127360 | bytes 9437184 | tf_op jit(solution)/shard_map/attend_back/pallas_call | solution.py:363
  510.6 14.6 %collective-permute-done.30 = bf16[2,1024,256]{2,1,0:T(8,128)(2,1)S(1)} collective-permute-done((bf16[2,1024,256]{2,1,0:T(8,128)(2,1)S(1)}, bf16[2,1024,256]{2,1,0:T(8,128)(2,1)S(1)}, u32[]{:S(2)}, u32[]{:S(2)}) %collective-permute-start.30) | collective-permute-done | bytes 1048608 | tf_op jit(solution)/shard_map/ppermute | solution.py:20
  544.6 5.7 convolution_convert_fusion.8
  568.1 12.4 %collective-permute-done.43 = bf16[2,128,1536]{2,1,0:T(8,128)(2,1)S(1)} collective-permute-done((bf16[2,128,1536]{2,1,0:T(8,128)(2,1)S(1)}, bf16[2,128,1536]{2,1,0:T(8,128)(2,1)S(1)}, u32[]{:S(2)}, u32[]{:S(2)}) %collective-permute-start.43) | collective-permute-done | bytes 786464 | tf_op jit(solution)/shard_map/ppermute | solution.py:20
  592.4 17.3 %collective-permute-done.44 = bf16[1,128,1536]{2,1,0:T(8,128)(2,1)S(1)} collective-permute-done((bf16[1,128,1536]{2,1,0:T(8,128)(2,1)S(1)}, bf16[1,128,1536]{2,1,0:T(8,128)(2,1)S(1)}, u32[]{:S(2)}, u32[]{:S(2)}) %collective-permute-start.44) | collective-permute-done | bytes 393248 | tf_op jit(solution)/shard_map/ppermute | solution.py:20
  624.1 7.9 %collective-permute-done.37 = bf16[256,2048]{1,0:T(8,128)(2,1)} collective-permute-done((bf16[256,2048]{1,0:T(8,128)(2,1)}, bf16[256,2048]{1,0:T(8,128)(2,1)}, u32[]{:S(2)}, u32[]{:S(2)}) %collective-permute-start.37) | collective-permute-done | bytes 1048608 | tf_op jit(solution)/shard_map/ppermute | solution.py:20
  648.9 6.1 collective-permute-done.49
  (434 shorter events, 262.6 us)
Async XLA Ops:
  7.2 168.1 %all-gather.2.cloned.1.call-start = ((), (), s32[]{:S(2)}) async-start(), calls=%async_computation.2 | async-start | bytes 9437184 | tf_op jit(solution)/shard_map/all_gather | solution.py:643
  15.0 52.5 %collective-permute-start.1 = (bf16[256,2048]{1,0:T(8,128)(2,1)S(1)}, bf16[256,2048]{1,0:T(8,128)(2,1)S(1)}, u32[]{:S(2)}, u32[]{:S(2)}) collective-permute-start(bf16[256,2048]{1,0:T(8,128)(2,1)S(1)} %fusion.10), channel_id=1, source_target_pairs={{0,2},{1,3},{2,0},{3,1},{4,6},{5,7},{6,4},{7,5},{8,10},{9,11},{10,... | collective-permute-start | bytes 3145736 | tf_op jit(solution)/shard_map/ppermute | solution.py:20
  15.1 53.5 %collective-permute-start = (bf16[256,2048]{1,0:T(8,128)(2,1)S(1)}, bf16[256,2048]{1,0:T(8,128)(2,1)}, u32[]{:S(2)}, u32[]{:S(2)}) collective-permute-start(bf16[256,2048]{1,0:T(8,128)(2,1)S(1)} %fusion.10), channel_id=1, source_target_pairs={{0,1},{1,0},{2,3},{3,2},{4,5},{5,4},{6,7},{7,6},{8,9},{9,8},{10,11... | collective-permute-start | bytes 3145736 | tf_op jit(solution)/shard_map/ppermute | solution.py:20
  101.7 517.2 %reduce-scatter.3.cloned.1.call-start = ((), (), s32[]{:S(2)}) async-start(), calls=%async_computation.3 | async-start | bytes 9437184 | tf_op jit(solution)/shard_map/reduce_scatter | solution.py:710
  101.8 71.5 %collective-permute-start.10 = (bf16[256,2048]{1,0:T(8,128)(2,1)S(1)}, bf16[256,2048]{1,0:T(8,128)(2,1)S(1)}, u32[]{:S(2)}, u32[]{:S(2)}) collective-permute-start(bf16[256,2048]{1,0:T(8,128)(2,1)S(1)} %fusion.16.branch_ref), channel_id=1, source_target_pairs={{0,2},{1,3},{2,0},{3,1},{4,6},{5,7},{6,4},{7,5},{8,10},{9,11},{10,... | collective-permute-start | bytes 3145736 | tf_op jit(solution)/shard_map/ppermute | solution.py:20
  105.2 69.1 %collective-permute-start.9 = (bf16[256,2048]{1,0:T(8,128)(2,1)S(1)}, bf16[256,2048]{1,0:T(8,128)(2,1)S(1)}, u32[]{:S(2)}, u32[]{:S(2)}) collective-permute-start(bf16[256,2048]{1,0:T(8,128)(2,1)S(1)} %fusion.16.branch_ref), channel_id=1, source_target_pairs={{0,1},{1,0},{2,3},{3,2},{4,5},{5,4},{6,7},{7,6},{8,9},{9,8},{10,11... | collective-permute-start | bytes 3145736 | tf_op jit(solution)/shard_map/ppermute | solution.py:20
  130.3 41.6 %collective-permute-start.7 = (bf16[256,512]{1,0:T(8,128)(2,1)S(1)}, bf16[256,512]{1,0:T(8,128)(2,1)S(1)}, u32[]{:S(2)}, u32[]{:S(2)}) collective-permute-start(bf16[256,512]{1,0:T(8,128)(2,1)S(1)} %get-tuple-element.438), channel_id=1, source_target_pairs={{0,2},{1,3},{2,0},{3,1},{4,6},{5,7},{6,4},{7,5},{8,10},{9,11},{10,... | collective-permute-start | bytes 786440 | tf_op jit(solution)/shard_map/ppermute | solution.py:20
  186.6 69.1 %collective-permute-start.12 = (bf16[256,2048]{1,0:T(8,128)(2,1)S(1)}, bf16[256,2048]{1,0:T(8,128)(2,1)S(1)}, u32[]{:S(2)}, u32[]{:S(2)}) collective-permute-start(bf16[256,2048]{1,0:T(8,128)(2,1)S(1)} %get-tuple-element.294.rows_ref), channel_id=1, source_target_pairs={{0,2},{1,3},{2,0},{3,1},{4,6},{5,7},{6,4},{7,5},{8,10},{9,11},{10,... | collective-permute-start | bytes 3145736 | tf_op jit(solution)/shard_map/ppermute | solution.py:20
  190.1 44.6 %collective-permute-start.11 = (bf16[256,2048]{1,0:T(8,128)(2,1)S(1)}, bf16[256,2048]{1,0:T(8,128)(2,1)S(1)}, u32[]{:S(2)}, u32[]{:S(2)}) collective-permute-start(bf16[256,2048]{1,0:T(8,128)(2,1)S(1)} %get-tuple-element.294.rows_ref), channel_id=1, source_target_pairs={{0,1},{1,0},{2,3},{3,2},{4,5},{5,4},{6,7},{7,6},{8,9},{9,8},{10,11... | collective-permute-start | bytes 3145736 | tf_op jit(solution)/shard_map/ppermute | solution.py:20
  190.1 65.7 %collective-permute-start.13 = (bf16[256,2048]{1,0:T(8,128)(2,1)S(1)}, bf16[256,2048]{1,0:T(8,128)(2,1)S(1)}, u32[]{:S(2)}, u32[]{:S(2)}) collective-permute-start(bf16[256,2048]{1,0:T(8,128)(2,1)S(1)} %copy-done.25), channel_id=1, source_target_pairs={{0,1},{1,0},{2,3},{3,2},{4,5},{5,4},{6,7},{7,6},{8,9},{9,8},{10,11... | collective-permute-start | bytes 3145736 | tf_op jit(solution)/shard_map/ppermute | solution.py:20
  321.6 324.5 %reduce-scatter.5.cloned.1.call-start = ((), (), s32[]{:S(2)}) async-start(), calls=%async_computation.4 | async-start | bytes 9437184 | tf_op jit(solution)/shard_map/reduce_scatter | solution.py:710
  347.7 45.5 %collective-permute-start.18 = (bf16[256,2048]{1,0:T(8,128)(2,1)}, bf16[256,2048]{1,0:T(8,128)(2,1)}, u32[]{:S(2)}, u32[]{:S(2)}) collective-permute-start(bf16[256,2048]{1,0:T(8,128)(2,1)} %add_convert_fusion.3), channel_id=1, source_target_pairs={{0,2},{1,3},{2,0},{3,1},{4,6},{5,7},{6,4},{7,5},{8,10},{9,11},{10,... | collective-permute-start | bytes 3145736 | tf_op jit(solution)/shard_map/ppermute | solution.py:20
  350.4 44.0 %collective-permute-start.17 = (bf16[256,2048]{1,0:T(8,128)(2,1)}, bf16[256,2048]{1,0:T(8,128)(2,1)}, u32[]{:S(2)}, u32[]{:S(2)}) collective-permute-start(bf16[256,2048]{1,0:T(8,128)(2,1)} %get-tuple-element.302), channel_id=1, source_target_pairs={{0,1},{1,0},{2,3},{3,2},{4,5},{5,4},{6,7},{7,6},{8,9},{9,8},{10,11... | collective-permute-start | bytes 3145736 | tf_op jit(solution)/shard_map/ppermute | solution.py:20
  405.6 54.9 %collective-permute-start.23 = (bf16[2048,1024]{1,0:T(8,128)(2,1)}, bf16[2048,1024]{1,0:T(8,128)(2,1)}, u32[]{:S(2)}, u32[]{:S(2)}) collective-permute-start(bf16[2048,1024]{1,0:T(8,128)(2,1)} %convolution_convert_fusion.2), channel_id=1, source_target_pairs={{0,4},{4,0},{8,12},{12,8},{16,20},{20,16},{24,28},{28,24},{1,5},{5... | collective-permute-start | bytes 12582920 | tf_op jit(solution)/shard_map/ppermute | solution.py:20
  406.1 54.3 %collective-permute-start.19 = (bf16[256,2048]{1,0:T(8,128)(2,1)}, bf16[256,2048]{1,0:T(8,128)(2,1)}, u32[]{:S(2)}, u32[]{:S(2)}) collective-permute-start(bf16[256,2048]{1,0:T(8,128)(2,1)} %get-tuple-element.312), channel_id=1, source_target_pairs={{0,1},{1,0},{2,3},{3,2},{4,5},{5,4},{6,7},{7,6},{8,9},{9,8},{10,11... | collective-permute-start | bytes 3145736 | tf_op jit(solution)/shard_map/ppermute | solution.py:20
  414.5 46.0 %collective-permute-start.26 = (bf16[2,1024,256]{2,1,0:T(8,128)(2,1)}, bf16[2,1024,256]{2,1,0:T(8,128)(2,1)}, u32[]{:S(2)}, u32[]{:S(2)}) collective-permute-start(bf16[2,1024,256]{2,1,0:T(8,128)(2,1)} %pad_maximum_fusion.13), channel_id=1, source_target_pairs={{0,16},{4,20},{8,24},{12,28},{16,0},{20,4},{24,8},{28,12},{1,17},{... | collective-permute-start | bytes 3145736 | tf_op jit(solution)/shard_map/ppermute | solution.py:20
  417.1 43.3 %collective-permute-start.25 = (bf16[2,1024,256]{2,1,0:T(8,128)(2,1)}, bf16[2,1024,256]{2,1,0:T(8,128)(2,1)}, u32[]{:S(2)}, u32[]{:S(2)}) collective-permute-start(bf16[2,1024,256]{2,1,0:T(8,128)(2,1)} %pad_maximum_fusion.12), channel_id=1, source_target_pairs={{0,8},{4,12},{8,0},{12,4},{16,24},{20,28},{24,16},{28,20},{1,9},{5... | collective-permute-start | bytes 3145736 | tf_op jit(solution)/shard_map/ppermute | solution.py:20
  461.7 48.9 %collective-permute-start.28 = (bf16[1,1024,256]{2,1,0:T(8,128)(2,1)S(1)}, bf16[1,1024,256]{2,1,0:T(8,128)(2,1)S(1)}, u32[]{:S(2)}, u32[]{:S(2)}) collective-permute-start(bf16[1,1024,256]{2,1,0:T(8,128)(2,1)S(1)} %bitcast.156), channel_id=1, source_target_pairs={{0,8},{4,12},{8,0},{12,4},{16,24},{20,28},{24,16},{28,20},{1,9},{5... | collective-permute-start | bytes 1572872 | tf_op jit(solution)/shard_map/ppermute | solution.py:20
  464.4 46.2 %collective-permute-start.27 = (bf16[1,1024,256]{2,1,0:T(8,128)(2,1)S(1)}, bf16[1,1024,256]{2,1,0:T(8,128)(2,1)S(1)}, u32[]{:S(2)}, u32[]{:S(2)}) collective-permute-start(bf16[1,1024,256]{2,1,0:T(8,128)(2,1)S(1)} %bitcast.157), channel_id=1, source_target_pairs={{0,16},{4,20},{8,24},{12,28},{16,0},{20,4},{24,8},{28,12},{1,17},{... | collective-permute-start | bytes 1572872 | tf_op jit(solution)/shard_map/ppermute | solution.py:20
  468.4 89.7 %collective-permute-start.32 = (bf16[256,2048]{1,0:T(8,128)(2,1)}, bf16[256,2048]{1,0:T(8,128)(2,1)}, u32[]{:S(2)}, u32[]{:S(2)}) collective-permute-start(bf16[256,2048]{1,0:T(8,128)(2,1)} %add_convert_fusion.2), channel_id=1, source_target_pairs={{0,2},{1,3},{2,0},{3,1},{4,6},{5,7},{6,4},{7,5},{8,10},{9,11},{10,... | collective-permute-start | bytes 3145736 | tf_op jit(solution)/shard_map/ppermute | solution.py:20
  475.5 49.7 %collective-permute-start.30 = (bf16[2,1024,256]{2,1,0:T(8,128)(2,1)S(1)}, bf16[2,1024,256]{2,1,0:T(8,128)(2,1)S(1)}, u32[]{:S(2)}, u32[]{:S(2)}) collective-permute-start(bf16[2,1024,256]{2,1,0:T(8,128)(2,1)S(1)} %pad_maximum_fusion.15), channel_id=1, source_target_pairs={{0,16},{4,20},{8,24},{12,28},{16,0},{20,4},{24,8},{28,12},{1,17},{... | collective-permute-start | bytes 3145736 | tf_op jit(solution)/shard_map/ppermute | solution.py:20
  476.2 49.1 %collective-permute-start.29 = (bf16[2,1024,256]{2,1,0:T(8,128)(2,1)S(1)}, bf16[2,1024,256]{2,1,0:T(8,128)(2,1)S(1)}, u32[]{:S(2)}, u32[]{:S(2)}) collective-permute-start(bf16[2,1024,256]{2,1,0:T(8,128)(2,1)S(1)} %pad_maximum_fusion.14), channel_id=1, source_target_pairs={{0,8},{4,12},{8,0},{12,4},{16,24},{20,28},{24,16},{28,20},{1,9},{5... | collective-permute-start | bytes 3145736 | tf_op jit(solution)/shard_map/ppermute | solution.py:20
  584.3 47.8 %collective-permute-start.36 = (bf16[256,2048]{1,0:T(8,128)(2,1)}, bf16[256,2048]{1,0:T(8,128)(2,1)}, u32[]{:S(2)}, u32[]{:S(2)}) collective-permute-start(bf16[256,2048]{1,0:T(8,128)(2,1)} %convolution_convert_fusion.8), channel_id=1, source_target_pairs={{0,1},{1,0},{2,3},{3,2},{4,5},{5,4},{6,7},{7,6},{8,9},{9,8},{10,11... | collective-permute-start | bytes 3145736 | tf_op jit(solution)/shard_map/ppermute | solution.py:20
  585.7 46.3 %collective-permute-start.37 = (bf16[256,2048]{1,0:T(8,128)(2,1)}, bf16[256,2048]{1,0:T(8,128)(2,1)}, u32[]{:S(2)}, u32[]{:S(2)}) collective-permute-start(bf16[256,2048]{1,0:T(8,128)(2,1)} %get-tuple-element.418), channel_id=1, source_target_pairs={{0,2},{1,3},{2,0},{3,1},{4,6},{5,7},{6,4},{7,5},{8,10},{9,11},{10,... | collective-permute-start | bytes 3145736 | tf_op jit(solution)/shard_map/ppermute | solution.py:20
  (140 other events, 1920.7 us)
Sparse Core Ops, SparseCore 0:
  101.8 56.2 all-gather.1
  321.8 72.2 reduce-scatter.2
  439.6 99.6 reduce-scatter.4

commit v2 on v1

--- a/solution.py
+++ b/solution.py
@@ -13,6 +13,7 @@
 NEGATIVE = -1e30
 LOW = jnp.bfloat16
 F32 = jnp.float32
+BRIEF = pl.CostEstimate(flops=1, bytes_accessed=1, transcendentals=0)
 
 
 def hop(value, axis, mask):
@@ -89,65 +90,57 @@
     )
 
 
-class BlockSum:
-    def __init__(self, kept, sent, axis, dim):
-        self.axis, self.dim, self.kept = axis, dim, kept
-        self.size = lax.axis_size(axis)
-        self.masks = [1 << b for b in range(1, self.size.bit_length() - 1)]
-        self.flight = hop(sent, axis, 1)
-        self.halves = None
-
-    def part(self, value, j, low):
-        step = self.kept.shape[self.dim] // (self.size // 2)
-        if self.dim == 0:
-            half = step // 2
-            return value[j * step + low * half : j * step + (low + 1) * half].astype(F32)
-        half = self.kept.shape[0] // 2
-        return value[low * half : (low + 1) * half, j * step : (j + 1) * step].astype(F32)
-
-    def step(self, k):
-        if k == 0:
-            self.halves = [
-                {
-                    2 * j: self.part(self.kept, j, low) + self.part(self.flight, j, low)
-                    for j in range(self.size // 2)
-                }
-                for low in (0, 1)
-            ]
-        else:
-            self.land(k - 1)
-        self.flight = []
-        for low, order in ((0, self.masks), (1, self.masks[::-1])):
-            held = self.halves[low]
-            gone = [r for r in held if r & order[k]]
-            self.flight.append(
-                hop(jnp.stack([held[r] for r in gone]).astype(LOW), self.axis, order[k])
-            )
-
-    def land(self, k):
-        for low, order in ((0, self.masks), (1, self.masks[::-1])):
-            held = self.halves[low]
-            gone = [r for r in held if r & order[k]]
-            self.halves[low] = {
-                r ^ order[k]: held[r ^ order[k]] + self.flight[low][n].astype(F32)
-                for n, r in enumerate(gone)
-            }
-
-    @property
-    def steps(self):
-        return len(self.masks)
+class DeviceSum:
+    def __init__(self, parts, axis):
+        self.keep, self.send = [parts[0], parts[2]], [parts[1], parts[3]]
+        self.axis, self.turn = axis, 0
+        self.flight = None
+
+    def masks(self):
+        return 2 << self.turn, (lax.axis_size(self.axis) // 2) >> self.turn
+
+    def land(self):
+        self.turn += 1
+        for side in (0, 1):
+            value = self.keep[side].astype(F32) + self.flight[side].astype(F32)
+            half = value.shape[0] // 2
+            if half and side == 0:
+                self.keep[0], self.send[0] = value[0::2], value[1::2].astype(LOW)
+            elif half:
+                self.keep[1], self.send[1] = value[:half], value[half:].astype(LOW)
+            else:
+                self.keep[side] = value
 
     def result(self):
-        self.land(self.steps - 1)
-        return jnp.concatenate([half[0] for half in self.halves], axis=0)
+        return jnp.concatenate([value[0] for value in self.keep], axis=0)
 
     @property
     def state(self):
-        return self.kept, self.flight, self.halves
+        return self.keep, self.send, self.flight
 
     @state.setter
     def state(self, value):
-        self.kept, self.flight, self.halves = value
+        self.keep, self.send, self.flight = value
+
+
+def fly(*sums):
+    groups = {}
+    for one in sums:
+        one.flight = [None, None]
+        for side, mask in enumerate(one.masks()):
+            groups.setdefault((mask, one.send[side].shape[-1]), []).append((one, side))
+    for (mask, wide), parts in sorted(groups.items(), key=lambda item: item[0]):
+        rows = [one.send[side].reshape(-1, wide) for one, side in parts]
+        flight = hop(jnp.concatenate(rows, axis=0), sums[0].axis, mask)
+        start = 0
+        for (one, side), some in zip(parts, rows):
+            end = start + some.shape[0]
+            one.flight[side] = flight[start:end].reshape(one.send[side].shape)
+            start = end
+
+
+def device_steps(axis):
+    return (lax.axis_size(axis) // 2).bit_length() - 1
 
 
 def sum_everywhere(vector, axes):
@@ -344,11 +337,7 @@
         compiler_params=pltpu.CompilerParams(
             dimension_semantics=("arbitrary",), vmem_limit_bytes=24 << 20
         ),
-        cost_estimate=pl.CostEstimate(
-            flops=blocks * heads * 14 * 2 * SEG**3 * 4,
-            bytes_accessed=rows * wide * 4,
-            transcendentals=0,
-        ),
+        cost_estimate=BRIEF,
     )(place, share, qkv)
 
 
@@ -389,7 +378,7 @@
             dimension_semantics=("arbitrary",), vmem_limit_bytes=24 << 20
         ),
         cost_estimate=pl.CostEstimate(
-            flops=blocks * heads * 30 * 2 * SEG**3 * 4,
+            flops=blocks * heads * 240 * SEG**3,
             bytes_accessed=rows * wide * 6,
             transcendentals=0,
         ),
@@ -454,11 +443,7 @@
         compiler_params=pltpu.CompilerParams(
             dimension_semantics=("arbitrary",), vmem_limit_bytes=24 << 20
         ),
-        cost_estimate=pl.CostEstimate(
-            flops=2 * rows * features * ranks * width,
-            bytes_accessed=2 * ranks * width * features,
-            transcendentals=0,
-        ),
+        cost_estimate=BRIEF,
     )(place, *[mixed[p] for p in range(ranks)], out_full, tokens, gain[None])
 
 
@@ -481,23 +466,20 @@
         compiler_params=pltpu.CompilerParams(
             dimension_semantics=("arbitrary",), vmem_limit_bytes=24 << 20
         ),
-        cost_estimate=pl.CostEstimate(
-            flops=2 * rows * features * ranks * width,
-            bytes_accessed=2 * ranks * width * features,
-            transcendentals=0,
-        ),
+        cost_estimate=BRIEF,
     )(grad_attn, out_full)
 
 
 def feed_kernel(
+    place,
     rows_ref,
     branch_ref,
     gate_ref,
     up_ref,
     down_ref,
-    hidden_ref,
-    gate_back_ref,
-    up_back_ref,
+    made_ref,
+    kept_ref,
+    sent_ref,
     two_ref,
     mlp_ref,
     two_sum,
@@ -509,6 +491,14 @@
     def _():
         two_sum[...] = jnp.zeros_like(two_sum)
         mlp_sum[...] = jnp.zeros_like(mlp_sum)
+        size = lax.axis_size("dp")
+        block = rows_ref.shape[1] // size
+        for k, source in enumerate((rows_ref, branch_ref)):
+            for r in range(size):
+                start = pl.multiple_of((place[2] ^ r) * block, block)
+                target = sent_ref if r % 2 else kept_ref
+                at = r // 2 * block
+                target[k, :, at : at + block] = source[:, pl.ds(start, block)]
 
     rows = rows_ref[...]
     gate_pre = rows_by(rows, gate_ref[...], (1, 0))
@@ -523,9 +513,9 @@
     hidden = (curved * up_pre).astype(LOW)
     gate_back = (grad_hidden * up_pre * slope).astype(LOW)
     up_back = (grad_hidden * curved).astype(LOW)
-    hidden_ref[...] = hidden
-    gate_back_ref[...] = gate_back
-    up_back_ref[...] = up_back
+    made_ref[0] = hidden
+    made_ref[1] = gate_back
+    made_ref[2] = up_back
     two_sum[...] += rows_by(gate_back, gate_ref[...], (1, 1)) + rows_by(up_back, up_ref[...], (1, 1))
     mlp_sum[...] += rows_by(hidden, down_ref[...], (1, 0))
 
@@ -535,38 +525,140 @@
         mlp_ref[...] = mlp_sum[...].astype(mlp_ref.dtype)
 
 
-def feed_forward(rows, branch, gate_weight, up_weight, down_weight, kind):
+def feed_forward(rows, branch, gate_weight, up_weight, down_weight, place, kind):
     count, features = rows.shape
     units = gate_weight.shape[1]
     tile = min(512, units)
-    columns = pl.BlockSpec((features, tile), lambda step: (0, step))
-    made = pl.BlockSpec((count, tile), lambda step: (0, step))
+    columns = pl.BlockSpec((features, tile), lambda step, place: (0, step))
+    half = (2, count, features // 2)
     return pl.pallas_call(
         feed_kernel,
         name="feed_forward",
         out_shape=(
-            *[jax.ShapeDtypeStruct((count, units), LOW)] * 3,
+            jax.ShapeDtypeStruct((3, count, units), LOW),
+            *[jax.ShapeDtypeStruct(half, LOW)] * 2,
             *[jax.ShapeDtypeStruct((count, features), kind)] * 2,
         ),
-        grid=(units // tile,),
-        in_specs=[
-            whole((count, features)),
-            whole((count, features)),
-            columns,
-            columns,
-            pl.BlockSpec((tile, features), lambda step: (step, 0)),
+        grid_spec=pltpu.PrefetchScalarGridSpec(
+            num_scalar_prefetch=1,
+            grid=(units // tile,),
+            in_specs=[
+                whole((count, features)),
+                whole((count, features)),
+                columns,
+                columns,
+                pl.BlockSpec((tile, features), lambda step, place: (step, 0)),
+            ],
+            out_specs=[
+                pl.BlockSpec((3, count, tile), lambda step, place: (0, 0, step)),
+                *[whole(half)] * 2,
+                *[whole((count, features))] * 2,
+            ],
+            scratch_shapes=[pltpu.VMEM((count, features), F32)] * 2,
+        ),
+        compiler_params=pltpu.CompilerParams(
+            dimension_semantics=("arbitrary",), vmem_limit_bytes=44 << 20
+        ),
+        cost_estimate=BRIEF,
+    )(place, rows, branch, gate_weight, up_weight, down_weight)
+
+
+def project_back_kernel(*refs):
+    count = (len(refs) - 2) // 3
+    rows_refs, one_refs, weight_ref = refs[:count], refs[count : 2 * count], refs[2 * count]
+    out_refs, gain_ref = refs[2 * count + 1 : -1], refs[-1]
+    weight = weight_ref[...]
+    gain = jnp.zeros(gain_ref.shape, F32)
+    for rows_ref, one_ref, out_ref in zip(rows_refs, one_refs, out_refs):
+        value = rows_by(rows_ref[...], weight, (1, 1))
+        out_ref[...] = value.astype(out_ref.dtype)
+        gain = gain + jnp.sum(value * one_ref[...].astype(F32), axis=0, keepdims=True)
+    gain_ref[...] = gain
+
+
+def project_rows_back(rows, weight, count, one, wanted, kinds):
+    features, wide = weight.shape
+    tile = min(512, features)
+    made = pl.BlockSpec((count, tile), lambda step: (0, step))
+    *parts, gain = pl.pallas_call(
+        project_back_kernel,
+        name="project_back",
+        out_shape=[jax.ShapeDtypeStruct((count, features), kind) for kind in kinds]
+        + [jax.ShapeDtypeStruct((1, features), F32)],
+        grid=(features // tile,),
+        in_specs=[pl.BlockSpec((count, wide), lambda step, p=p: (p, 0)) for p in wanted]
+        + [made] * len(wanted)
+        + [pl.BlockSpec((tile, wide), lambda step: (step, 0))],
+        out_specs=[made] * len(wanted) + [pl.BlockSpec((1, tile), lambda step: (0, step))],
+        compiler_params=pltpu.CompilerParams(
+            dimension_semantics=("arbitrary",), vmem_limit_bytes=24 << 20
+        ),
+        cost_estimate=BRIEF,
+    )(*[rows] * len(wanted), *[one[p] for p in wanted], weight)
+    return dict(zip(wanted, parts)), gain[0]
+
+
+def weight_kernel(*refs):
+    *in_refs, low_keep, low_send, high_keep, high_send = refs
+    half = len(in_refs) // 2
+    step = pl.program_id(0)
+    steps = pl.num_programs(0)
+    value = rows_by(in_refs[0][...], in_refs[half][...], (0, 0))
+    for left, right in zip(in_refs[1:half], in_refs[half + 1 :]):
+        value = value + rows_by(left[...], right[...], (0, 0))
+    value = value.astype(LOW)
+    middle = value.shape[0] // 2
+    odd = lax.rem(step, 2) == 1
+    upper = step >= steps // 2
+
+    @pl.when(jnp.logical_not(odd))
+    def _():
+        low_keep[...] = value[:middle]
+
+    @pl.when(odd)
+    def _():
+        low_send[...] = value[:middle]
+
+    @pl.when(jnp.logical_not(upper))
+    def _():
+        high_keep[...] = value[middle:]
+
+    @pl.when(upper)
+    def _():
+        high_send[...] = value[middle:]
+
+
+def weight_blocks(lefts, rights, blocks):
+    across = lefts[0][0].shape[2] // blocks
+    along = rights[0][0].shape[2]
+
+    def left_spec(pair):
+        return pl.BlockSpec((None, pair[0].shape[1], across), lambda step: (pair[1], 0, step))
+
+    def right_spec(pair):
+        return pl.BlockSpec((None, pair[0].shape[1], along), lambda step: (pair[1], 0, 0))
+
+    def out_spec_of(place):
+        return pl.BlockSpec((None, across // 2, along), lambda step: (place(step), 0, 0))
+
+    half = blocks // 2
+    return pl.pallas_call(
+        weight_kernel,
+        name="weight_blocks",
+        out_shape=[jax.ShapeDtypeStruct((half, across // 2, along), LOW)] * 4,
+        grid=(blocks,),
+        in_specs=[left_spec(pair) for pair in lefts] + [right_spec(pair) for pair in rights],
+        out_specs=[
+            out_spec_of(lambda step: lax.div(step, 2)),
+            out_spec_of(lambda step: lax.div(step, 2)),
+            out_spec_of(lambda step: jnp.minimum(step, half - 1)),
+            out_spec_of(lambda step: jnp.maximum(step - half, 0)),
         ],
-        out_specs=[made] * 3 + [whole((count, features))] * 2,
-        scratch_shapes=[pltpu.VMEM((count, features), F32)] * 2,
         compiler_params=pltpu.CompilerParams(
             dimension_semantics=("arbitrary",), vmem_limit_bytes=40 << 20
         ),
-        cost_estimate=pl.CostEstimate(
-            flops=12 * count * features * units,
-            bytes_accessed=6 * features * units,
-            transcendentals=count * units,
-        ),
-    )(rows, branch, gate_weight, up_weight, down_weight)
+        cost_estimate=BRIEF,
+    )(*[pair[0] for pair in lefts], *[pair[0] for pair in rights])
 
 
 def inverse_rms(values):
@@ -606,7 +698,7 @@
     per_chunk = row_count // SEG
     rank = lax.axis_index("mp")
     pieces = range(ranks)
-    place = jnp.stack([rank, lengths[0]]).astype(jnp.int32)
+    place = jnp.stack([rank, lengths[0], lax.axis_index("dp")]).astype(jnp.int32)
     live = (rank * row_count + jnp.arange(row_count) < lengths[0]).astype(F32)[:, None]
     share = jax.nn.sigmoid(memory_gate)
 
@@ -624,6 +716,7 @@
     out_slice = lax.dynamic_slice_in_dim(
         out_weight, lax.axis_index("dp") * slice_rows, slice_rows, axis=0
     )
+    out_slice, normed_one = hold((out_slice, normed_one))
     qkv_weight = jnp.concatenate([query_weight, key_weight, value_weight], axis=1)
 
     def project(rows):
@@ -648,72 +741,89 @@
     qkv.update({p: project(one[p]) for p in far})
     qkv = stacked(qkv)
     mixed, memories, normers = attend(qkv, place, share, per_chunk)
-    one_blocks = relative_blocks(stacked(one), "dp")
-    mixed, one_blocks = hold((mixed, one_blocks))
+    mixed = hold(mixed)
 
     mixed = swap_pieces(
         {p: mixed[p * row_count : (p + 1) * row_count] for p in pieces}, "mp"
     )
-    mixed, branch, out_full = hold((mixed, branch, out_full))
+    mixed, branch = hold((mixed, branch))
 
     out_full = out_full.reshape(blocks, ranks, slice_rows, features)
     state, normed_two = out_project(mixed, out_full, tokens, mlp_gain, place)
     mixed = stacked(mixed, axis=1)
 
-    hidden, gate_back, up_back, two_parts, mlp_parts = {}, {}, {}, {}, {}
+    made, kept, sent, two_parts, mlp_parts = {}, {}, {}, {}, {}
 
     def feed(p):
         kind = LOW if p == 1 or p in far else F32
-        hidden[p], gate_back[p], up_back[p], two_parts[p], mlp_parts[p] = feed_forward(
-            two[p], branch[p], gate_weight, up_weight, down_weight, kind
+        made[p], kept[p], sent[p], two_parts[p], mlp_parts[p] = feed_forward(
+            two[p], branch[p], gate_weight, up_weight, down_weight, place, kind
         )
+
+    their_made, their_kept = {}, {}
+
+    def share_rows(p):
+        their_made[p] = hop(made[p], "dp", 1)
+        their_kept[p] = hop(sent[p], "dp", 1)
 
     two = gather_near(normed_two, "mp")
     branch.update(gather_far(branch, "mp"))
     feed(0)
+    one_kept, one_sent = relative_blocks(stacked(one), "dp")
+    their_mixed = hop(mixed, "dp", 1)
+    two, made, kept, sent, two_parts, mlp_parts, branch, one_kept, one_sent, their_mixed = hold(
+        (two, made, kept, sent, two_parts, mlp_parts, branch, one_kept, one_sent, their_mixed)
+    )
+
+    two.update(gather_far(two, "mp"))
+    share_rows(0)
+    their_one = hop(one_sent, "dp", 1)
     feed(1)
-    two, hidden, gate_back, up_back, two_parts, mlp_parts, branch = hold(
-        (two, hidden, gate_back, up_back, two_parts, mlp_parts, branch)
-    )
-
-    two.update(gather_far(two, "mp"))
+    two, made, kept, sent, two_parts, mlp_parts, their_made, their_kept, their_one = hold(
+        (two, made, kept, sent, two_parts, mlp_parts, their_made, their_kept, their_one)
+    )
+
+    mlp_near = reduce_near(mlp_parts, None, "mp", (1,))
+    share_rows(1)
+    for p in far:
+        feed(p)
+    two, made, kept, sent, two_parts, mlp_parts, their_made, their_kept, mlp_near = hold(
+        (two, made, kept, sent, two_parts, mlp_parts, their_made, their_kept, mlp_near)
+    )
+
+    two_far = reduce_far(two_parts, "mp")
+    for p in far:
+        share_rows(p)
     for p in near[1:]:
         feed(p)
-    branch_blocks = relative_blocks(stacked(branch), "dp")
-    two, hidden, gate_back, up_back, two_parts, mlp_parts, branch, branch_blocks = hold(
-        (two, hidden, gate_back, up_back, two_parts, mlp_parts, branch, branch_blocks)
-    )
-
-    mlp_near = reduce_near(mlp_parts, None, "mp", (1,))
-    for p in far:
-        feed(p)
-    two, hidden, gate_back, up_back, two_parts, mlp_parts, mlp_near = hold(
-        (two, hidden, gate_back, up_back, two_parts, mlp_parts, mlp_near)
-    )
-
-    two_far = reduce_far(two_parts, "mp")
-    all_two = stacked(two)
-    gate_product = product(all_two, stacked(gate_back))
-    all_hidden, all_up_back = stacked(hidden), stacked(up_back)
-    two_parts, two_far, all_hidden, all_up_back, _ = hold(
-        (two_parts, two_far, all_hidden, all_up_back, gate_product)
-    )
+    made, kept, sent, two_parts, mlp_parts, their_made, their_kept, two_far = hold(
+        (made, kept, sent, two_parts, mlp_parts, their_made, their_kept, two_far)
+    )
+
+    steps = device_steps("dp")
+
+    def weights_of(left, right):
+        return DeviceSum(
+            weight_blocks(
+                [(kept[p], left) for p in pieces] + [(their_kept[p], left) for p in pieces],
+                [(made[p], right) for p in pieces] + [(their_made[p], right) for p in pieces],
+                blocks // 2,
+            ),
+            "dp",
+        )
 
     two_near = reduce_near(two_parts, two_far, "mp")
-    up_product = product(all_two, all_up_back)
-    down_products = [product(all_hidden, half) for half in branch_blocks]
-    two_near, mlp_parts, down_products, _ = hold(
-        (two_near, mlp_parts, down_products, up_product)
-    )
-
-    def spread(value, dim):
-        return lax.psum_scatter(value, "dp", scatter_dimension=dim, tiled=True).astype(F32)
-
-    grad_gate = spread(gate_product, 0)
-    grad_up = spread(up_product, 0)
+    for p in near[1:]:
+        share_rows(p)
+    gate_sum = weights_of(0, 1)
+    fly(gate_sum)
+    up_sum = weights_of(0, 2)
+    two_near, mlp_parts, gate_sum.state, up_sum.state, made, kept, their_made, their_kept = hold(
+        (two_near, mlp_parts, gate_sum.state, up_sum.state, made, kept, their_made, their_kept)
+    )
 
     mlp_far = reduce_far(mlp_parts, "mp")
-    down_sum = BlockSum(*down_products, "dp", 1)
+    fly(up_sum)
     grad_normed_two = total(two_parts[0], two_near)
     grad_through, grad_mlp_gain = normed_back(
         state, inverse_rms(state), mlp_gain, grad_normed_two
@@ -721,71 +831,109 @@
     grad_state = upstream + grad_through
     grad_attn = (grad_state * live).astype(LOW)
     grad_mixed = out_back(grad_attn, out_full)
+    attn_kept, attn_sent = relative_blocks(grad_attn, "dp")
+    their_attn = hop(attn_sent, "dp", 1)
+    down_sum = weights_of(1, 0)
+    (
+        mlp_far, grad_mixed, attn_kept, their_attn, grad_state, grad_mlp_gain, mlp_parts,
+        gate_sum.state, up_sum.state, down_sum.state,
+    ) = hold(
+        (
+            mlp_far, grad_mixed, attn_kept, their_attn, grad_state, grad_mlp_gain, mlp_parts,
+            gate_sum.state, up_sum.state, down_sum.state,
+        )
+    )
     grad_mixed = stacked(swap_pieces({p: grad_mixed[p] for p in pieces}, "mp"))
-    out_products = [product(mixed, half) for half in relative_blocks(grad_attn, "dp")]
-    out_sum = BlockSum(*out_products, "dp", 1)
-    down_sum.step(0)
-    mlp_far, grad_mixed, out_sum.state, down_sum.state, mlp_parts, grad_state, grad_mlp_gain = hold(
-        (mlp_far, grad_mixed, out_sum.state, down_sum.state, mlp_parts, grad_state, grad_mlp_gain)
-    )
-
-    out_sum.step(0)
-    for k in range(1, down_sum.steps):
-        down_sum.step(k)
+    fly(down_sum)
+    out_sum = DeviceSum(
+        weight_blocks(
+            [(attn_kept[None], 0), (their_attn[None], 0)],
+            [(mixed[None], 0), (their_mixed[None], 0)],
+            blocks // 2,
+        ),
+        "dp",
+    )
+    gate_sum.land()
+    up_sum.land()
+    grad_mixed, mlp_parts, gate_sum.state, up_sum.state, down_sum.state, out_sum.state = hold(
+        (grad_mixed, mlp_parts, gate_sum.state, up_sum.state, down_sum.state, out_sum.state)
+    )
+
     mlp_near.update(reduce_near(mlp_parts, mlp_far, "mp", near[1:]))
+    fly(out_sum, *([gate_sum, up_sum] if steps > 1 else []))
+    down_sum.land()
     grad_qkv, grad_mix = attend_back(
         qkv, grad_mixed, memories, normers, place, share, per_chunk
     )
-    grad_qkv, grad_mix, down_sum.state, out_sum.state = hold(
-        (grad_qkv, grad_mix, down_sum.state, out_sum.state)
-    )
-    one_parts = {}
-
-    def project_back(p):
-        value = rows_by(grad_qkv[p * row_count : (p + 1) * row_count], qkv_weight, (1, 1))
-        one_parts[p] = value.astype(LOW) if p == 1 or p in far else value
-
-    for p in far:
-        project_back(p)
-    one_parts, grad_qkv = hold((one_parts, grad_qkv))
+    grad_qkv, grad_mix, mlp_near, out_sum.state, down_sum.state, gate_sum.state, up_sum.state = hold(
+        (grad_qkv, grad_mix, mlp_near, out_sum.state, down_sum.state, gate_sum.state, up_sum.state)
+    )
+
+    def project_back(wanted):
+        kinds = [LOW if p == 1 or p in far else F32 for p in wanted]
+        return project_rows_back(grad_qkv, qkv_weight, row_count, one, wanted, kinds)
+
+    their_qkv = hop(grad_qkv, "dp", 1)
+    one_parts, gain_far = project_back(far)
+    one_parts, grad_qkv, out_sum.state, down_sum.state, mlp_near = hold(
+        (one_parts, grad_qkv, out_sum.state, down_sum.state, mlp_near)
+    )
     one_far = reduce_far(one_parts, "mp")
-    qkv_products = [product(half, grad_qkv) for half in one_blocks]
-    qkv_sum = BlockSum(*qkv_products, "dp", 0)
-    for k in range(1, out_sum.steps):
-        out_sum.step(k)
-    for p in [0] + near:
-        project_back(p)
-    grad_down = down_sum.result()
-    one_parts, one_far, mlp_near, out_sum.state, qkv_sum.state, grad_down = hold(
-        (one_parts, one_far, mlp_near, out_sum.state, qkv_sum.state, grad_down)
+    qkv_sum = DeviceSum(
+        weight_blocks(
+            [(one_kept[None], 0), (their_one[None], 0)],
+            [(grad_qkv[None], 0), (their_qkv[None], 0)],
+            blocks // 2,
+        ),
+        "dp",
+    )
+    grad_qkv, qkv_sum.state, out_sum.state, down_sum.state = hold(
+        (grad_qkv, qkv_sum.state, out_sum.state, down_sum.state)
+    )
+    out_sum.land()
+    if steps > 1:
+        fly(down_sum, out_sum)
+    more_parts, gain_near = project_back([0] + near)
+    one_parts.update(more_parts)
+    one_parts, one_far, qkv_sum.state, mlp_near = hold(
+        (one_parts, one_far, qkv_sum.state, mlp_near)
     )
 
     one_near = reduce_near(one_parts, one_far, "mp")
     block_out = (state + live * total(mlp_parts[0], mlp_near)).astype(LOW)
-    grad_attn_gain = (
-        sum(jnp.sum(one[p].astype(F32) * one_parts[p].astype(F32), axis=0) for p in pieces)
-        / attn_gain
-    )
+    grad_attn_gain = (gain_far + gain_near) / attn_gain
     grad_share = jnp.sum(grad_mix, axis=1) * share * (1.0 - share)
     share_full = lax.dynamic_update_slice(
         jnp.zeros((heads * ranks,), F32), grad_share, (rank * heads,)
     )
-    small = sum_everywhere(
-        jnp.concatenate([grad_attn_gain, grad_mlp_gain, share_full]), ("mp", "dp")
-    )
-    for k in range(qkv_sum.steps):
-        qkv_sum.step(k)
+    small = jnp.concatenate([grad_attn_gain, grad_mlp_gain, share_full])
+    fly(qkv_sum)
+    for k in range(1, steps):
+        for some in ([gate_sum, up_sum], [down_sum, out_sum]):
+            for one_sum in some:
+                one_sum.land()
+            if k + 1 < steps:
+                fly(*some)
+        qkv_sum.land()
+        fly(qkv_sum)
+    qkv_sum.land()
+    grad_gate, grad_up = gate_sum.result(), up_sum.result()
+    grad_down = down_sum.result().T
     grad_proj = qkv_sum.result()
     grad_out_part = out_sum.result()
-    one_near, small, grad_proj, grad_out_part = hold((one_near, small, grad_proj, grad_out_part))
-
+    out_parts = {p: grad_out_part[:, p * width : (p + 1) * width] for p in pieces}
+    out_parts = {p: out_parts[p].astype(LOW) if p else out_parts[p] for p in pieces}
+    one_near, small, out_parts, block_out, grad_gate, grad_up, grad_down, grad_proj = hold(
+        (one_near, small, out_parts, block_out, grad_gate, grad_up, grad_down, grad_proj)
+    )
+
+    small = sum_everywhere(small, ("mp", "dp"))
     grad_query, grad_key, grad_value = (
         grad_proj[:, j * width : (j + 1) * width] for j in range(3)
     )
-    out_parts = {p: grad_out_part[p * width : (p + 1) * width] for p in pieces}
     grad_out = total(
-        out_parts[0], {p: hop(out_parts[p].astype(LOW), "mp", p) for p in range(1, ranks)}
-    )
+        out_parts[0], {p: hop(out_parts[p], "mp", p) for p in range(1, ranks)}
+    ).T
     grad_normed_one = total(one_parts[0], one_near)
     grad_inputs = normed_back(inputs, inverse_one, attn_gain, grad_normed_one)[0]
     grad_tokens = grad_state + grad_inputs

time: 677 us -> 628 us (0.928)
  Pallas kernels: 128 us -> 206 us
  matrix products: 79.1 us -> 17.1 us
  other arithmetic: 86.3 us -> 49.4 us
  waiting for transfers between devices: 240 us -> 213 us
  local copies, waits for them, and re-layouts: 44.5 us -> 58.6 us
  starting transfers between devices: 72.6 us -> 61.3 us
    pallas_call x4 -> x11, Pallas kernels: 76.1 us -> 154 us  [the longest x4 83.8 us: feed_forward(): pl.pallas_call(feed_kernel, name='feed_forward', out_shape=(jax.ShapeDtyp...]
    dot_general x16 -> x4, matrix products: 79.1 us -> 17.1 us  [rows_by(): lax.dot_general(left, right, ((contract[:1], contract[1:]), ((), ())), pr...]
    ppermute x50 -> x61, waiting for transfers between devices: 240 us -> 213 us  [hop(): return lax.ppermute(value, axis, [(j, j ^ mask) for j in range(size)])]
    add x16 -> x11, other arithmetic: 27.1 us -> 12.3 us  [the longest x10 12.3 us: land(): value = self.keep[side].astype(F32) + self.flight[side].astype(F32)]
    ppermute x50 -> x61, starting transfers between devices: 72.5 us -> 61.2 us  [hop(): return lax.ppermute(value, axis, [(j, j ^ mask) for j in range(size)])]
    unnamed x236 -> x184, local copies, waits for them, and re-layouts: 36.4 us -> 43.9 us
    convert_element_type x3 -> x0, other arithmetic: 7.17 us -> none  [the longest x2 5.61 us: spread(): lax.psum_scatter(value, 'dp', scatter_dimension=dim, tiled=True).astype(F32)]
  transfers between devices with their start and end apart: 53 -> 62, of which waited for: 24 -> 30; matrix products, arithmetic and copies ran while one was open for 25% -> 14% of each run, Pallas kernels for 18% -> 33%
where the time goes in v2:
time: 628 us; the launch traced here: 621 us
  waiting for transfers between devices  213 us (34%)
  Pallas kernels  206 us (33%)
  starting transfers between devices  61.3 us (10%)
  local copies, waits for them, and re-layouts  58.6 us (9%)
  other arithmetic  49.4 us (8%)
  matrix products  17.1 us (3%)
  between operations  16.5 us (3%)
    ppermute x61, waiting for transfers between devices, hop(): return lax.ppermute(value, axis, [(j, j ^ mask) for j in range(size)])  213 us
    pallas_call x4, Pallas kernels, feed_forward(): pl.pallas_call(feed_kernel, name='feed_forward', out_shape=(jax.ShapeDtyp...  83.8 us
    ppermute x61, starting transfers between devices, hop(): return lax.ppermute(value, axis, [(j, j ^ mask) for j in range(size)])  61.2 us
    pallas_call x5, Pallas kernels, weight_blocks(): pl.pallas_call(weight_kernel, name='weight_blocks', out_shape=[jax.ShapeD...  58.8 us
    unnamed x184, local copies, waits for them, and re-layouts  43.9 us
    pallas_call x1, Pallas kernels, attend_back(): pl.pallas_call(attend_back_kernel, name='attend_back', out_shape=(jax.Sha...  28.1 us
    dot_general x4, matrix products, rows_by(): lax.dot_general(left, right, ((contract[:1], contract[1:]), ((), ())), pr...  17.1 us
    pallas_call x1, Pallas kernels, attend(): pl.pallas_call(attend_kernel, name='attend', out_shape=(jax.ShapeDtypeStr...  14.6 us
  transfers between devices with their start and end apart: 62, of which 30 were waited for; matrix products, arithmetic and copies ran while one was open for 14% of the time, Pallas kernels for 33%

profile of v2, /device:TPU:8, one launch (start us, length us, event | category | flops | bytes accessed | tf_op | source)
XLA Modules:
  0.0 621.3 jit_solution(3201136663825446716)
XLA Ops:
  23.9 5.6 convolution_convert_fusion.3
  30.7 38.4 %collective-permute-done.1.refs_5_ = bf16[256,2048]{1,0:T(8,128)(2,1)S(1)} collective-permute-done((bf16[256,2048]{1,0:T(8,128)(2,1)S(1)}, bf16[256,2048]{1,0:T(8,128)(2,1)S(1)}, u32[]{:S(2)}, u32[]{:S(2)}) %collective-permute-start.1) | collective-permute-done | bytes 1048608 | tf_op jit(solution)/shard_map/ppermute | solution.py:21
  79.7 20.5 %collective-permute-done.4.refs_1_ = bf16[256,2048]{1,0:T(8,128)(2,1)} collective-permute-done((bf16[256,2048]{1,0:T(8,128)(2,1)S(1)}, bf16[256,2048]{1,0:T(8,128)(2,1)}, u32[]{:S(2)}, u32[]{:S(2)}) %collective-permute-start.4) | collective-permute-done | bytes 1048608 | tf_op jit(solution)/shard_map/ppermute | solution.py:21
  115.3 14.6 %attend.1 = (bf16[1024,512]{1,0:T(8,128)(2,1)S(1)}, f32[8,4,128,128]{3,2,1,0:T(8,128)S(1)}, f32[8,4,128]{2,1,0:T(4,128)S(1)}) custom-call(s32[3]{0:T(128)S(1)} %pad_add_fusion.place, f32[4]{0:T(128)S(1)} %add_divide_fusion.share, bf16[1024,1536]{1,0:T(8,128)(2,1)S(1)} %copy-done.11), custom_call_target="tpu_custom_call" | custom-call | flops 1 | bytes 1 | tf_op jit(solution)/shard_map/attend/pallas_call | solution.py:315
  135.4 32.7 %collective-permute-done.8.refs_3_ = bf16[256,512]{1,0:T(8,128)(2,1)S(1)} collective-permute-done((bf16[256,512]{1,0:T(8,128)(2,1)S(1)}, bf16[256,512]{1,0:T(8,128)(2,1)S(1)}, u32[]{:S(2)}, u32[]{:S(2)}) %collective-permute-start.8) | collective-permute-done | bytes 262176 | tf_op jit(solution)/shard_map/ppermute | solution.py:21
  197.2 20.2 %feed_forward.4 = (bf16[3,256,2048]{2,1,0:T(8,128)(2,1)}, bf16[2,256,1024]{2,1,0:T(8,128)(2,1)S(1)}, bf16[2,256,1024]{2,1,0:T(8,128)(2,1)}, f32[256,2048]{1,0:T(8,128)S(1)}, f32[256,2048]{1,0:T(8,128)S(1)}) custom-call(s32[3]{0:T(128)S(1)} %pad_add_fusion.place, bf16[256,2048]{1,0:T(8,128)(2,1)S(1)} %get-tuple-element.320.rows_ref, ...), custom_call_target="tpu_custom_call" | custom-call | flops 1 | bytes 1 | tf_op jit(solution)/shard_map/feed_forward/pallas_call | solution.py:534
  218.7 17.8 %collective-permute-done.12.rows_ref = bf16[256,2048]{1,0:T(8,128)(2,1)S(1)} collective-permute-done((bf16[256,2048]{1,0:T(8,128)(2,1)S(1)}, bf16[256,2048]{1,0:T(8,128)(2,1)S(1)}, u32[]{:S(2)}, u32[]{:S(2)}) %collective-permute-start.12) | collective-permute-done | bytes 1048608 | tf_op jit(solution)/shard_map/ppermute | solution.py:21
  236.5 10.2 %collective-permute-done.11.rows_ref = bf16[256,2048]{1,0:T(8,128)(2,1)S(1)} collective-permute-done((bf16[256,2048]{1,0:T(8,128)(2,1)S(1)}, bf16[256,2048]{1,0:T(8,128)(2,1)S(1)}, u32[]{:S(2)}, u32[]{:S(2)}) %collective-permute-start.11) | collective-permute-done | bytes 1048608 | tf_op jit(solution)/shard_map/ppermute | solution.py:21
  248.5 21.5 %feed_forward.5 = (bf16[3,256,2048]{2,1,0:T(8,128)(2,1)S(1)}, bf16[2,256,1024]{2,1,0:T(8,128)(2,1)S(1)}, bf16[2,256,1024]{2,1,0:T(8,128)(2,1)}, bf16[256,2048]{1,0:T(8,128)(2,1)S(1)}, bf16[256,2048]{1,0:T(8,128)(2,1)}) custom-call(s32[3]{0:T(128)S(1)} %pad_add_fusion.place, bf16[256,2048]{1,0:T(8,128)(2,1)S(1)} %collective-permute-done.11.rows_ref, ...), custom_call_target="tpu_custom_call" | custom-call | flops 1 | bytes 1 | tf_op jit(solution)/shard_map/feed_forward/pallas_call | solution.py:534
  275.5 21.4 %feed_forward.6 = (bf16[3,256,2048]{2,1,0:T(8,128)(2,1)S(1)}, bf16[2,256,1024]{2,1,0:T(8,128)(2,1)S(1)}, bf16[2,256,1024]{2,1,0:T(8,128)(2,1)}, bf16[256,2048]{1,0:T(8,128)(2,1)}, bf16[256,2048]{1,0:T(8,128)(2,1)}) custom-call(s32[3]{0:T(128)S(1)} %pad_add_fusion.place, bf16[256,2048]{1,0:T(8,128)(2,1)S(1)} %collective-permute-done.15.rows_ref, ...), custom_call_target="tpu_custom_call" | custom-call | flops 1 | bytes 1 | tf_op jit(solution)/shard_map/feed_forward/pallas_call | solution.py:534
  303.0 20.7 %feed_forward.7 = (bf16[3,256,2048]{2,1,0:T(8,128)(2,1)}, bf16[2,256,1024]{2,1,0:T(8,128)(2,1)S(1)}, bf16[2,256,1024]{2,1,0:T(8,128)(2,1)S(1)}, f32[256,2048]{1,0:T(8,128)S(1)}, f32[256,2048]{1,0:T(8,128)S(1)}) custom-call(s32[3]{0:T(128)S(1)} %pad_add_fusion.place, bf16[256,2048]{1,0:T(8,128)(2,1)S(1)} %copy-done.34, ...), custom_call_target="tpu_custom_call" | custom-call | flops 1 | bytes 1 | tf_op jit(solution)/shard_map/feed_forward/pallas_call | solution.py:534
  334.1 13.9 %weight_blocks.5 = (bf16[2,128,2048]{2,1,0:T(8,128)(2,1)S(1)}, bf16[2,128,2048]{2,1,0:T(8,128)(2,1)S(1)}, bf16[2,128,2048]{2,1,0:T(8,128)(2,1)S(1)}, bf16[2,128,2048]{2,1,0:T(8,128)(2,1)S(1)}) custom-call(bf16[2,256,1024]{2,1,0:T(8,128)(2,1)S(1)} %get-tuple-element.432.refs_0_, bf16[2,256,1024]{2,1,0:T(8,128)(2,1)S(1)} %copy-done.14, ...), custom_call_target="tpu_custom_call" | custom-call | flops 1 | bytes 1 | tf_op jit(solution)/shard_map/weight_blocks/pallas_call | solution.py:645
  351.3 14.9 %weight_blocks.6 = (bf16[2,128,2048]{2,1,0:T(8,128)(2,1)S(1)}, bf16[2,128,2048]{2,1,0:T(8,128)(2,1)S(1)}, bf16[2,128,2048]{2,1,0:T(8,128)(2,1)S(1)}, bf16[2,128,2048]{2,1,0:T(8,128)(2,1)}) custom-call(bf16[2,256,1024]{2,1,0:T(8,128)(2,1)S(1)} %get-tuple-element.432.refs_0_, bf16[2,256,1024]{2,1,0:T(8,128)(2,1)S(1)} %copy-done.14, ...), custom_call_target="tpu_custom_call" | custom-call | flops 1 | bytes 1 | tf_op jit(solution)/shard_map/weight_blocks/pallas_call | solution.py:645
  366.2 11.9 %collective-permute-done.26 = bf16[256,2048]{1,0:T(8,128)(2,1)S(1)} collective-permute-done((bf16[256,2048]{1,0:T(8,128)(2,1)}, bf16[256,2048]{1,0:T(8,128)(2,1)S(1)}, u32[]{:S(2)}, u32[]{:S(2)}) %collective-permute-start.26) | collective-permute-done | bytes 1048608 | tf_op jit(solution)/shard_map/ppermute | solution.py:21
  392.4 13.9 %weight_blocks.7 = (bf16[2,128,2048]{2,1,0:T(8,128)(2,1)S(1)}, bf16[2,128,2048]{2,1,0:T(8,128)(2,1)S(1)}, bf16[2,128,2048]{2,1,0:T(8,128)(2,1)S(1)}, bf16[2,128,2048]{2,1,0:T(8,128)(2,1)S(1)}) custom-call(bf16[2,256,1024]{2,1,0:T(8,128)(2,1)S(1)} %get-tuple-element.432.refs_0_, bf16[2,256,1024]{2,1,0:T(8,128)(2,1)S(1)} %copy-done.14, ...), custom_call_target="tpu_custom_call" | custom-call | flops 1 | bytes 1 | tf_op jit(solution)/shard_map/weight_blocks/pallas_call | solution.py:645
  421.3 5.8 weight_blocks.8
  444.2 28.1 %attend_back.1 = (bf16[1024,1536]{1,0:T(8,128)(2,1)S(1)}, f32[4,128]{1,0:T(4,128)S(1)}) custom-call(s32[3]{0:T(128)S(1)} %pad_add_fusion.place, f32[4]{0:T(128)S(1)} %add_divide_fusion.share, bf16[1024,1536]{1,0:T(8,128)(2,1)S(1)} %copy-done.12, bf16[1024,512]{1,0:T(8,128)(2,1)S(1)} %pad_maximum_fusion.10.grad_ref, f32[8,4,128,128]{3,2,1,0:T(8,128)S(1)} %copy-done.47, ...), custom_call_target="tpu_custom_call" | custom-call | flops 16106127360 | bytes 9437184 | tf_op jit(solution)/shard_map/attend_back/pallas_call | solution.py:352
  475.7 10.0 %collective-permute-done.41 = bf16[512,2048]{1,0:T(8,128)(2,1)S(1)} collective-permute-done((bf16[512,2048]{1,0:T(8,128)(2,1)S(1)}, bf16[512,2048]{1,0:T(8,128)(2,1)S(1)}, u32[]{:S(2)}, u32[]{:S(2)}) %collective-permute-start.41) | collective-permute-done | bytes 2097184 | tf_op jit(solution)/shard_map/ppermute | solution.py:21
  504.6 10.3 %weight_blocks.9 = (bf16[2,128,1536]{2,1,0:T(8,128)(2,1)S(1)}, bf16[2,128,1536]{2,1,0:T(8,128)(2,1)S(1)}, bf16[2,128,1536]{2,1,0:T(8,128)(2,1)S(1)}, bf16[2,128,1536]{2,1,0:T(8,128)(2,1)S(1)}) custom-call(bf16[1,1024,1024]{2,1,0:T(8,128)(2,1)S(1)} %bitcast.136, bf16[1,1024,1024]{2,1,0:T(8,128)(2,1)S(1)} %bitcast.137, bf16[1,1024,1536]{2,1,0:T(8,128)(2,1)S(1)} %bitcast.129, ...), custom_call_target="tpu_custom_call" | custom-call | flops 1 | bytes 1 | tf_op jit(solution)/shard_map/weight_blocks/pallas_call | solution.py:645
  515.0 7.2 %project_back.3 = (f32[256,2048]{1,0:T(8,128)S(1)}, bf16[256,2048]{1,0:T(8,128)(2,1)S(1)}, f32[256,2048]{1,0:T(8,128)S(1)}, f32[1,2048]{1,0:T(1,128)S(1)}) custom-call(bf16[1024,1536]{1,0:T(8,128)(2,1)S(1)} %get-tuple-element.525.refs_0_.refs_1_.refs_2_, bf16[1024,1536]{1,0:T(8,128)(2,1)S(1)} %get-tuple-element.525.refs_0_.refs_1_.refs_2_, ...), custom_call_target="tpu_custom_call" | custom-call | flops 1 | bytes 1 | tf_op jit(solution)/shard_map/project_back/pallas_call | solution.py:583
  535.7 6.9 %collective-permute-done.49 = bf16[256,1536]{1,0:T(8,128)(2,1)S(1)} collective-permute-done((bf16[256,1536]{1,0:T(8,128)(2,1)S(1)}, bf16[256,1536]{1,0:T(8,128)(2,1)S(1)}, u32[]{:S(2)}, u32[]{:S(2)}) %collective-permute-start.49) | collective-permute-done | bytes 786464 | tf_op jit(solution)/shard_map/ppermute | solution.py:21
  546.0 21.8 %collective-permute-done.47 = bf16[256,2048]{1,0:T(8,128)(2,1)S(1)} collective-permute-done((bf16[256,2048]{1,0:T(8,128)(2,1)S(1)}, bf16[256,2048]{1,0:T(8,128)(2,1)S(1)}, u32[]{:S(2)}, u32[]{:S(2)}) %collective-permute-start.47) | collective-permute-done | bytes 1048608 | tf_op jit(solution)/shard_map/ppermute | solution.py:21
  597.7 7.0 %collective-permute-done.54 = bf16[256,512]{1,0:T(8,128)(2,1)S(1)} collective-permute-done((bf16[256,512]{1,0:T(8,128)(2,1)}, bf16[256,512]{1,0:T(8,128)(2,1)S(1)}, u32[]{:S(2)}, u32[]{:S(2)}) %collective-permute-start.54) | collective-permute-done | bytes 262176 | tf_op jit(solution)/shard_map/ppermute | solution.py:21
  605.4 6.5 %collective-permute-done.55 = bf16[256,512]{1,0:T(8,128)(2,1)} collective-permute-done((bf16[256,512]{1,0:T(8,128)(2,1)S(1)}, bf16[256,512]{1,0:T(8,128)(2,1)}, u32[]{:S(2)}, u32[]{:S(2)}) %collective-permute-start.55) | collective-permute-done | bytes 262176 | tf_op jit(solution)/shard_map/ppermute | solution.py:21
  (410 shorter events, 223.2 us)
Async XLA Ops:
  7.2 170.1 %all-gather.2.cloned.1.call-start = ((), (), s32[]{:S(2)}) async-start(), calls=%async_computation | async-start | bytes 9437184 | tf_op jit(solution)/shard_map/all_gather | solution.py:736
  13.5 55.6 %collective-permute-start.1 = (bf16[256,2048]{1,0:T(8,128)(2,1)S(1)}, bf16[256,2048]{1,0:T(8,128)(2,1)S(1)}, u32[]{:S(2)}, u32[]{:S(2)}) collective-permute-start(bf16[256,2048]{1,0:T(8,128)(2,1)S(1)} %fusion.4.refs_3_), channel_id=1, source_target_pairs={{0,2},{1,3},{2,0},{3,1},{4,6},{5,7},{6,4},{7,5},{8,10},{9,11},{10,... | collective-permute-start | bytes 3145736 | tf_op jit(solution)/shard_map/ppermute | solution.py:21
  13.6 56.7 %collective-permute-start = (bf16[256,2048]{1,0:T(8,128)(2,1)S(1)}, bf16[256,2048]{1,0:T(8,128)(2,1)}, u32[]{:S(2)}, u32[]{:S(2)}) collective-permute-start(bf16[256,2048]{1,0:T(8,128)(2,1)S(1)} %fusion.4.refs_3_), channel_id=1, source_target_pairs={{0,1},{1,0},{2,3},{3,2},{4,5},{5,4},{6,7},{7,6},{8,9},{9,8},{10,11... | collective-permute-start | bytes 3145736 | tf_op jit(solution)/shard_map/ppermute | solution.py:21
  70.7 29.5 %collective-permute-start.4 = (bf16[256,2048]{1,0:T(8,128)(2,1)S(1)}, bf16[256,2048]{1,0:T(8,128)(2,1)}, u32[]{:S(2)}, u32[]{:S(2)}) collective-permute-start(bf16[256,2048]{1,0:T(8,128)(2,1)S(1)} %collective-permute-done.1.refs_5_), channel_id=1, source_target_pairs={{0,1},{1,0},{2,3},{3,2},{4,5},{5,4},{6,7},{7,6},{8,9},{9,8},{10,11... | collective-permute-start | bytes 3145736 | tf_op jit(solution)/shard_map/ppermute | solution.py:21
  102.5 70.3 %collective-permute-start.10 = (bf16[256,2048]{1,0:T(8,128)(2,1)}, bf16[256,2048]{1,0:T(8,128)(2,1)}, u32[]{:S(2)}, u32[]{:S(2)}) collective-permute-start(bf16[256,2048]{1,0:T(8,128)(2,1)} %fusion.10.branch_ref), channel_id=1, source_target_pairs={{0,2},{1,3},{2,0},{3,1},{4,6},{5,7},{6,4},{7,5},{8,10},{9,11},{10,... | collective-permute-start | bytes 3145736 | tf_op jit(solution)/shard_map/ppermute | solution.py:21
  105.9 67.0 %collective-permute-start.9 = (bf16[256,2048]{1,0:T(8,128)(2,1)}, bf16[256,2048]{1,0:T(8,128)(2,1)}, u32[]{:S(2)}, u32[]{:S(2)}) collective-permute-start(bf16[256,2048]{1,0:T(8,128)(2,1)} %fusion.10.branch_ref), channel_id=1, source_target_pairs={{0,1},{1,0},{2,3},{3,2},{4,5},{5,4},{6,7},{7,6},{8,9},{9,8},{10,11... | collective-permute-start | bytes 3145736 | tf_op jit(solution)/shard_map/ppermute | solution.py:21
  130.0 38.0 %collective-permute-start.8 = (bf16[256,512]{1,0:T(8,128)(2,1)S(1)}, bf16[256,512]{1,0:T(8,128)(2,1)S(1)}, u32[]{:S(2)}, u32[]{:S(2)}) collective-permute-start(bf16[256,512]{1,0:T(8,128)(2,1)S(1)} %get-tuple-element.642), channel_id=1, source_target_pairs={{0,3},{1,2},{2,1},{3,0},{4,7},{5,6},{6,5},{7,4},{8,11},{9,10},{10,... | collective-permute-start | bytes 786440 | tf_op jit(solution)/shard_map/ppermute | solution.py:21
  130.4 42.4 %collective-permute-start.7 = (bf16[256,512]{1,0:T(8,128)(2,1)S(1)}, bf16[256,512]{1,0:T(8,128)(2,1)S(1)}, u32[]{:S(2)}, u32[]{:S(2)}) collective-permute-start(bf16[256,512]{1,0:T(8,128)(2,1)S(1)} %get-tuple-element.643), channel_id=1, source_target_pairs={{0,2},{1,3},{2,0},{3,1},{4,6},{5,7},{6,4},{7,5},{8,10},{9,11},{10,... | collective-permute-start | bytes 786440 | tf_op jit(solution)/shard_map/ppermute | solution.py:21
  133.9 38.9 %collective-permute-start.6 = (bf16[256,512]{1,0:T(8,128)(2,1)S(1)}, bf16[256,512]{1,0:T(8,128)(2,1)S(1)}, u32[]{:S(2)}, u32[]{:S(2)}) collective-permute-start(bf16[256,512]{1,0:T(8,128)(2,1)S(1)} %get-tuple-element.644), channel_id=1, source_target_pairs={{0,1},{1,0},{2,3},{3,2},{4,5},{5,4},{6,7},{7,6},{8,9},{9,8},{10,11... | collective-permute-start | bytes 786440 | tf_op jit(solution)/shard_map/ppermute | solution.py:21
  175.9 42.8 %collective-permute-start.14 = (bf16[256,2048]{1,0:T(8,128)(2,1)}, bf16[256,2048]{1,0:T(8,128)(2,1)}, u32[]{:S(2)}, u32[]{:S(2)}) collective-permute-start(bf16[256,2048]{1,0:T(8,128)(2,1)} %constant_dynamic-update-slice_fusion.7), channel_id=1, source_target_pairs={{0,4},{4,0},{8,12},{12,8},{16,20},{20,16},{24,28},{28,24},{1,5},{5... | collective-permute-start | bytes 3145736 | tf_op jit(solution)/shard_map/ppermute | solution.py:21
  175.9 42.8 %collective-permute-start.13 = (bf16[256,2048]{1,0:T(8,128)(2,1)}, bf16[256,2048]{1,0:T(8,128)(2,1)}, u32[]{:S(2)}, u32[]{:S(2)}) collective-permute-start(bf16[256,2048]{1,0:T(8,128)(2,1)} %collective-permute-done.10.branch_ref), channel_id=1, source_target_pairs={{0,1},{1,0},{2,3},{3,2},{4,5},{5,4},{6,7},{7,6},{8,9},{9,8},{10,11... | collective-permute-start | bytes 3145736 | tf_op jit(solution)/shard_map/ppermute | solution.py:21
  188.8 47.7 %collective-permute-start.12 = (bf16[256,2048]{1,0:T(8,128)(2,1)S(1)}, bf16[256,2048]{1,0:T(8,128)(2,1)S(1)}, u32[]{:S(2)}, u32[]{:S(2)}) collective-permute-start(bf16[256,2048]{1,0:T(8,128)(2,1)S(1)} %get-tuple-element.320.rows_ref), channel_id=1, source_target_pairs={{0,2},{1,3},{2,0},{3,1},{4,6},{5,7},{6,4},{7,5},{8,10},{9,11},{10,... | collective-permute-start | bytes 3145736 | tf_op jit(solution)/shard_map/ppermute | solution.py:21
  190.9 55.8 %collective-permute-start.11 = (bf16[256,2048]{1,0:T(8,128)(2,1)S(1)}, bf16[256,2048]{1,0:T(8,128)(2,1)S(1)}, u32[]{:S(2)}, u32[]{:S(2)}) collective-permute-start(bf16[256,2048]{1,0:T(8,128)(2,1)S(1)} %get-tuple-element.320.rows_ref), channel_id=1, source_target_pairs={{0,1},{1,0},{2,3},{3,2},{4,5},{5,4},{6,7},{7,6},{8,9},{9,8},{10,11... | collective-permute-start | bytes 3145736 | tf_op jit(solution)/shard_map/ppermute | solution.py:21
  329.9 48.3 %collective-permute-start.26 = (bf16[256,2048]{1,0:T(8,128)(2,1)}, bf16[256,2048]{1,0:T(8,128)(2,1)S(1)}, u32[]{:S(2)}, u32[]{:S(2)}) collective-permute-start(bf16[256,2048]{1,0:T(8,128)(2,1)} %add_convert_fusion.3), channel_id=1, source_target_pairs={{0,2},{1,3},{2,0},{3,1},{4,6},{5,7},{6,4},{7,5},{8,10},{9,11},{10,... | collective-permute-start | bytes 3145736 | tf_op jit(solution)/shard_map/ppermute | solution.py:21
  333.0 46.6 %collective-permute-start.25 = (bf16[256,2048]{1,0:T(8,128)(2,1)S(1)}, bf16[256,2048]{1,0:T(8,128)(2,1)S(1)}, u32[]{:S(2)}, u32[]{:S(2)}) collective-permute-start(bf16[256,2048]{1,0:T(8,128)(2,1)S(1)} %copy-done.49), channel_id=1, source_target_pairs={{0,1},{1,0},{2,3},{3,2},{4,5},{5,4},{6,7},{7,6},{8,9},{9,8},{10,11... | collective-permute-start | bytes 3145736 | tf_op jit(solution)/shard_map/ppermute | solution.py:21
  348.0 31.6 %collective-permute-start.30 = (bf16[256,2048]{1,0:T(8,128)(2,1)S(1)}, bf16[256,2048]{1,0:T(8,128)(2,1)}, u32[]{:S(2)}, u32[]{:S(2)}) collective-permute-start(bf16[256,2048]{1,0:T(8,128)(2,1)S(1)} %bitcast.147), channel_id=1, source_target_pairs={{0,16},{4,20},{8,24},{12,28},{16,0},{20,4},{24,8},{28,12},{1,17},{... | collective-permute-start | bytes 3145736 | tf_op jit(solution)/shard_map/ppermute | solution.py:21
  349.6 30.0 %collective-permute-start.29 = (bf16[256,2048]{1,0:T(8,128)(2,1)S(1)}, bf16[256,2048]{1,0:T(8,128)(2,1)}, u32[]{:S(2)}, u32[]{:S(2)}) collective-permute-start(bf16[256,2048]{1,0:T(8,128)(2,1)S(1)} %bitcast.146), channel_id=1, source_target_pairs={{0,8},{4,12},{8,0},{12,4},{16,24},{20,28},{24,16},{28,20},{1,9},{5... | collective-permute-start | bytes 3145736 | tf_op jit(solution)/shard_map/ppermute | solution.py:21
  437.5 51.7 %collective-permute-start.40 = (bf16[256,2048]{1,0:T(8,128)(2,1)S(1)}, bf16[256,2048]{1,0:T(8,128)(2,1)S(1)}, u32[]{:S(2)}, u32[]{:S(2)}) collective-permute-start(bf16[256,2048]{1,0:T(8,128)(2,1)S(1)} %add_convert_fusion.2), channel_id=1, source_target_pairs={{0,2},{1,3},{2,0},{3,1},{4,6},{5,7},{6,4},{7,5},{8,10},{9,11},{10,... | collective-permute-start | bytes 3145736 | tf_op jit(solution)/shard_map/ppermute | solution.py:21
  439.9 45.8 %collective-permute-start.41 = (bf16[512,2048]{1,0:T(8,128)(2,1)S(1)}, bf16[512,2048]{1,0:T(8,128)(2,1)S(1)}, u32[]{:S(2)}, u32[]{:S(2)}) collective-permute-start(bf16[512,2048]{1,0:T(8,128)(2,1)S(1)} %pad_maximum_fusion.4), channel_id=1, source_target_pairs={{0,8},{4,12},{8,0},{12,4},{16,24},{20,28},{24,16},{28,20},{1,9},{5... | collective-permute-start | bytes 6291464 | tf_op jit(solution)/shard_map/ppermute | solution.py:21
  441.3 44.8 %collective-permute-start.42 = (bf16[512,2048]{1,0:T(8,128)(2,1)S(1)}, bf16[512,2048]{1,0:T(8,128)(2,1)S(1)}, u32[]{:S(2)}, u32[]{:S(2)}) collective-permute-start(bf16[512,2048]{1,0:T(8,128)(2,1)S(1)} %pad_maximum_fusion.5), channel_id=1, source_target_pairs={{0,16},{4,20},{8,24},{12,28},{16,0},{20,4},{24,8},{28,12},{1,17},{... | collective-permute-start | bytes 6291464 | tf_op jit(solution)/shard_map/ppermute | solution.py:21
  526.9 49.0 %collective-permute-start.46 = (bf16[256,2048]{1,0:T(8,128)(2,1)S(1)}, bf16[256,2048]{1,0:T(8,128)(2,1)S(1)}, u32[]{:S(2)}, u32[]{:S(2)}) collective-permute-start(bf16[256,2048]{1,0:T(8,128)(2,1)S(1)} %add_convert_fusion.1), channel_id=1, source_target_pairs={{0,2},{1,3},{2,0},{3,1},{4,6},{5,7},{6,4},{7,5},{8,10},{9,11},{10,... | collective-permute-start | bytes 3145736 | tf_op jit(solution)/shard_map/ppermute | solution.py:21
  528.1 47.9 %collective-permute-start.45 = (bf16[256,2048]{1,0:T(8,128)(2,1)S(1)}, bf16[256,2048]{1,0:T(8,128)(2,1)S(1)}, u32[]{:S(2)}, u32[]{:S(2)}) collective-permute-start(bf16[256,2048]{1,0:T(8,128)(2,1)S(1)} %get-tuple-element.536), channel_id=1, source_target_pairs={{0,1},{1,0},{2,3},{3,2},{4,5},{5,4},{6,7},{7,6},{8,9},{9,8},{10,11... | collective-permute-start | bytes 3145736 | tf_op jit(solution)/shard_map/ppermute | solution.py:21
  529.9 37.9 %collective-permute-start.47 = (bf16[256,2048]{1,0:T(8,128)(2,1)S(1)}, bf16[256,2048]{1,0:T(8,128)(2,1)S(1)}, u32[]{:S(2)}, u32[]{:S(2)}) collective-permute-start(bf16[256,2048]{1,0:T(8,128)(2,1)S(1)} %pad_maximum_fusion.11), channel_id=1, source_target_pairs={{0,16},{4,20},{8,24},{12,28},{16,0},{20,4},{24,8},{28,12},{1,17},{... | collective-permute-start | bytes 3145736 | tf_op jit(solution)/shard_map/ppermute | solution.py:21
  545.3 29.3 %collective-permute-start.50 = (bf16[128,1536]{1,0:T(8,128)(2,1)S(1)}, bf16[128,1536]{1,0:T(8,128)(2,1)S(1)}, u32[]{:S(2)}, u32[]{:S(2)}) collective-permute-start(bf16[128,1536]{1,0:T(8,128)(2,1)S(1)} %fusion.20), channel_id=1, source_target_pairs={{0,16},{4,20},{8,24},{12,28},{16,0},{20,4},{24,8},{28,12},{1,17},{... | collective-permute-start | bytes 1179656 | tf_op jit(solution)/shard_map/ppermute | solution.py:21
  (132 other events, 1880.9 us)
Sparse Core Ops, SparseCore 0:
  102.5 56.2 all-gather.1

commit v3 on v2

--- a/solution.py
+++ b/solution.py
@@ -143,12 +143,11 @@
     return (lax.axis_size(axis) // 2).bit_length() - 1
 
 
-def sum_everywhere(vector, axes):
-    for axis in axes:
-        bit = 1
-        while bit < lax.axis_size(axis):
-            vector = vector + hop(vector, axis, bit)
-            bit *= 2
+def sum_everywhere(vector, axis):
+    bit = 1
+    while bit < lax.axis_size(axis):
+        vector = vector + hop(vector, axis, bit)
+        bit *= 2
     return vector
 
 
@@ -228,8 +227,9 @@
 
 
 def attend_back_kernel(
-    place, share, qkv_ref, grad_ref, memory_ref, normer_ref, out_ref, mix_ref, grad_memory, grad_normer
+    place, share, qkv_ref, *more_refs
 ):
+    *grad_refs, memory_ref, normer_ref, out_ref, mix_ref, grad_memory, grad_normer, grad_ref = more_refs
     heads = grad_memory.shape[0]
     width = heads * DK
     step = pl.program_id(0)
@@ -240,6 +240,15 @@
         grad_memory[...] = jnp.zeros_like(grad_memory)
         grad_normer[...] = jnp.zeros_like(grad_normer)
         mix_ref[...] = jnp.zeros_like(mix_ref)
+
+    per_chunk = pl.num_programs(0) // len(grad_refs)
+    chunk = lax.div(segment, per_chunk) ^ place[0]
+    start = pl.multiple_of(lax.rem(segment, per_chunk) * SEG, SEG)
+    for k, piece_ref in enumerate(grad_refs):
+
+        @pl.when(chunk == k)
+        def _():
+            grad_ref[...] = piece_ref[pl.ds(start, SEG), :]
 
     live = live_column(segment, place[1])
     for h in range(heads):
@@ -362,7 +371,7 @@
             in_specs=[
                 pl.BlockSpec(memory_space=pltpu.SMEM),
                 pl.BlockSpec((SEG, wide), row_map),
-                pl.BlockSpec((SEG, heads * DK), row_map),
+                *[whole(piece.shape) for piece in grad_mixed],
                 pl.BlockSpec(
                     (1, heads, DK, DK), lambda step, place: (blocks - 1 - step, 0, 0, 0)
                 ),
@@ -372,7 +381,11 @@
                 pl.BlockSpec((SEG, wide), row_map),
                 pl.BlockSpec((heads, DK), lambda step, place: (0, 0)),
             ],
-            scratch_shapes=[pltpu.VMEM((heads, DK, DK), F32), pltpu.VMEM((heads, DK), F32)],
+            scratch_shapes=[
+                pltpu.VMEM((heads, DK, DK), F32),
+                pltpu.VMEM((heads, DK), F32),
+                pltpu.VMEM((SEG, heads * DK), LOW),
+            ],
         ),
         compiler_params=pltpu.CompilerParams(
             dimension_semantics=("arbitrary",), vmem_limit_bytes=24 << 20
@@ -382,7 +395,7 @@
             bytes_accessed=rows * wide * 6,
             transcendentals=0,
         ),
-    )(place, share, qkv, grad_mixed, memories, normers)
+    )(place, share, qkv, *grad_mixed, memories, normers)
 
 
 def live_rows(place, rows):
@@ -391,7 +404,7 @@
 
 
 def out_project_kernel(place, *refs):
-    *mixed_refs, out_ref, tokens_ref, gain_ref, state_ref, normed_ref = refs
+    *mixed_refs, out_ref, tokens_ref, gain_ref, state_ref, normed_ref, beside_ref = refs
     step = pl.program_id(0)
 
     @pl.when(step == 0)
@@ -403,7 +416,10 @@
 
         @pl.when(step == k)
         def _():
-            state_ref[...] += rows_by(mixed_ref[...], weight, (1, 0))
+            rows = mixed_ref[...]
+            width = rows.shape[1]
+            beside_ref[:, k * width : (k + 1) * width] = rows
+            state_ref[...] += rows_by(rows, weight, (1, 0))
 
     @pl.when(step == len(mixed_refs) - 1)
     def _():
@@ -432,42 +448,84 @@
         out_shape=(
             jax.ShapeDtypeStruct((rows, features), F32),
             jax.ShapeDtypeStruct((rows, features), LOW),
+            jax.ShapeDtypeStruct((rows, ranks * width), LOW),
         ),
         grid_spec=pltpu.PrefetchScalarGridSpec(
             num_scalar_prefetch=1,
             grid=(ranks,),
             in_specs=[whole((rows, width))] * ranks
             + [out_spec(out_full), whole((rows, features)), whole((1, features))],
-            out_specs=[whole((rows, features))] * 2,
+            out_specs=[whole((rows, features))] * 2 + [whole((rows, ranks * width))],
         ),
         compiler_params=pltpu.CompilerParams(
-            dimension_semantics=("arbitrary",), vmem_limit_bytes=24 << 20
+            dimension_semantics=("arbitrary",), vmem_limit_bytes=56 << 20
         ),
         cost_estimate=BRIEF,
     )(place, *[mixed[p] for p in range(ranks)], out_full, tokens, gain[None])
 
 
-def out_back_kernel(grad_ref, out_ref, back_ref):
-    weight = out_ref[...].reshape(-1, out_ref.shape[-1])
-    back_ref[0] = rows_by(grad_ref[...], weight, (1, 1)).astype(LOW)
-
-
-def out_back(grad_attn, out_full):
-    rows, features = grad_attn.shape
+def out_back_kernel(near, place, own_ref, *refs):
+    near_refs = refs[:near]
+    out_ref, state_ref, up_ref, gain_ref, *refs = refs[near:]
+    grad_ref, attn_ref, kept_ref, sent_ref, gain_sum_ref, *back_refs = refs
+    step = pl.program_id(0)
+
+    @pl.when(step == 0)
+    def _():
+        grad = own_ref[...]
+        for near_ref in near_refs:
+            grad = grad + near_ref[...].astype(F32)
+        state = state_ref[...]
+        through, gain_sum = normed_back(state, inverse_rms(state), gain_ref[...], grad)
+        grad = up_ref[...].astype(F32) + through
+        grad_ref[...] = grad
+        gain_sum_ref[...] = gain_sum[None]
+        attn_ref[...] = (grad * live_rows(place, grad.shape[0])).astype(LOW)
+        split_columns(place, attn_ref, kept_ref, sent_ref)
+
+    back = rows_by(attn_ref[...], out_ref[...].reshape(-1, out_ref.shape[-1]), (1, 1)).astype(LOW)
+    for k, back_ref in enumerate(back_refs):
+
+        @pl.when(step == k)
+        def _():
+            back_ref[...] = back
+
+
+def split_columns(place, source, kept, sent):
+    size = lax.axis_size("dp")
+    block = source.shape[1] // size
+    for r in range(size):
+        start = pl.multiple_of((place[2] ^ r) * block, block)
+        target = sent if r % 2 else kept
+        target[:, r // 2 * block : (r // 2 + 1) * block] = source[:, pl.ds(start, block)]
+
+
+def out_back(own, near, out_full, state, cotangent, gain, place):
+    rows, features = own.shape
     blocks, ranks, slice_rows, _ = out_full.shape
     width = blocks * slice_rows
-    return pl.pallas_call(
-        out_back_kernel,
+    square, half = (rows, features), (rows, features // 2)
+    shapes = [
+        (square, F32), (square, LOW), (half, LOW), (half, LOW), ((1, features), F32),
+        *[((rows, width), LOW)] * ranks,
+    ]
+    grad, _, kept, sent, gain_sum, *backs = pl.pallas_call(
+        functools.partial(out_back_kernel, len(near)),
         name="out_back",
-        out_shape=jax.ShapeDtypeStruct((ranks, rows, width), LOW),
-        grid=(ranks,),
-        in_specs=[whole((rows, features)), out_spec(out_full)],
-        out_specs=pl.BlockSpec((1, rows, width), lambda step: (step, 0, 0)),
+        out_shape=[jax.ShapeDtypeStruct(*shape) for shape in shapes],
+        grid_spec=pltpu.PrefetchScalarGridSpec(
+            num_scalar_prefetch=1,
+            grid=(ranks,),
+            in_specs=[whole(square)] * (1 + len(near))
+            + [out_spec(out_full), whole(square), whole(square), whole((1, features))],
+            out_specs=[whole(shape) for shape, _ in shapes],
+        ),
         compiler_params=pltpu.CompilerParams(
-            dimension_semantics=("arbitrary",), vmem_limit_bytes=24 << 20
+            dimension_semantics=("arbitrary",), vmem_limit_bytes=56 << 20
         ),
         cost_estimate=BRIEF,
-    )(grad_attn, out_full)
+    )(place, own, *near, out_full, state, cotangent, gain[None])
+    return grad, kept, sent, gain_sum[0], backs
 
 
 def feed_kernel(
@@ -491,14 +549,8 @@
     def _():
         two_sum[...] = jnp.zeros_like(two_sum)
         mlp_sum[...] = jnp.zeros_like(mlp_sum)
-        size = lax.axis_size("dp")
-        block = rows_ref.shape[1] // size
         for k, source in enumerate((rows_ref, branch_ref)):
-            for r in range(size):
-                start = pl.multiple_of((place[2] ^ r) * block, block)
-                target = sent_ref if r % 2 else kept_ref
-                at = r // 2 * block
-                target[k, :, at : at + block] = source[:, pl.ds(start, block)]
+            split_columns(place, source, kept_ref.at[k], sent_ref.at[k])
 
     rows = rows_ref[...]
     gate_pre = rows_by(rows, gate_ref[...], (1, 0))
@@ -749,8 +801,7 @@
     mixed, branch = hold((mixed, branch))
 
     out_full = out_full.reshape(blocks, ranks, slice_rows, features)
-    state, normed_two = out_project(mixed, out_full, tokens, mlp_gain, place)
-    mixed = stacked(mixed, axis=1)
+    state, normed_two, mixed = out_project(mixed, out_full, tokens, mlp_gain, place)
 
     made, kept, sent, two_parts, mlp_parts = {}, {}, {}, {}, {}
 
@@ -818,22 +869,23 @@
     gate_sum = weights_of(0, 1)
     fly(gate_sum)
     up_sum = weights_of(0, 2)
-    two_near, mlp_parts, gate_sum.state, up_sum.state, made, kept, their_made, their_kept = hold(
-        (two_near, mlp_parts, gate_sum.state, up_sum.state, made, kept, their_made, their_kept)
+    down_sum = weights_of(1, 0)
+    two_near, mlp_parts, gate_sum.state, up_sum.state, down_sum.state = hold(
+        (two_near, mlp_parts, gate_sum.state, up_sum.state, down_sum.state)
     )
 
     mlp_far = reduce_far(mlp_parts, "mp")
     fly(up_sum)
-    grad_normed_two = total(two_parts[0], two_near)
-    grad_through, grad_mlp_gain = normed_back(
-        state, inverse_rms(state), mlp_gain, grad_normed_two
-    )
-    grad_state = upstream + grad_through
-    grad_attn = (grad_state * live).astype(LOW)
-    grad_mixed = out_back(grad_attn, out_full)
-    attn_kept, attn_sent = relative_blocks(grad_attn, "dp")
+    grad_state, attn_kept, attn_sent, grad_mlp_gain, grad_mixed = out_back(
+        two_parts[0],
+        [two_near[p] for p in sorted(two_near)],
+        out_full,
+        state,
+        cotangent,
+        mlp_gain,
+        place,
+    )
     their_attn = hop(attn_sent, "dp", 1)
-    down_sum = weights_of(1, 0)
     (
         mlp_far, grad_mixed, attn_kept, their_attn, grad_state, grad_mlp_gain, mlp_parts,
         gate_sum.state, up_sum.state, down_sum.state,
@@ -843,7 +895,7 @@
             gate_sum.state, up_sum.state, down_sum.state,
         )
     )
-    grad_mixed = stacked(swap_pieces({p: grad_mixed[p] for p in pieces}, "mp"))
+    grad_mixed = swap_pieces(grad_mixed, "mp")
     fly(down_sum)
     out_sum = DeviceSum(
         weight_blocks(
@@ -863,7 +915,7 @@
     fly(out_sum, *([gate_sum, up_sum] if steps > 1 else []))
     down_sum.land()
     grad_qkv, grad_mix = attend_back(
-        qkv, grad_mixed, memories, normers, place, share, per_chunk
+        qkv, [grad_mixed[p] for p in pieces], memories, normers, place, share, per_chunk
     )
     grad_qkv, grad_mix, mlp_near, out_sum.state, down_sum.state, gate_sum.state, up_sum.state = hold(
         (grad_qkv, grad_mix, mlp_near, out_sum.state, down_sum.state, gate_sum.state, up_sum.state)
@@ -927,13 +979,13 @@
         (one_near, small, out_parts, block_out, grad_gate, grad_up, grad_down, grad_proj)
     )
 
-    small = sum_everywhere(small, ("mp", "dp"))
-    grad_query, grad_key, grad_value = (
-        grad_proj[:, j * width : (j + 1) * width] for j in range(3)
-    )
+    small = sum_everywhere(sum_everywhere(small, "mp"), "dp")
     grad_out = total(
         out_parts[0], {p: hop(out_parts[p], "mp", p) for p in range(1, ranks)}
     ).T
+    grad_query, grad_key, grad_value = (
+        grad_proj[:, j * width : (j + 1) * width] for j in range(3)
+    )
     grad_normed_one = total(one_parts[0], one_near)
     grad_inputs = normed_back(inputs, inverse_one, attn_gain, grad_normed_one)[0]
     grad_tokens = grad_state + grad_inputs
@@ -949,7 +1001,7 @@
         grad_down,
         small[:features],
         small[features : 2 * features],
-        small[2 * features :],
+        small[2 * features : 2 * features + heads * ranks],
     )
 
 

time: 628 us -> 623 us (level)
  Pallas kernels: 206 us -> 217 us
  other arithmetic: 49.4 us -> 40 us
  local copies, waits for them, and re-layouts: 58.6 us -> 50.6 us
    pallas_call x1, Pallas kernels: 3.57 us -> 13.2 us  [out_back(): pl.pallas_call(functools.partial(out_back_kernel, len(near)), name='out_b...]
    unnamed x184 -> x207, local copies, waits for them, and re-layouts: 43.9 us -> 35.5 us
  transfers between devices with their start and end apart: 62 -> 62, of which waited for: 30 -> 34; matrix products, arithmetic and copies ran while one was open for 14% -> 12% of each run, Pallas kernels for 33% -> 35%
where the time goes in v3:
time: 623 us; the launch traced here: 617 us
  waiting for transfers between devices  219 us (35%)
  Pallas kernels  217 us (35%)
  starting transfers between devices  58.9 us (9%)
  local copies, waits for them, and re-layouts  50.6 us (8%)
  other arithmetic  40 us (6%)
  between operations  16.5 us (3%)
  matrix products  15.5 us (2%)
    ppermute x61, waiting for transfers between devices, hop(): return lax.ppermute(value, axis, [(j, j ^ mask) for j in range(size)])  219 us
    pallas_call x4, Pallas kernels, feed_forward(): pl.pallas_call(feed_kernel, name='feed_forward', out_shape=(jax.ShapeDtyp...  83.8 us
    ppermute x61, starting transfers between devices, hop(): return lax.ppermute(value, axis, [(j, j ^ mask) for j in range(size)])  58.8 us
    pallas_call x5, Pallas kernels, weight_blocks(): pl.pallas_call(weight_kernel, name='weight_blocks', out_shape=[jax.ShapeD...  57.5 us
    unnamed x207, local copies, waits for them, and re-layouts  35.5 us
    pallas_call x1, Pallas kernels, attend_back(): pl.pallas_call(attend_back_kernel, name='attend_back', out_shape=(jax.Sha...  28.3 us
    dot_general x4, matrix products, rows_by(): lax.dot_general(left, right, ((contract[:1], contract[1:]), ((), ())), pr...  15.5 us
    pallas_call x1, Pallas kernels, attend(): pl.pallas_call(attend_kernel, name='attend', out_shape=(jax.ShapeDtypeStr...  14.6 us
  transfers between devices with their start and end apart: 62, of which 34 were waited for; matrix products, arithmetic and copies ran while one was open for 12% of the time, Pallas kernels for 35%

profile of v3, /device:TPU:8, one launch (start us, length us, event | category | flops | bytes accessed | tf_op | source)
XLA Modules:
  0.0 617.4 jit_solution(18393576429872744897)
XLA Ops:
  30.7 38.4 %collective-permute-done.1.refs_5_ = bf16[256,2048]{1,0:T(8,128)(2,1)S(1)} collective-permute-done((bf16[256,2048]{1,0:T(8,128)(2,1)S(1)}, bf16[256,2048]{1,0:T(8,128)(2,1)S(1)}, u32[]{:S(2)}, u32[]{:S(2)}) %collective-permute-start.1) | collective-permute-done | bytes 1048608 | tf_op jit(solution)/shard_map/ppermute | solution.py:21
  79.6 20.4 %collective-permute-done.4.refs_1_ = bf16[256,2048]{1,0:T(8,128)(2,1)S(1)} collective-permute-done((bf16[256,2048]{1,0:T(8,128)(2,1)S(1)}, bf16[256,2048]{1,0:T(8,128)(2,1)S(1)}, u32[]{:S(2)}, u32[]{:S(2)}) %collective-permute-start.4) | collective-permute-done | bytes 1048608 | tf_op jit(solution)/shard_map/ppermute | solution.py:21
  111.6 14.6 %attend.1 = (bf16[1024,512]{1,0:T(8,128)(2,1)S(1)}, f32[8,4,128,128]{3,2,1,0:T(8,128)S(1)}, f32[8,4,128]{2,1,0:T(4,128)S(1)}) custom-call(s32[3]{0:T(128)S(1)} %pad_add_fusion.place, f32[4]{0:T(128)S(1)} %add_divide_fusion.share, bf16[1024,1536]{1,0:T(8,128)(2,1)S(1)} %pad_maximum_fusion.qkv_ref), custom_call_target="tpu_custom_call" | custom-call | flops 1 | bytes 1 | tf_op jit(solution)/shard_map/attend/pallas_call | solution.py:324
  133.3 35.1 %collective-permute-done.8.refs_3_ = bf16[256,512]{1,0:T(8,128)(2,1)S(1)} collective-permute-done((bf16[256,512]{1,0:T(8,128)(2,1)S(1)}, bf16[256,512]{1,0:T(8,128)(2,1)S(1)}, u32[]{:S(2)}, u32[]{:S(2)}) %collective-permute-start.8) | collective-permute-done | bytes 262176 | tf_op jit(solution)/shard_map/ppermute | solution.py:21
  174.6 9.8 %out_project.1 = (f32[256,2048]{1,0:T(8,128)}, bf16[256,2048]{1,0:T(8,128)(2,1)}, bf16[256,2048]{1,0:T(8,128)(2,1)}) custom-call(s32[3]{0:T(128)} %copy-done.49, bf16[256,512]{1,0:T(8,128)(2,1)} %get-tuple-element.315.refs_0_, bf16[256,512]{1,0:T(8,128)(2,1)} %copy-done.90, bf16[256,512]{1,0:T(8,128)(2,1)} %copy-done.89, bf16[256,512]{1,0:T(8,128)(2,1)} %copy-done.88, ...), custom_call_target="tpu_custom_call" | custom-call | flops 1 | bytes 1 | tf_op jit(solution)/shard_map/out_project/pallas_call | solution.py:445
  195.5 20.9 %feed_forward.4 = (bf16[3,256,2048]{2,1,0:T(8,128)(2,1)}, bf16[2,256,1024]{2,1,0:T(8,128)(2,1)S(1)}, bf16[2,256,1024]{2,1,0:T(8,128)(2,1)}, f32[256,2048]{1,0:T(8,128)S(1)}, f32[256,2048]{1,0:T(8,128)S(1)}) custom-call(s32[3]{0:T(128)S(1)} %copy-done.50, bf16[256,2048]{1,0:T(8,128)(2,1)S(1)} %copy-done.37, ...), custom_call_target="tpu_custom_call" | custom-call | flops 1 | bytes 1 | tf_op jit(solution)/shard_map/feed_forward/pallas_call | solution.py:586
  218.7 13.8 %collective-permute-done.12.rows_ref = bf16[256,2048]{1,0:T(8,128)(2,1)S(1)} collective-permute-done((bf16[256,2048]{1,0:T(8,128)(2,1)}, bf16[256,2048]{1,0:T(8,128)(2,1)S(1)}, u32[]{:S(2)}, u32[]{:S(2)}) %collective-permute-start.12) | collective-permute-done | bytes 1048608 | tf_op jit(solution)/shard_map/ppermute | solution.py:21
  232.6 10.9 %collective-permute-done.11.rows_ref = bf16[256,2048]{1,0:T(8,128)(2,1)S(1)} collective-permute-done((bf16[256,2048]{1,0:T(8,128)(2,1)}, bf16[256,2048]{1,0:T(8,128)(2,1)S(1)}, u32[]{:S(2)}, u32[]{:S(2)}) %collective-permute-start.11) | collective-permute-done | bytes 1048608 | tf_op jit(solution)/shard_map/ppermute | solution.py:21
  244.4 21.5 %feed_forward.5 = (bf16[3,256,2048]{2,1,0:T(8,128)(2,1)S(1)}, bf16[2,256,1024]{2,1,0:T(8,128)(2,1)S(1)}, bf16[2,256,1024]{2,1,0:T(8,128)(2,1)}, bf16[256,2048]{1,0:T(8,128)(2,1)S(1)}, bf16[256,2048]{1,0:T(8,128)(2,1)}) custom-call(s32[3]{0:T(128)S(1)} %copy-done.50, bf16[256,2048]{1,0:T(8,128)(2,1)S(1)} %collective-permute-done.11.rows_ref, ...), custom_call_target="tpu_custom_call" | custom-call | flops 1 | bytes 1 | tf_op jit(solution)/shard_map/feed_forward/pallas_call | solution.py:586
  271.3 20.8 %feed_forward.6 = (bf16[3,256,2048]{2,1,0:T(8,128)(2,1)S(1)}, bf16[2,256,1024]{2,1,0:T(8,128)(2,1)S(1)}, bf16[2,256,1024]{2,1,0:T(8,128)(2,1)}, bf16[256,2048]{1,0:T(8,128)(2,1)}, bf16[256,2048]{1,0:T(8,128)(2,1)}) custom-call(s32[3]{0:T(128)S(1)} %copy-done.50, bf16[256,2048]{1,0:T(8,128)(2,1)S(1)} %collective-permute-done.15.rows_ref, ...), custom_call_target="tpu_custom_call" | custom-call | flops 1 | bytes 1 | tf_op jit(solution)/shard_map/feed_forward/pallas_call | solution.py:586
  298.8 20.7 %feed_forward.7 = (bf16[3,256,2048]{2,1,0:T(8,128)(2,1)}, bf16[2,256,1024]{2,1,0:T(8,128)(2,1)S(1)}, bf16[2,256,1024]{2,1,0:T(8,128)(2,1)S(1)}, f32[256,2048]{1,0:T(8,128)S(1)}, f32[256,2048]{1,0:T(8,128)S(1)}) custom-call(s32[3]{0:T(128)S(1)} %copy-done.50, bf16[256,2048]{1,0:T(8,128)(2,1)S(1)} %copy-done.34, ...), custom_call_target="tpu_custom_call" | custom-call | flops 1 | bytes 1 | tf_op jit(solution)/shard_map/feed_forward/pallas_call | solution.py:586
  329.6 13.9 %weight_blocks.5 = (bf16[2,128,2048]{2,1,0:T(8,128)(2,1)S(1)}, bf16[2,128,2048]{2,1,0:T(8,128)(2,1)S(1)}, bf16[2,128,2048]{2,1,0:T(8,128)(2,1)S(1)}, bf16[2,128,2048]{2,1,0:T(8,128)(2,1)S(1)}) custom-call(bf16[2,256,1024]{2,1,0:T(8,128)(2,1)S(1)} %get-tuple-element.398.refs_0_, bf16[2,256,1024]{2,1,0:T(8,128)(2,1)S(1)} %get-tuple-element.399.refs_1_, ...), custom_call_target="tpu_custom_call" | custom-call | flops 1 | bytes 1 | tf_op jit(solution)/shard_map/weight_blocks/pallas_call | solution.py:697
  347.5 13.9 %weight_blocks.7 = (bf16[2,128,2048]{2,1,0:T(8,128)(2,1)S(1)}, bf16[2,128,2048]{2,1,0:T(8,128)(2,1)S(1)}, bf16[2,128,2048]{2,1,0:T(8,128)(2,1)S(1)}, bf16[2,128,2048]{2,1,0:T(8,128)(2,1)S(1)}) custom-call(bf16[2,256,1024]{2,1,0:T(8,128)(2,1)S(1)} %get-tuple-element.398.refs_0_, bf16[2,256,1024]{2,1,0:T(8,128)(2,1)S(1)} %get-tuple-element.399.refs_1_, ...), custom_call_target="tpu_custom_call" | custom-call | flops 1 | bytes 1 | tf_op jit(solution)/shard_map/weight_blocks/pallas_call | solution.py:697
  361.4 15.5 %weight_blocks.6 = (bf16[2,128,2048]{2,1,0:T(8,128)(2,1)S(1)}, bf16[2,128,2048]{2,1,0:T(8,128)(2,1)}, bf16[2,128,2048]{2,1,0:T(8,128)(2,1)S(1)}, bf16[2,128,2048]{2,1,0:T(8,128)(2,1)}) custom-call(bf16[2,256,1024]{2,1,0:T(8,128)(2,1)S(1)} %get-tuple-element.398.refs_0_, bf16[2,256,1024]{2,1,0:T(8,128)(2,1)S(1)} %get-tuple-element.399.refs_1_, ...), custom_call_target="tpu_custom_call" | custom-call | flops 1 | bytes 1 | tf_op jit(solution)/shard_map/weight_blocks/pallas_call | solution.py:697
  380.5 13.2 %out_back.1 = (f32[256,2048]{1,0:T(8,128)}, bf16[256,2048]{1,0:T(8,128)(2,1)}, bf16[256,1024]{1,0:T(8,128)(2,1)}, bf16[256,1024]{1,0:T(8,128)(2,1)}, f32[1,2048]...) custom-call(s32[3]{0:T(128)} %copy-done.49, ...), custom_call_target="tpu_custom_call" | custom-call | flops 1 | bytes 1 | tf_op jit(solution)/shard_map/out_back/pallas_call | solution.py:512
  395.8 8.1 %collective-permute-done.34 = bf16[256,2048]{1,0:T(8,128)(2,1)} collective-permute-done((bf16[256,2048]{1,0:T(8,128)(2,1)}, bf16[256,2048]{1,0:T(8,128)(2,1)}, u32[]{:S(2)}, u32[]{:S(2)}) %collective-permute-start.34) | collective-permute-done | bytes 1048608 | tf_op jit(solution)/shard_map/ppermute | solution.py:21
  441.3 28.3 %attend_back.1 = (bf16[1024,1536]{1,0:T(8,128)(2,1)S(1)}, f32[4,128]{1,0:T(4,128)S(1)}) custom-call(s32[3]{0:T(128)S(1)} %copy-done.51, f32[4]{0:T(128)S(1)} %add_divide_fusion.share, bf16[1024,1536]{1,0:T(8,128)(2,1)S(1)} %copy-done.7, bf16[256,512]{1,0:T(8,128)(2,1)S(1)} %copy-done.60, bf16[256,512]{1,0:T(8,128)(2,1)S(1)} %collective-permute-done.35.more_refs_1_, ...), custom_call_target="tpu_custom_call" | custom-call | flops 16106127360 | bytes 9437184 | tf_op jit(solution)/shard_map/attend_back/pallas_call | solution.py:361
  473.0 7.0 %collective-permute-done.41 = bf16[512,2048]{1,0:T(8,128)(2,1)S(1)} collective-permute-done((bf16[512,2048]{1,0:T(8,128)(2,1)S(1)}, bf16[512,2048]{1,0:T(8,128)(2,1)S(1)}, u32[]{:S(2)}, u32[]{:S(2)}) %collective-permute-start.41) | collective-permute-done | bytes 2097184 | tf_op jit(solution)/shard_map/ppermute | solution.py:21
  499.6 10.4 %weight_blocks.9 = (bf16[2,128,1536]{2,1,0:T(8,128)(2,1)S(1)}, bf16[2,128,1536]{2,1,0:T(8,128)(2,1)S(1)}, bf16[2,128,1536]{2,1,0:T(8,128)(2,1)S(1)}, bf16[2,128,1536]{2,1,0:T(8,128)(2,1)S(1)}) custom-call(bf16[1,1024,1024]{2,1,0:T(8,128)(2,1)S(1)} %bitcast.125, bf16[1,1024,1024]{2,1,0:T(8,128)(2,1)S(1)} %bitcast.126, bf16[1,1024,1536]{2,1,0:T(8,128)(2,1)S(1)} %bitcast.122, ...), custom_call_target="tpu_custom_call" | custom-call | flops 1 | bytes 1 | tf_op jit(solution)/shard_map/weight_blocks/pallas_call | solution.py:697
  510.0 6.3 %project_back.3 = (f32[256,2048]{1,0:T(8,128)S(1)}, bf16[256,2048]{1,0:T(8,128)(2,1)S(1)}, f32[256,2048]{1,0:T(8,128)S(1)}, f32[1,2048]{1,0:T(1,128)S(1)}) custom-call(bf16[1024,1536]{1,0:T(8,128)(2,1)S(1)} %get-tuple-element.531.refs_0_.refs_1_.refs_2_, bf16[1024,1536]{1,0:T(8,128)(2,1)S(1)} %get-tuple-element.531.refs_0_.refs_1_.refs_2_, ...), custom_call_target="tpu_custom_call" | custom-call | flops 1 | bytes 1 | tf_op jit(solution)/shard_map/project_back/pallas_call | solution.py:635
  529.2 8.4 %collective-permute-done.49 = bf16[256,1536]{1,0:T(8,128)(2,1)S(1)} collective-permute-done((bf16[256,1536]{1,0:T(8,128)(2,1)S(1)}, bf16[256,1536]{1,0:T(8,128)(2,1)S(1)}, u32[]{:S(2)}, u32[]{:S(2)}) %collective-permute-start.49) | collective-permute-done | bytes 786464 | tf_op jit(solution)/shard_map/ppermute | solution.py:21
  540.6 21.6 %collective-permute-done.47 = bf16[256,2048]{1,0:T(8,128)(2,1)S(1)} collective-permute-done((bf16[256,2048]{1,0:T(8,128)(2,1)S(1)}, bf16[256,2048]{1,0:T(8,128)(2,1)S(1)}, u32[]{:S(2)}, u32[]{:S(2)}) %collective-permute-start.47) | collective-permute-done | bytes 1048608 | tf_op jit(solution)/shard_map/ppermute | solution.py:21
  592.3 6.3 %collective-permute-done.54 = bf16[256,512]{1,0:T(8,128)(2,1)} collective-permute-done((bf16[256,512]{1,0:T(8,128)(2,1)}, bf16[256,512]{1,0:T(8,128)(2,1)}, u32[]{:S(2)}, u32[]{:S(2)}) %collective-permute-start.54) | collective-permute-done | bytes 262176 | tf_op jit(solution)/shard_map/ppermute | solution.py:21
  598.7 7.4 %collective-permute-done.55 = bf16[256,512]{1,0:T(8,128)(2,1)} collective-permute-done((bf16[256,512]{1,0:T(8,128)(2,1)}, bf16[256,512]{1,0:T(8,128)(2,1)}, u32[]{:S(2)}, u32[]{:S(2)}) %collective-permute-start.55) | collective-permute-done | bytes 262176 | tf_op jit(solution)/shard_map/ppermute | solution.py:21
  (421 shorter events, 213.6 us)
Async XLA Ops:
  7.2 167.4 %all-gather.2.cloned.1.call-start = ((), (), s32[]{:S(2)}) async-start(), calls=%async_computation | async-start | bytes 9437184 | tf_op jit(solution)/shard_map/all_gather | solution.py:788
  13.5 55.6 %collective-permute-start.1 = (bf16[256,2048]{1,0:T(8,128)(2,1)S(1)}, bf16[256,2048]{1,0:T(8,128)(2,1)S(1)}, u32[]{:S(2)}, u32[]{:S(2)}) collective-permute-start(bf16[256,2048]{1,0:T(8,128)(2,1)S(1)} %fusion.4.refs_3_), channel_id=1, source_target_pairs={{0,2},{1,3},{2,0},{3,1},{4,6},{5,7},{6,4},{7,5},{8,10},{9,11},{10,... | collective-permute-start | bytes 3145736 | tf_op jit(solution)/shard_map/ppermute | solution.py:21
  13.6 56.6 %collective-permute-start = (bf16[256,2048]{1,0:T(8,128)(2,1)S(1)}, bf16[256,2048]{1,0:T(8,128)(2,1)S(1)}, u32[]{:S(2)}, u32[]{:S(2)}) collective-permute-start(bf16[256,2048]{1,0:T(8,128)(2,1)S(1)} %fusion.4.refs_3_), channel_id=1, source_target_pairs={{0,1},{1,0},{2,3},{3,2},{4,5},{5,4},{6,7},{7,6},{8,9},{9,8},{10,11... | collective-permute-start | bytes 3145736 | tf_op jit(solution)/shard_map/ppermute | solution.py:21
  70.6 29.4 %collective-permute-start.4 = (bf16[256,2048]{1,0:T(8,128)(2,1)S(1)}, bf16[256,2048]{1,0:T(8,128)(2,1)S(1)}, u32[]{:S(2)}, u32[]{:S(2)}) collective-permute-start(bf16[256,2048]{1,0:T(8,128)(2,1)S(1)} %collective-permute-done.1.refs_5_), channel_id=1, source_target_pairs={{0,1},{1,0},{2,3},{3,2},{4,5},{5,4},{6,7},{7,6},{8,9},{9,8},{10,11... | collective-permute-start | bytes 3145736 | tf_op jit(solution)/shard_map/ppermute | solution.py:21
  102.7 70.5 %collective-permute-start.10 = (bf16[256,2048]{1,0:T(8,128)(2,1)}, bf16[256,2048]{1,0:T(8,128)(2,1)}, u32[]{:S(2)}, u32[]{:S(2)}) collective-permute-start(bf16[256,2048]{1,0:T(8,128)(2,1)} %multiply_convert_fusion.branch_ref), channel_id=1, source_target_pairs={{0,2},{1,3},{2,0},{3,1},{4,6},{5,7},{6,4},{7,5},{8,10},{9,11},{10,... | collective-permute-start | bytes 3145736 | tf_op jit(solution)/shard_map/ppermute | solution.py:21
  106.2 67.0 %collective-permute-start.9 = (bf16[256,2048]{1,0:T(8,128)(2,1)}, bf16[256,2048]{1,0:T(8,128)(2,1)}, u32[]{:S(2)}, u32[]{:S(2)}) collective-permute-start(bf16[256,2048]{1,0:T(8,128)(2,1)} %multiply_convert_fusion.branch_ref), channel_id=1, source_target_pairs={{0,1},{1,0},{2,3},{3,2},{4,5},{5,4},{6,7},{7,6},{8,9},{9,8},{10,11... | collective-permute-start | bytes 3145736 | tf_op jit(solution)/shard_map/ppermute | solution.py:21
  127.0 41.4 %collective-permute-start.8 = (bf16[256,512]{1,0:T(8,128)(2,1)S(1)}, bf16[256,512]{1,0:T(8,128)(2,1)S(1)}, u32[]{:S(2)}, u32[]{:S(2)}) collective-permute-start(bf16[256,512]{1,0:T(8,128)(2,1)S(1)} %get-tuple-element.632), channel_id=1, source_target_pairs={{0,3},{1,2},{2,1},{3,0},{4,7},{5,6},{6,5},{7,4},{8,11},{9,10},{10,... | collective-permute-start | bytes 786440 | tf_op jit(solution)/shard_map/ppermute | solution.py:21
  127.4 45.8 %collective-permute-start.7 = (bf16[256,512]{1,0:T(8,128)(2,1)S(1)}, bf16[256,512]{1,0:T(8,128)(2,1)S(1)}, u32[]{:S(2)}, u32[]{:S(2)}) collective-permute-start(bf16[256,512]{1,0:T(8,128)(2,1)S(1)} %get-tuple-element.633), channel_id=1, source_target_pairs={{0,2},{1,3},{2,0},{3,1},{4,6},{5,7},{6,4},{7,5},{8,10},{9,11},{10,... | collective-permute-start | bytes 786440 | tf_op jit(solution)/shard_map/ppermute | solution.py:21
  131.1 42.0 %collective-permute-start.6 = (bf16[256,512]{1,0:T(8,128)(2,1)S(1)}, bf16[256,512]{1,0:T(8,128)(2,1)S(1)}, u32[]{:S(2)}, u32[]{:S(2)}) collective-permute-start(bf16[256,512]{1,0:T(8,128)(2,1)S(1)} %get-tuple-element.634), channel_id=1, source_target_pairs={{0,1},{1,0},{2,3},{3,2},{4,5},{5,4},{6,7},{7,6},{8,9},{9,8},{10,11... | collective-permute-start | bytes 786440 | tf_op jit(solution)/shard_map/ppermute | solution.py:21
  173.2 44.5 %collective-permute-start.13 = (bf16[256,2048]{1,0:T(8,128)(2,1)}, bf16[256,2048]{1,0:T(8,128)(2,1)S(1)}, u32[]{:S(2)}, u32[]{:S(2)}) collective-permute-start(bf16[256,2048]{1,0:T(8,128)(2,1)} %collective-permute-done.10.branch_ref), channel_id=1, source_target_pairs={{0,1},{1,0},{2,3},{3,2},{4,5},{5,4},{6,7},{7,6},{8,9},{9,8},{10,11... | collective-permute-start | bytes 3145736 | tf_op jit(solution)/shard_map/ppermute | solution.py:21
  184.4 48.1 %collective-permute-start.12 = (bf16[256,2048]{1,0:T(8,128)(2,1)}, bf16[256,2048]{1,0:T(8,128)(2,1)S(1)}, u32[]{:S(2)}, u32[]{:S(2)}) collective-permute-start(bf16[256,2048]{1,0:T(8,128)(2,1)} %get-tuple-element.323.rows_ref), channel_id=1, source_target_pairs={{0,2},{1,3},{2,0},{3,1},{4,6},{5,7},{6,4},{7,5},{8,10},{9,11},{10,... | collective-permute-start | bytes 3145736 | tf_op jit(solution)/shard_map/ppermute | solution.py:21
  187.1 56.3 %collective-permute-start.11 = (bf16[256,2048]{1,0:T(8,128)(2,1)}, bf16[256,2048]{1,0:T(8,128)(2,1)S(1)}, u32[]{:S(2)}, u32[]{:S(2)}) collective-permute-start(bf16[256,2048]{1,0:T(8,128)(2,1)} %get-tuple-element.323.rows_ref), channel_id=1, source_target_pairs={{0,1},{1,0},{2,3},{3,2},{4,5},{5,4},{6,7},{7,6},{8,9},{9,8},{10,11... | collective-permute-start | bytes 3145736 | tf_op jit(solution)/shard_map/ppermute | solution.py:21
  188.5 30.3 %collective-permute-start.14 = (bf16[256,2048]{1,0:T(8,128)(2,1)}, bf16[256,2048]{1,0:T(8,128)(2,1)S(1)}, u32[]{:S(2)}, u32[]{:S(2)}) collective-permute-start(bf16[256,2048]{1,0:T(8,128)(2,1)} %get-tuple-element.335), channel_id=1, source_target_pairs={{0,4},{4,0},{8,12},{12,8},{16,20},{20,16},{24,28},{28,24},{1,5},{5... | collective-permute-start | bytes 3145736 | tf_op jit(solution)/shard_map/ppermute | solution.py:21
  323.9 55.0 %collective-permute-start.26 = (bf16[256,2048]{1,0:T(8,128)(2,1)}, bf16[256,2048]{1,0:T(8,128)(2,1)S(1)}, u32[]{:S(2)}, u32[]{:S(2)}) collective-permute-start(bf16[256,2048]{1,0:T(8,128)(2,1)} %add_convert_fusion.3), channel_id=1, source_target_pairs={{0,2},{1,3},{2,0},{3,1},{4,6},{5,7},{6,4},{7,5},{8,10},{9,11},{10,... | collective-permute-start | bytes 3145736 | tf_op jit(solution)/shard_map/ppermute | solution.py:21
  327.2 51.7 %collective-permute-start.25 = (bf16[256,2048]{1,0:T(8,128)(2,1)S(1)}, bf16[256,2048]{1,0:T(8,128)(2,1)S(1)}, u32[]{:S(2)}, u32[]{:S(2)}) collective-permute-start(bf16[256,2048]{1,0:T(8,128)(2,1)S(1)} %copy-done.59), channel_id=1, source_target_pairs={{0,1},{1,0},{2,3},{3,2},{4,5},{5,4},{6,7},{7,6},{8,9},{9,8},{10,11... | collective-permute-start | bytes 3145736 | tf_op jit(solution)/shard_map/ppermute | solution.py:21
  344.4 34.5 %collective-permute-start.30 = (bf16[256,2048]{1,0:T(8,128)(2,1)S(1)}, bf16[256,2048]{1,0:T(8,128)(2,1)}, u32[]{:S(2)}, u32[]{:S(2)}) collective-permute-start(bf16[256,2048]{1,0:T(8,128)(2,1)S(1)} %bitcast.136), channel_id=1, source_target_pairs={{0,16},{4,20},{8,24},{12,28},{16,0},{20,4},{24,8},{28,12},{1,17},{... | collective-permute-start | bytes 3145736 | tf_op jit(solution)/shard_map/ppermute | solution.py:21
  346.0 33.0 %collective-permute-start.29 = (bf16[256,2048]{1,0:T(8,128)(2,1)S(1)}, bf16[256,2048]{1,0:T(8,128)(2,1)}, u32[]{:S(2)}, u32[]{:S(2)}) collective-permute-start(bf16[256,2048]{1,0:T(8,128)(2,1)S(1)} %bitcast.135), channel_id=1, source_target_pairs={{0,8},{4,12},{8,0},{12,4},{16,24},{20,28},{24,16},{28,20},{1,9},{5... | collective-permute-start | bytes 3145736 | tf_op jit(solution)/shard_map/ppermute | solution.py:21
  432.7 51.5 %collective-permute-start.40 = (bf16[256,2048]{1,0:T(8,128)(2,1)S(1)}, bf16[256,2048]{1,0:T(8,128)(2,1)S(1)}, u32[]{:S(2)}, u32[]{:S(2)}) collective-permute-start(bf16[256,2048]{1,0:T(8,128)(2,1)S(1)} %add_convert_fusion.2), channel_id=1, source_target_pairs={{0,2},{1,3},{2,0},{3,1},{4,6},{5,7},{6,4},{7,5},{8,10},{9,11},{10,... | collective-permute-start | bytes 3145736 | tf_op jit(solution)/shard_map/ppermute | solution.py:21
  436.8 43.2 %collective-permute-start.41 = (bf16[512,2048]{1,0:T(8,128)(2,1)S(1)}, bf16[512,2048]{1,0:T(8,128)(2,1)S(1)}, u32[]{:S(2)}, u32[]{:S(2)}) collective-permute-start(bf16[512,2048]{1,0:T(8,128)(2,1)S(1)} %pad_maximum_fusion.4), channel_id=1, source_target_pairs={{0,8},{4,12},{8,0},{12,4},{16,24},{20,28},{24,16},{28,20},{1,9},{5... | collective-permute-start | bytes 6291464 | tf_op jit(solution)/shard_map/ppermute | solution.py:21
  438.6 42.8 %collective-permute-start.42 = (bf16[512,2048]{1,0:T(8,128)(2,1)S(1)}, bf16[512,2048]{1,0:T(8,128)(2,1)S(1)}, u32[]{:S(2)}, u32[]{:S(2)}) collective-permute-start(bf16[512,2048]{1,0:T(8,128)(2,1)S(1)} %pad_maximum_fusion.5), channel_id=1, source_target_pairs={{0,16},{4,20},{8,24},{12,28},{16,0},{20,4},{24,8},{28,12},{1,17},{... | collective-permute-start | bytes 6291464 | tf_op jit(solution)/shard_map/ppermute | solution.py:21
  521.4 49.0 %collective-permute-start.46 = (bf16[256,2048]{1,0:T(8,128)(2,1)S(1)}, bf16[256,2048]{1,0:T(8,128)(2,1)S(1)}, u32[]{:S(2)}, u32[]{:S(2)}) collective-permute-start(bf16[256,2048]{1,0:T(8,128)(2,1)S(1)} %add_convert_fusion.1), channel_id=1, source_target_pairs={{0,2},{1,3},{2,0},{3,1},{4,6},{5,7},{6,4},{7,5},{8,10},{9,11},{10,... | collective-permute-start | bytes 3145736 | tf_op jit(solution)/shard_map/ppermute | solution.py:21
  522.2 48.2 %collective-permute-start.45 = (bf16[256,2048]{1,0:T(8,128)(2,1)S(1)}, bf16[256,2048]{1,0:T(8,128)(2,1)S(1)}, u32[]{:S(2)}, u32[]{:S(2)}) collective-permute-start(bf16[256,2048]{1,0:T(8,128)(2,1)S(1)} %get-tuple-element.542), channel_id=1, source_target_pairs={{0,1},{1,0},{2,3},{3,2},{4,5},{5,4},{6,7},{7,6},{8,9},{9,8},{10,11... | collective-permute-start | bytes 3145736 | tf_op jit(solution)/shard_map/ppermute | solution.py:21
  523.2 39.0 %collective-permute-start.47 = (bf16[256,2048]{1,0:T(8,128)(2,1)S(1)}, bf16[256,2048]{1,0:T(8,128)(2,1)S(1)}, u32[]{:S(2)}, u32[]{:S(2)}) collective-permute-start(bf16[256,2048]{1,0:T(8,128)(2,1)S(1)} %pad_maximum_fusion.10), channel_id=1, source_target_pairs={{0,16},{4,20},{8,24},{12,28},{16,0},{20,4},{24,8},{28,12},{1,17},{... | collective-permute-start | bytes 3145736 | tf_op jit(solution)/shard_map/ppermute | solution.py:21
  539.8 29.3 %collective-permute-start.50 = (bf16[128,1536]{1,0:T(8,128)(2,1)S(1)}, bf16[128,1536]{1,0:T(8,128)(2,1)S(1)}, u32[]{:S(2)}, u32[]{:S(2)}) collective-permute-start(bf16[128,1536]{1,0:T(8,128)(2,1)S(1)} %fusion.19), channel_id=1, source_target_pairs={{0,16},{4,20},{8,24},{12,28},{16,0},{20,4},{24,8},{28,12},{1,17},{... | collective-permute-start | bytes 1179656 | tf_op jit(solution)/shard_map/ppermute | solution.py:21
  (145 other events, 1582.9 us)
Sparse Core Ops, SparseCore 0:
  102.6 56.3 all-gather.1

commit v4 on v3

--- a/solution.py
+++ b/solution.py
@@ -404,7 +404,7 @@
 
 
 def out_project_kernel(place, *refs):
-    *mixed_refs, out_ref, tokens_ref, gain_ref, state_ref, normed_ref, beside_ref = refs
+    *mixed_refs, out_ref, tokens_ref, gain_ref, state_ref, normed_ref, beside_ref, piece = refs
     step = pl.program_id(0)
 
     @pl.when(step == 0)
@@ -419,7 +419,9 @@
             rows = mixed_ref[...]
             width = rows.shape[1]
             beside_ref[:, k * width : (k + 1) * width] = rows
-            state_ref[...] += rows_by(rows, weight, (1, 0))
+            piece[...] = rows
+
+    state_ref[...] += rows_by(piece[...], weight, (1, 0))
 
     @pl.when(step == len(mixed_refs) - 1)
     def _():
@@ -456,6 +458,7 @@
             in_specs=[whole((rows, width))] * ranks
             + [out_spec(out_full), whole((rows, features)), whole((1, features))],
             out_specs=[whole((rows, features))] * 2 + [whole((rows, ranks * width))],
+            scratch_shapes=[pltpu.VMEM((rows, width), LOW)],
         ),
         compiler_params=pltpu.CompilerParams(
             dimension_semantics=("arbitrary",), vmem_limit_bytes=56 << 20
@@ -643,7 +646,7 @@
         + [pl.BlockSpec((tile, wide), lambda step: (step, 0))],
         out_specs=[made] * len(wanted) + [pl.BlockSpec((1, tile), lambda step: (0, step))],
         compiler_params=pltpu.CompilerParams(
-            dimension_semantics=("arbitrary",), vmem_limit_bytes=24 << 20
+            dimension_semantics=("arbitrary",), vmem_limit_bytes=56 << 20
         ),
         cost_estimate=BRIEF,
     )(*[rows] * len(wanted), *[one[p] for p in wanted], weight)

time: 623 us -> 624 us (level)
  transfers between devices with their start and end apart: 62 -> 62, of which waited for: 34 -> 33; matrix products, arithmetic and copies ran while one was open for 12% -> 12% of each run, Pallas kernels for 35% -> 36%
where the time goes in v4:
time: 624 us; the launch traced here: 618 us
  Pallas kernels  223 us (36%)
  waiting for transfers between devices  214 us (34%)
  starting transfers between devices  60.6 us (10%)
  local copies, waits for them, and re-layouts  47.3 us (8%)
  other arithmetic  40.9 us (7%)
  between operations  16.5 us (3%)
  matrix products  15.5 us (2%)
    ppermute x61, waiting for transfers between devices, hop(): return lax.ppermute(value, axis, [(j, j ^ mask) for j in range(size)])  214 us
    pallas_call x4, Pallas kernels, feed_forward(): pl.pallas_call(feed_kernel, name='feed_forward', out_shape=(jax.ShapeDtyp...  83.8 us
    ppermute x61, starting transfers between devices, hop(): return lax.ppermute(value, axis, [(j, j ^ mask) for j in range(size)])  60.5 us
    pallas_call x5, Pallas kernels, weight_blocks(): pl.pallas_call(weight_kernel, name='weight_blocks', out_shape=[jax.ShapeD...  57.3 us
    unnamed x207, local copies, waits for them, and re-layouts  32.2 us
    pallas_call x1, Pallas kernels, attend_back(): pl.pallas_call(attend_back_kernel, name='attend_back', out_shape=(jax.Sha...  28.3 us
    pallas_call x2, Pallas kernels, project_rows_back(): pl.pallas_call(project_back_kernel, name='project_back', out_shape=[jax.S...  15.7 us
    dot_general x4, matrix products, rows_by(): lax.dot_general(left, right, ((contract[:1], contract[1:]), ((), ())), pr...  15.5 us
  transfers between devices with their start and end apart: 62, of which 33 were waited for; matrix products, arithmetic and copies ran while one was open for 12% of the time, Pallas kernels for 36%

profile of v4, /device:TPU:8, one launch (start us, length us, event | category | flops | bytes accessed | tf_op | source)
XLA Modules:
  0.0 617.9 jit_solution(3625822681365934807)
XLA Ops:
  30.7 38.4 %collective-permute-done.1.refs_5_ = bf16[256,2048]{1,0:T(8,128)(2,1)S(1)} collective-permute-done((bf16[256,2048]{1,0:T(8,128)(2,1)S(1)}, bf16[256,2048]{1,0:T(8,128)(2,1)S(1)}, u32[]{:S(2)}, u32[]{:S(2)}) %collective-permute-start.1) | collective-permute-done | bytes 1048608 | tf_op jit(solution)/shard_map/ppermute | solution.py:21
  79.6 20.4 %collective-permute-done.4.refs_1_ = bf16[256,2048]{1,0:T(8,128)(2,1)S(1)} collective-permute-done((bf16[256,2048]{1,0:T(8,128)(2,1)S(1)}, bf16[256,2048]{1,0:T(8,128)(2,1)S(1)}, u32[]{:S(2)}, u32[]{:S(2)}) %collective-permute-start.4) | collective-permute-done | bytes 1048608 | tf_op jit(solution)/shard_map/ppermute | solution.py:21
  111.6 14.6 %attend.1 = (bf16[1024,512]{1,0:T(8,128)(2,1)S(1)}, f32[8,4,128,128]{3,2,1,0:T(8,128)S(1)}, f32[8,4,128]{2,1,0:T(4,128)S(1)}) custom-call(s32[3]{0:T(128)S(1)} %pad_add_fusion.place, f32[4]{0:T(128)S(1)} %add_divide_fusion.share, bf16[1024,1536]{1,0:T(8,128)(2,1)S(1)} %pad_maximum_fusion.qkv_ref), custom_call_target="tpu_custom_call" | custom-call | flops 1 | bytes 1 | tf_op jit(solution)/shard_map/attend/pallas_call | solution.py:324
  133.3 35.1 %collective-permute-done.8.refs_3_ = bf16[256,512]{1,0:T(8,128)(2,1)S(1)} collective-permute-done((bf16[256,512]{1,0:T(8,128)(2,1)S(1)}, bf16[256,512]{1,0:T(8,128)(2,1)S(1)}, u32[]{:S(2)}, u32[]{:S(2)}) %collective-permute-start.8) | collective-permute-done | bytes 262176 | tf_op jit(solution)/shard_map/ppermute | solution.py:21
  174.6 10.4 %out_project.1 = (f32[256,2048]{1,0:T(8,128)}, bf16[256,2048]{1,0:T(8,128)(2,1)}, bf16[256,2048]{1,0:T(8,128)(2,1)}) custom-call(s32[3]{0:T(128)} %copy-done.37, bf16[256,512]{1,0:T(8,128)(2,1)} %get-tuple-element.315.refs_0_, bf16[256,512]{1,0:T(8,128)(2,1)} %copy-done.89, bf16[256,512]{1,0:T(8,128)(2,1)} %copy-done.88, bf16[256,512]{1,0:T(8,128)(2,1)} %copy-done.87, ...), custom_call_target="tpu_custom_call" | custom-call | flops 1 | bytes 1 | tf_op jit(solution)/shard_map/out_project/pallas_call | solution.py:447
  196.1 20.9 %feed_forward.4 = (bf16[3,256,2048]{2,1,0:T(8,128)(2,1)}, bf16[2,256,1024]{2,1,0:T(8,128)(2,1)S(1)}, bf16[2,256,1024]{2,1,0:T(8,128)(2,1)}, f32[256,2048]{1,0:T(8,128)S(1)}, f32[256,2048]{1,0:T(8,128)S(1)}) custom-call(s32[3]{0:T(128)S(1)} %copy-done.38, bf16[256,2048]{1,0:T(8,128)(2,1)S(1)} %copy-done.25, ...), custom_call_target="tpu_custom_call" | custom-call | flops 1 | bytes 1 | tf_op jit(solution)/shard_map/feed_forward/pallas_call | solution.py:589
  219.3 13.8 %collective-permute-done.12.rows_ref = bf16[256,2048]{1,0:T(8,128)(2,1)S(1)} collective-permute-done((bf16[256,2048]{1,0:T(8,128)(2,1)}, bf16[256,2048]{1,0:T(8,128)(2,1)S(1)}, u32[]{:S(2)}, u32[]{:S(2)}) %collective-permute-start.12) | collective-permute-done | bytes 1048608 | tf_op jit(solution)/shard_map/ppermute | solution.py:21
  233.1 10.4 %collective-permute-done.11.rows_ref = bf16[256,2048]{1,0:T(8,128)(2,1)S(1)} collective-permute-done((bf16[256,2048]{1,0:T(8,128)(2,1)}, bf16[256,2048]{1,0:T(8,128)(2,1)S(1)}, u32[]{:S(2)}, u32[]{:S(2)}) %collective-permute-start.11) | collective-permute-done | bytes 1048608 | tf_op jit(solution)/shard_map/ppermute | solution.py:21
  244.4 21.5 %feed_forward.5 = (bf16[3,256,2048]{2,1,0:T(8,128)(2,1)S(1)}, bf16[2,256,1024]{2,1,0:T(8,128)(2,1)S(1)}, bf16[2,256,1024]{2,1,0:T(8,128)(2,1)}, bf16[256,2048]{1,0:T(8,128)(2,1)S(1)}, bf16[256,2048]{1,0:T(8,128)(2,1)}) custom-call(s32[3]{0:T(128)S(1)} %copy-done.38, bf16[256,2048]{1,0:T(8,128)(2,1)S(1)} %collective-permute-done.11.rows_ref, ...), custom_call_target="tpu_custom_call" | custom-call | flops 1 | bytes 1 | tf_op jit(solution)/shard_map/feed_forward/pallas_call | solution.py:589
  271.3 20.8 %feed_forward.6 = (bf16[3,256,2048]{2,1,0:T(8,128)(2,1)S(1)}, bf16[2,256,1024]{2,1,0:T(8,128)(2,1)S(1)}, bf16[2,256,1024]{2,1,0:T(8,128)(2,1)}, bf16[256,2048]{1,0:T(8,128)(2,1)}, bf16[256,2048]{1,0:T(8,128)(2,1)}) custom-call(s32[3]{0:T(128)S(1)} %copy-done.38, bf16[256,2048]{1,0:T(8,128)(2,1)S(1)} %collective-permute-done.15.rows_ref, ...), custom_call_target="tpu_custom_call" | custom-call | flops 1 | bytes 1 | tf_op jit(solution)/shard_map/feed_forward/pallas_call | solution.py:589
  298.8 20.7 %feed_forward.7 = (bf16[3,256,2048]{2,1,0:T(8,128)(2,1)}, bf16[2,256,1024]{2,1,0:T(8,128)(2,1)S(1)}, bf16[2,256,1024]{2,1,0:T(8,128)(2,1)S(1)}, f32[256,2048]{1,0:T(8,128)S(1)}, f32[256,2048]{1,0:T(8,128)S(1)}) custom-call(s32[3]{0:T(128)S(1)} %copy-done.38, bf16[256,2048]{1,0:T(8,128)(2,1)S(1)} %copy-done.22, ...), custom_call_target="tpu_custom_call" | custom-call | flops 1 | bytes 1 | tf_op jit(solution)/shard_map/feed_forward/pallas_call | solution.py:589
  329.6 13.9 %weight_blocks.5 = (bf16[2,128,2048]{2,1,0:T(8,128)(2,1)S(1)}, bf16[2,128,2048]{2,1,0:T(8,128)(2,1)S(1)}, bf16[2,128,2048]{2,1,0:T(8,128)(2,1)S(1)}, bf16[2,128,2048]{2,1,0:T(8,128)(2,1)S(1)}) custom-call(bf16[2,256,1024]{2,1,0:T(8,128)(2,1)S(1)} %get-tuple-element.398.refs_0_, bf16[2,256,1024]{2,1,0:T(8,128)(2,1)S(1)} %get-tuple-element.399.refs_1_, ...), custom_call_target="tpu_custom_call" | custom-call | flops 1 | bytes 1 | tf_op jit(solution)/shard_map/weight_blocks/pallas_call | solution.py:700
  347.5 13.9 %weight_blocks.7 = (bf16[2,128,2048]{2,1,0:T(8,128)(2,1)S(1)}, bf16[2,128,2048]{2,1,0:T(8,128)(2,1)S(1)}, bf16[2,128,2048]{2,1,0:T(8,128)(2,1)S(1)}, bf16[2,128,2048]{2,1,0:T(8,128)(2,1)S(1)}) custom-call(bf16[2,256,1024]{2,1,0:T(8,128)(2,1)S(1)} %get-tuple-element.398.refs_0_, bf16[2,256,1024]{2,1,0:T(8,128)(2,1)S(1)} %get-tuple-element.399.refs_1_, ...), custom_call_target="tpu_custom_call" | custom-call | flops 1 | bytes 1 | tf_op jit(solution)/shard_map/weight_blocks/pallas_call | solution.py:700
  361.4 15.6 %weight_blocks.6 = (bf16[2,128,2048]{2,1,0:T(8,128)(2,1)S(1)}, bf16[2,128,2048]{2,1,0:T(8,128)(2,1)}, bf16[2,128,2048]{2,1,0:T(8,128)(2,1)S(1)}, bf16[2,128,2048]{2,1,0:T(8,128)(2,1)}) custom-call(bf16[2,256,1024]{2,1,0:T(8,128)(2,1)S(1)} %get-tuple-element.398.refs_0_, bf16[2,256,1024]{2,1,0:T(8,128)(2,1)S(1)} %get-tuple-element.399.refs_1_, ...), custom_call_target="tpu_custom_call" | custom-call | flops 1 | bytes 1 | tf_op jit(solution)/shard_map/weight_blocks/pallas_call | solution.py:700
  380.6 13.2 %out_back.1 = (f32[256,2048]{1,0:T(8,128)}, bf16[256,2048]{1,0:T(8,128)(2,1)}, bf16[256,1024]{1,0:T(8,128)(2,1)}, bf16[256,1024]{1,0:T(8,128)(2,1)}, f32[1,2048]...) custom-call(s32[3]{0:T(128)} %copy-done.37, ...), custom_call_target="tpu_custom_call" | custom-call | flops 1 | bytes 1 | tf_op jit(solution)/shard_map/out_back/pallas_call | solution.py:515
  395.9 8.1 %collective-permute-done.34 = bf16[256,2048]{1,0:T(8,128)(2,1)} collective-permute-done((bf16[256,2048]{1,0:T(8,128)(2,1)}, bf16[256,2048]{1,0:T(8,128)(2,1)}, u32[]{:S(2)}, u32[]{:S(2)}) %collective-permute-start.34) | collective-permute-done | bytes 1048608 | tf_op jit(solution)/shard_map/ppermute | solution.py:21
  441.3 28.3 %attend_back.1 = (bf16[1024,1536]{1,0:T(8,128)(2,1)S(1)}, f32[4,128]{1,0:T(4,128)S(1)}) custom-call(s32[3]{0:T(128)S(1)} %copy-done.39, f32[4]{0:T(128)S(1)} %add_divide_fusion.share, bf16[1024,1536]{1,0:T(8,128)(2,1)S(1)} %copy-done.7, bf16[256,512]{1,0:T(8,128)(2,1)S(1)} %copy-done.48, bf16[256,512]{1,0:T(8,128)(2,1)S(1)} %collective-permute-done.35.more_refs_1_, ...), custom_call_target="tpu_custom_call" | custom-call | flops 16106127360 | bytes 9437184 | tf_op jit(solution)/shard_map/attend_back/pallas_call | solution.py:361
  473.9 6.2 collective-permute-done.41
  499.1 10.2 %weight_blocks.9 = (bf16[2,128,1536]{2,1,0:T(8,128)(2,1)S(1)}, bf16[2,128,1536]{2,1,0:T(8,128)(2,1)S(1)}, bf16[2,128,1536]{2,1,0:T(8,128)(2,1)S(1)}, bf16[2,128,1536]{2,1,0:T(8,128)(2,1)S(1)}) custom-call(bf16[1,1024,1024]{2,1,0:T(8,128)(2,1)S(1)} %bitcast.123, bf16[1,1024,1024]{2,1,0:T(8,128)(2,1)S(1)} %bitcast.124, bf16[1,1024,1536]{2,1,0:T(8,128)(2,1)S(1)} %bitcast.122, ...), custom_call_target="tpu_custom_call" | custom-call | flops 1 | bytes 1 | tf_op jit(solution)/shard_map/weight_blocks/pallas_call | solution.py:700
  509.3 9.6 %project_back.3 = (f32[256,2048]{1,0:T(8,128)}, bf16[256,2048]{1,0:T(8,128)(2,1)}, f32[256,2048]{1,0:T(8,128)}, f32[1,2048]{1,0:T(1,128)}) custom-call(bf16[1024,1536]{1,0:T(8,128)(2,1)} %copy-done.2, bf16[1024,1536]{1,0:T(8,128)(2,1)} %copy-done.2, bf16[1024,1536]{1,0:T(8,128)(2,1)} %copy-done.2, bf16[256,2048]{1,0:T(8,128)(2,1)} %copy-done.52, ...), custom_call_target="tpu_custom_call" | custom-call | flops 1 | bytes 1 | tf_op jit(solution)/shard_map/project_back/pallas_call | solution.py:638
  532.0 7.0 %collective-permute-done.49 = bf16[256,1536]{1,0:T(8,128)(2,1)S(1)} collective-permute-done((bf16[256,1536]{1,0:T(8,128)(2,1)S(1)}, bf16[256,1536]{1,0:T(8,128)(2,1)S(1)}, u32[]{:S(2)}, u32[]{:S(2)}) %collective-permute-start.49) | collective-permute-done | bytes 786464 | tf_op jit(solution)/shard_map/ppermute | solution.py:21
  541.0 21.6 %collective-permute-done.47 = bf16[256,2048]{1,0:T(8,128)(2,1)S(1)} collective-permute-done((bf16[256,2048]{1,0:T(8,128)(2,1)S(1)}, bf16[256,2048]{1,0:T(8,128)(2,1)S(1)}, u32[]{:S(2)}, u32[]{:S(2)}) %collective-permute-start.47) | collective-permute-done | bytes 1048608 | tf_op jit(solution)/shard_map/ppermute | solution.py:21
  594.6 7.0 %collective-permute-done.54 = bf16[256,512]{1,0:T(8,128)(2,1)S(1)} collective-permute-done((bf16[256,512]{1,0:T(8,128)(2,1)}, bf16[256,512]{1,0:T(8,128)(2,1)S(1)}, u32[]{:S(2)}, u32[]{:S(2)}) %collective-permute-start.54) | collective-permute-done | bytes 262176 | tf_op jit(solution)/shard_map/ppermute | solution.py:21
  602.4 6.1 collective-permute-done.55
  (420 shorter events, 213.9 us)
Async XLA Ops:
  7.2 167.4 %all-gather.2.cloned.1.call-start = ((), (), s32[]{:S(2)}) async-start(), calls=%async_computation | async-start | bytes 9437184 | tf_op jit(solution)/shard_map/all_gather | solution.py:791
  13.5 55.6 %collective-permute-start.1 = (bf16[256,2048]{1,0:T(8,128)(2,1)S(1)}, bf16[256,2048]{1,0:T(8,128)(2,1)S(1)}, u32[]{:S(2)}, u32[]{:S(2)}) collective-permute-start(bf16[256,2048]{1,0:T(8,128)(2,1)S(1)} %fusion.4.refs_3_), channel_id=1, source_target_pairs={{0,2},{1,3},{2,0},{3,1},{4,6},{5,7},{6,4},{7,5},{8,10},{9,11},{10,... | collective-permute-start | bytes 3145736 | tf_op jit(solution)/shard_map/ppermute | solution.py:21
  13.6 56.6 %collective-permute-start = (bf16[256,2048]{1,0:T(8,128)(2,1)S(1)}, bf16[256,2048]{1,0:T(8,128)(2,1)S(1)}, u32[]{:S(2)}, u32[]{:S(2)}) collective-permute-start(bf16[256,2048]{1,0:T(8,128)(2,1)S(1)} %fusion.4.refs_3_), channel_id=1, source_target_pairs={{0,1},{1,0},{2,3},{3,2},{4,5},{5,4},{6,7},{7,6},{8,9},{9,8},{10,11... | collective-permute-start | bytes 3145736 | tf_op jit(solution)/shard_map/ppermute | solution.py:21
  70.6 29.4 %collective-permute-start.4 = (bf16[256,2048]{1,0:T(8,128)(2,1)S(1)}, bf16[256,2048]{1,0:T(8,128)(2,1)S(1)}, u32[]{:S(2)}, u32[]{:S(2)}) collective-permute-start(bf16[256,2048]{1,0:T(8,128)(2,1)S(1)} %collective-permute-done.1.refs_5_), channel_id=1, source_target_pairs={{0,1},{1,0},{2,3},{3,2},{4,5},{5,4},{6,7},{7,6},{8,9},{9,8},{10,11... | collective-permute-start | bytes 3145736 | tf_op jit(solution)/shard_map/ppermute | solution.py:21
  102.7 70.5 %collective-permute-start.10 = (bf16[256,2048]{1,0:T(8,128)(2,1)}, bf16[256,2048]{1,0:T(8,128)(2,1)}, u32[]{:S(2)}, u32[]{:S(2)}) collective-permute-start(bf16[256,2048]{1,0:T(8,128)(2,1)} %multiply_convert_fusion.branch_ref), channel_id=1, source_target_pairs={{0,2},{1,3},{2,0},{3,1},{4,6},{5,7},{6,4},{7,5},{8,10},{9,11},{10,... | collective-permute-start | bytes 3145736 | tf_op jit(solution)/shard_map/ppermute | solution.py:21
  106.2 67.0 %collective-permute-start.9 = (bf16[256,2048]{1,0:T(8,128)(2,1)}, bf16[256,2048]{1,0:T(8,128)(2,1)}, u32[]{:S(2)}, u32[]{:S(2)}) collective-permute-start(bf16[256,2048]{1,0:T(8,128)(2,1)} %multiply_convert_fusion.branch_ref), channel_id=1, source_target_pairs={{0,1},{1,0},{2,3},{3,2},{4,5},{5,4},{6,7},{7,6},{8,9},{9,8},{10,11... | collective-permute-start | bytes 3145736 | tf_op jit(solution)/shard_map/ppermute | solution.py:21
  127.0 41.4 %collective-permute-start.8 = (bf16[256,512]{1,0:T(8,128)(2,1)S(1)}, bf16[256,512]{1,0:T(8,128)(2,1)S(1)}, u32[]{:S(2)}, u32[]{:S(2)}) collective-permute-start(bf16[256,512]{1,0:T(8,128)(2,1)S(1)} %get-tuple-element.632), channel_id=1, source_target_pairs={{0,3},{1,2},{2,1},{3,0},{4,7},{5,6},{6,5},{7,4},{8,11},{9,10},{10,... | collective-permute-start | bytes 786440 | tf_op jit(solution)/shard_map/ppermute | solution.py:21
  127.4 45.8 %collective-permute-start.7 = (bf16[256,512]{1,0:T(8,128)(2,1)S(1)}, bf16[256,512]{1,0:T(8,128)(2,1)S(1)}, u32[]{:S(2)}, u32[]{:S(2)}) collective-permute-start(bf16[256,512]{1,0:T(8,128)(2,1)S(1)} %get-tuple-element.633), channel_id=1, source_target_pairs={{0,2},{1,3},{2,0},{3,1},{4,6},{5,7},{6,4},{7,5},{8,10},{9,11},{10,... | collective-permute-start | bytes 786440 | tf_op jit(solution)/shard_map/ppermute | solution.py:21
  131.1 42.0 %collective-permute-start.6 = (bf16[256,512]{1,0:T(8,128)(2,1)S(1)}, bf16[256,512]{1,0:T(8,128)(2,1)S(1)}, u32[]{:S(2)}, u32[]{:S(2)}) collective-permute-start(bf16[256,512]{1,0:T(8,128)(2,1)S(1)} %get-tuple-element.634), channel_id=1, source_target_pairs={{0,1},{1,0},{2,3},{3,2},{4,5},{5,4},{6,7},{7,6},{8,9},{9,8},{10,11... | collective-permute-start | bytes 786440 | tf_op jit(solution)/shard_map/ppermute | solution.py:21
  173.2 45.1 %collective-permute-start.13 = (bf16[256,2048]{1,0:T(8,128)(2,1)}, bf16[256,2048]{1,0:T(8,128)(2,1)S(1)}, u32[]{:S(2)}, u32[]{:S(2)}) collective-permute-start(bf16[256,2048]{1,0:T(8,128)(2,1)} %collective-permute-done.10.branch_ref), channel_id=1, source_target_pairs={{0,1},{1,0},{2,3},{3,2},{4,5},{5,4},{6,7},{7,6},{8,9},{9,8},{10,11... | collective-permute-start | bytes 3145736 | tf_op jit(solution)/shard_map/ppermute | solution.py:21
  185.0 48.1 %collective-permute-start.12 = (bf16[256,2048]{1,0:T(8,128)(2,1)}, bf16[256,2048]{1,0:T(8,128)(2,1)S(1)}, u32[]{:S(2)}, u32[]{:S(2)}) collective-permute-start(bf16[256,2048]{1,0:T(8,128)(2,1)} %get-tuple-element.323.rows_ref), channel_id=1, source_target_pairs={{0,2},{1,3},{2,0},{3,1},{4,6},{5,7},{6,4},{7,5},{8,10},{9,11},{10,... | collective-permute-start | bytes 3145736 | tf_op jit(solution)/shard_map/ppermute | solution.py:21
  187.7 55.8 %collective-permute-start.11 = (bf16[256,2048]{1,0:T(8,128)(2,1)}, bf16[256,2048]{1,0:T(8,128)(2,1)S(1)}, u32[]{:S(2)}, u32[]{:S(2)}) collective-permute-start(bf16[256,2048]{1,0:T(8,128)(2,1)} %get-tuple-element.323.rows_ref), channel_id=1, source_target_pairs={{0,1},{1,0},{2,3},{3,2},{4,5},{5,4},{6,7},{7,6},{8,9},{9,8},{10,11... | collective-permute-start | bytes 3145736 | tf_op jit(solution)/shard_map/ppermute | solution.py:21
  189.0 30.3 %collective-permute-start.14 = (bf16[256,2048]{1,0:T(8,128)(2,1)}, bf16[256,2048]{1,0:T(8,128)(2,1)S(1)}, u32[]{:S(2)}, u32[]{:S(2)}) collective-permute-start(bf16[256,2048]{1,0:T(8,128)(2,1)} %get-tuple-element.335), channel_id=1, source_target_pairs={{0,4},{4,0},{8,12},{12,8},{16,20},{20,16},{24,28},{28,24},{1,5},{5... | collective-permute-start | bytes 3145736 | tf_op jit(solution)/shard_map/ppermute | solution.py:21
  323.9 55.1 %collective-permute-start.26 = (bf16[256,2048]{1,0:T(8,128)(2,1)}, bf16[256,2048]{1,0:T(8,128)(2,1)S(1)}, u32[]{:S(2)}, u32[]{:S(2)}) collective-permute-start(bf16[256,2048]{1,0:T(8,128)(2,1)} %add_convert_fusion.3), channel_id=1, source_target_pairs={{0,2},{1,3},{2,0},{3,1},{4,6},{5,7},{6,4},{7,5},{8,10},{9,11},{10,... | collective-permute-start | bytes 3145736 | tf_op jit(solution)/shard_map/ppermute | solution.py:21
  327.2 51.8 %collective-permute-start.25 = (bf16[256,2048]{1,0:T(8,128)(2,1)S(1)}, bf16[256,2048]{1,0:T(8,128)(2,1)S(1)}, u32[]{:S(2)}, u32[]{:S(2)}) collective-permute-start(bf16[256,2048]{1,0:T(8,128)(2,1)S(1)} %copy-done.47), channel_id=1, source_target_pairs={{0,1},{1,0},{2,3},{3,2},{4,5},{5,4},{6,7},{7,6},{8,9},{9,8},{10,11... | collective-permute-start | bytes 3145736 | tf_op jit(solution)/shard_map/ppermute | solution.py:21
  344.5 34.5 %collective-permute-start.30 = (bf16[256,2048]{1,0:T(8,128)(2,1)S(1)}, bf16[256,2048]{1,0:T(8,128)(2,1)}, u32[]{:S(2)}, u32[]{:S(2)}) collective-permute-start(bf16[256,2048]{1,0:T(8,128)(2,1)S(1)} %bitcast.134), channel_id=1, source_target_pairs={{0,16},{4,20},{8,24},{12,28},{16,0},{20,4},{24,8},{28,12},{1,17},{... | collective-permute-start | bytes 3145736 | tf_op jit(solution)/shard_map/ppermute | solution.py:21
  346.0 33.0 %collective-permute-start.29 = (bf16[256,2048]{1,0:T(8,128)(2,1)S(1)}, bf16[256,2048]{1,0:T(8,128)(2,1)}, u32[]{:S(2)}, u32[]{:S(2)}) collective-permute-start(bf16[256,2048]{1,0:T(8,128)(2,1)S(1)} %bitcast.133), channel_id=1, source_target_pairs={{0,8},{4,12},{8,0},{12,4},{16,24},{20,28},{24,16},{28,20},{1,9},{5... | collective-permute-start | bytes 3145736 | tf_op jit(solution)/shard_map/ppermute | solution.py:21
  432.7 51.5 %collective-permute-start.40 = (bf16[256,2048]{1,0:T(8,128)(2,1)S(1)}, bf16[256,2048]{1,0:T(8,128)(2,1)S(1)}, u32[]{:S(2)}, u32[]{:S(2)}) collective-permute-start(bf16[256,2048]{1,0:T(8,128)(2,1)S(1)} %add_convert_fusion.2), channel_id=1, source_target_pairs={{0,2},{1,3},{2,0},{3,1},{4,6},{5,7},{6,4},{7,5},{8,10},{9,11},{10,... | collective-permute-start | bytes 3145736 | tf_op jit(solution)/shard_map/ppermute | solution.py:21
  436.9 43.2 %collective-permute-start.41 = (bf16[512,2048]{1,0:T(8,128)(2,1)S(1)}, bf16[512,2048]{1,0:T(8,128)(2,1)S(1)}, u32[]{:S(2)}, u32[]{:S(2)}) collective-permute-start(bf16[512,2048]{1,0:T(8,128)(2,1)S(1)} %pad_maximum_fusion.4), channel_id=1, source_target_pairs={{0,8},{4,12},{8,0},{12,4},{16,24},{20,28},{24,16},{28,20},{1,9},{5... | collective-permute-start | bytes 6291464 | tf_op jit(solution)/shard_map/ppermute | solution.py:21
  438.6 42.8 %collective-permute-start.42 = (bf16[512,2048]{1,0:T(8,128)(2,1)S(1)}, bf16[512,2048]{1,0:T(8,128)(2,1)S(1)}, u32[]{:S(2)}, u32[]{:S(2)}) collective-permute-start(bf16[512,2048]{1,0:T(8,128)(2,1)S(1)} %pad_maximum_fusion.5), channel_id=1, source_target_pairs={{0,16},{4,20},{8,24},{12,28},{16,0},{20,4},{24,8},{28,12},{1,17},{... | collective-permute-start | bytes 6291464 | tf_op jit(solution)/shard_map/ppermute | solution.py:21
  522.8 49.8 %collective-permute-start.46 = (bf16[256,2048]{1,0:T(8,128)(2,1)S(1)}, bf16[256,2048]{1,0:T(8,128)(2,1)S(1)}, u32[]{:S(2)}, u32[]{:S(2)}) collective-permute-start(bf16[256,2048]{1,0:T(8,128)(2,1)S(1)} %add_convert_fusion.1), channel_id=1, source_target_pairs={{0,2},{1,3},{2,0},{3,1},{4,6},{5,7},{6,4},{7,5},{8,10},{9,11},{10,... | collective-permute-start | bytes 3145736 | tf_op jit(solution)/shard_map/ppermute | solution.py:21
  524.0 48.6 %collective-permute-start.45 = (bf16[256,2048]{1,0:T(8,128)(2,1)S(1)}, bf16[256,2048]{1,0:T(8,128)(2,1)S(1)}, u32[]{:S(2)}, u32[]{:S(2)}) collective-permute-start(bf16[256,2048]{1,0:T(8,128)(2,1)S(1)} %copy-done.99), channel_id=1, source_target_pairs={{0,1},{1,0},{2,3},{3,2},{4,5},{5,4},{6,7},{7,6},{8,9},{9,8},{10,11... | collective-permute-start | bytes 3145736 | tf_op jit(solution)/shard_map/ppermute | solution.py:21
  526.1 36.6 %collective-permute-start.47 = (bf16[256,2048]{1,0:T(8,128)(2,1)S(1)}, bf16[256,2048]{1,0:T(8,128)(2,1)S(1)}, u32[]{:S(2)}, u32[]{:S(2)}) collective-permute-start(bf16[256,2048]{1,0:T(8,128)(2,1)S(1)} %pad_maximum_fusion.10), channel_id=1, source_target_pairs={{0,16},{4,20},{8,24},{12,28},{16,0},{20,4},{24,8},{28,12},{1,17},{... | collective-permute-start | bytes 3145736 | tf_op jit(solution)/shard_map/ppermute | solution.py:21
  540.2 30.2 %collective-permute-start.50 = (bf16[128,1536]{1,0:T(8,128)(2,1)S(1)}, bf16[128,1536]{1,0:T(8,128)(2,1)S(1)}, u32[]{:S(2)}, u32[]{:S(2)}) collective-permute-start(bf16[128,1536]{1,0:T(8,128)(2,1)S(1)} %fusion.19), channel_id=1, source_target_pairs={{0,16},{4,20},{8,24},{12,28},{16,0},{20,4},{24,8},{28,12},{1,17},{... | collective-permute-start | bytes 1179656 | tf_op jit(solution)/shard_map/ppermute | solution.py:21
  (145 other events, 1558.9 us)
Sparse Core Ops, SparseCore 0:
  102.6 56.3 all-gather.1
